TPU v7x, 512 devices: a whole 4x4x16 slice. The times are simulated.
512 devices in a mesh: gz: 16 (over y, x_hi, core), ta: 32 (over x_lo, z).
Axes of the slice: x: 4 (x_hi: 2, x_lo: 2; x = x_hi * 2 + x_lo), y: 4, z: 16, core: 2. Of those that a mesh axis runs over, the one named last changes fastest.
Arguments:
- volume: bfloat16 [96, 24, 40, 12288], P('gz', None, None, 'ta'), may hold values from -6 to 6
- sketch_matrix: bfloat16 [12288, 256], P('ta'), may hold values from -0.4375 to 0.4375
- brain_voxels: int32 [57344], P('gz'), may hold values from 0 to 5759, as said below
Outputs:
- sketch: float32 [57344, 256], P(('gz', 'ta'))
Inputs may be any that keep to these rules, and one draw needn't show every extreme that they name: `brain_voxels`: each slab's 3584 entries are distinct and increasing; the first is 0 and the last 5759.
All inputs are finite; a program needn't handle non-finite values.
Results may differ from a plain program's by a relative error of at most 0.0003.
Values may be sent and summed in bfloat16 or wider, within the bound.
A program may use at most 64 MiB of HBM per device.

v0:
```python
import math

import jax
import jax.numpy as jnp
from jax import lax
from jax.sharding import PartitionSpec as P


def with_halo(shard, sides, width):
    for axis, dim in sides:
        peers, length = (lax.axis_size(axis), shard.shape[dim])
        up = [(i, (i + 1) % peers) for i in range(peers - 1)]
        down = [(j, i) for i, j in up]
        last = lax.slice_in_dim(shard, length - width, length, axis=dim)
        initial = lax.slice_in_dim(shard, 0, width, axis=dim)
        before = lax.ppermute(last, axis, up)
        after = lax.ppermute(initial, axis, down)
        shard = jnp.concatenate([before, shard, after], axis=dim)
    return shard


def kernel_taps():
    sigma = 3.0 / (2.0 * math.sqrt(2.0 * math.log(2.0)))
    raw_taps = [math.exp(-0.5 * (shift_k - 2) ** 2 / sigma**2) for shift_k in range(5)]
    summed = sum(raw_taps)
    return [value_k / summed for value_k in raw_taps]


def smooth_along(source, axis_num, kernel):
    extent = source.shape[axis_num]
    widths = [(0, 0)] * source.ndim
    widths[axis_num] = (2, 2)
    padded = jnp.pad(source, widths)
    summed = jnp.zeros_like(source)
    for shift_k in range(5):
        summed = summed + kernel[shift_k] * lax.slice_in_dim(
            padded, shift_k, shift_k + extent, axis=axis_num
        )
    return summed


def smooth_planes(padded, planes, kernel):
    summed = kernel[0] * padded[0:planes].astype(jnp.float32)
    for shift_k in range(1, 5):
        summed = summed + kernel[shift_k] * padded[shift_k : shift_k + planes].astype(jnp.float32)
    return summed


def shards(volume, sketch_matrix, brain_voxels):
    kernel = kernel_taps()
    planes, width_x, width_y, time_local = volume.shape
    slab_cells = planes * width_x * width_y
    weights = sketch_matrix.astype(jnp.float32)
    padded = with_halo(volume, (("gz", 0),), 2)
    signal = smooth_planes(padded, planes, kernel)
    signal = smooth_along(signal, 1, kernel)
    signal = smooth_along(signal, 2, kernel)
    picked = signal.reshape(slab_cells, time_local)[brain_voxels]
    return lax.psum_scatter(
        jnp.dot(
            picked, weights, precision=lax.Precision.HIGHEST, preferred_element_type=jnp.float32
        ),
        "ta",
        scatter_dimension=0,
        tiled=True,
    )


def solution(mesh):
    in_specs = (P("gz", None, None, "ta"), P("ta", None), P("gz"))
    out_specs = P(("gz", "ta"), None)
    return jax.shard_map(shards, mesh=mesh, in_specs=in_specs, out_specs=out_specs, check_vma=False)
```

profile of v0, /device:TPU:24, one launch (start us, length us, event | category | flops | bytes accessed | tf_op | source)
XLA Modules:
  0.0 239.6 jit_solution(6649190956623822486)
XLA Ops:
  6.5 0.0 copy-start
  6.5 0.0 reduce-scatter.2.cloned.1.call-start
  6.5 0.0 copy-start.1
  6.5 2.3 fusion.16
  8.8 2.1 collective-permute-start
  10.9 6.0 %collective-permute-start.1 = (bf16[2,24,40,384]{3,2,1,0:T(8,128)(2,1)S(1)}, bf16[2,24,40,384]{3,2,1,0:T(8,128)(2,1)S(1)}, u32[]{:S(2)}, u32[]{:S(2)}) collective-permute-start(bf16[2,24,40,384]{3,2,1,0:T(8,128)(2,1)S(1)} %get-tuple-element.8), channel_id=1, source_target_pairs={{32,0},{64,32},{96,64},{128,96},{160,128},{192,160},{224,192},{256... | collective-permute-start | bytes 4423688 | tf_op jit(solution)/shard_map/ppermute | solution.py:17
  16.9 0.7 compare_select_fusion
  17.7 25.6 %collective-permute-done = bf16[2,24,40,384]{3,2,1,0:T(8,128)(2,1)S(1)} collective-permute-done((bf16[2,24,40,384]{3,2,1,0:T(8,128)(2,1)S(1)}, bf16[2,24,40,384]{3,2,1,0:T(8,128)(2,1)S(1)}, u32[]{:S(2)}, u32[]{:S(2)}) %collective-permute-start) | collective-permute-done | bytes 1474592 | tf_op jit(solution)/shard_map/ppermute | solution.py:16
  43.2 1.3 constant_dynamic-update-slice_fusion.1
  44.5 0.0 copy-done.1
  44.5 2.9 %constant_dynamic-update-slice_fusion = (bf16[8,24,40,384]{3,2,1,0:T(8,128)(2,1)}, bf16[8,24,40,384]{3,2,1,0:T(8,128)(2,1)S(1)}) fusion(bf16[8,24,40,384]{3,2,1,0:T(8,128)(2,1)} %constant_dynamic-update-slice_fusion.1, bf16[6,24,40,384]{3,2,1,0:T(8,128)(2,1)S(1)} %copy-done.1), kind=kLoop, calls=%fused_computation.28 | loop fusion | bytes 13271040 | tf_op jit(solution)/shard_map/concatenate | solution.py:18
  47.4 0.0 collective-permute-done.1
  47.4 0.3 constant_dynamic-update-slice_fusion.2
  47.7 6.3 %multiply_add_fusion = f32[6,24,40,384]{3,2,1,0:T(8,128)S(1)} fusion(bf16[6,24,40,384]{3,2,1,0:T(8,128)(2,1)S(1)} %copy-done.1, bf16[8,24,40,384]{3,2,1,0:T(8,128)(2,1)S(1)} %constant_dynamic-update-slice_fusion.2, bf16[8,24,40,384]{3,2,1,0:T(8,128)(2,1)} %get-tuple-element.5), kind=kLoop, calls=%fused_computation.25 | loop fusion | flops 30965760 | bytes 30965760 | tf_op jit(solution)/shard_map/add | solution.py:45
  54.0 3.6 %fusion.4 = f32[6,24,40,384]{3,2,1,0:T(8,128)S(1)} fusion(f32[6,24,40,384]{3,2,1,0:T(8,128)S(1)} %multiply_add_fusion), kind=kLoop, calls=%fused_computation.13 | loop fusion | flops 19906560 | bytes 17694720 | tf_op jit(solution)/shard_map/add | solution.py:36
  57.6 6.8 %fusion.12 = f32[6,24,40,384]{3,2,1,0:T(8,128)} fusion(f32[6,24,40,384]{3,2,1,0:T(8,128)S(1)} %fusion.4), kind=kLoop, calls=%fused_computation.21 | loop fusion | flops 19906560 | bytes 17694720 | tf_op jit(solution)/shard_map/add | solution.py:36
  64.4 14.2 %gather_fusion = f32[3584,384]{1,0:T(8,128)} fusion(f32[5760,384]{1,0:T(8,128)} %bitcast.3, s32[4096]{0:T(1024)S(1)} %pad_clamp_fusion), kind=kCustom, calls=%fused_computation | custom fusion | bytes 11024384 | tf_op jit(solution)/shard_map/gather | solution.py:58
  78.6 0.0 copy-done
  78.6 7.5 %fusion.17 = f32[3584,256]{1,0:T(8,128)} fusion(f32[3584,384]{1,0:T(8,128)} %gather_fusion, bf16[384,256]{1,0:T(8,128)(2,1)S(1)} %copy-done), kind=kOutput, calls=%fused_computation.33 | convolution fusion | flops 4227858432 | bytes 9371648 | tf_op jit(solution)/shard_map/dot_general | solution.py:60
  86.1 0.0 reduce-scatter.2.cloned.1.call-update
  86.1 146.6 %reduce-scatter.2.cloned.1.call-done = f32[112,256]{1,0:T(8,128)} async-done(((f32[3584,256]{1,0:T(8,128)}), f32[112,256]{1,0:T(8,128)}) %reduce-scatter.2.cloned.1.call-update) | async-done | bytes 114704 | tf_op jit(solution)/shard_map/reduce_scatter | solution.py:59
  (1 shorter events, 0.0 us)
Async XLA Ops:
  6.5 72.1 %copy-start = (bf16[384,256]{1,0:T(8,128)(2,1)S(1)}, bf16[384,256]{1,0:T(8,128)(2,1)}, u32[]{:S(2)}) copy-start(bf16[384,256]{1,0:T(8,128)(2,1)} %param.4) | copy-start | bytes 589828
  6.5 226.2 %reduce-scatter.2.cloned.1.call-start = ((), (), s32[]{:S(2)}) async-start(), calls=%async_computation.1 | async-start | bytes 3784704 | tf_op jit(solution)/shard_map/reduce_scatter | solution.py:59
  6.5 38.0 %copy-start.1 = (bf16[6,24,40,384]{3,2,1,0:T(8,128)(2,1)S(1)}, bf16[6,24,40,384]{3,2,1,0:T(8,128)(2,1)}, u32[]{:S(2)}) copy-start(bf16[6,24,40,384]{3,2,1,0:T(8,128)(2,1)} %param.3) | copy-start | bytes 13271044
  8.8 34.4 %collective-permute-start = (bf16[2,24,40,384]{3,2,1,0:T(8,128)(2,1)S(1)}, bf16[2,24,40,384]{3,2,1,0:T(8,128)(2,1)S(1)}, u32[]{:S(2)}, u32[]{:S(2)}) collective-permute-start(bf16[2,24,40,384]{3,2,1,0:T(8,128)(2,1)S(1)} %get-tuple-element.7), channel_id=1, source_target_pairs={{0,32},{32,64},{64,96},{96,128},{128,160},{160,192},{192,224},{224... | collective-permute-start | bytes 4423688 | tf_op jit(solution)/shard_map/ppermute | solution.py:16
  10.9 36.5 %collective-permute-start.1 = (bf16[2,24,40,384]{3,2,1,0:T(8,128)(2,1)S(1)}, bf16[2,24,40,384]{3,2,1,0:T(8,128)(2,1)S(1)}, u32[]{:S(2)}, u32[]{:S(2)}) collective-permute-start(bf16[2,24,40,384]{3,2,1,0:T(8,128)(2,1)S(1)} %get-tuple-element.8), channel_id=1, source_target_pairs={{32,0},{64,32},{96,64},{128,96},{160,128},{192,160},{224,192},{256... | collective-permute-start | bytes 4423688 | tf_op jit(solution)/shard_map/ppermute | solution.py:17
Sparse Core Ops, SparseCore 0:
  86.2 146.4 reduce-scatter.1
where the time goes:
time: 240 us
  waiting for transfers between devices  172 us (72%)
  local copies, waits for them, and re-layouts  20.9 us (9%)
  other arithmetic  17.4 us (7%)
  between operations  13.4 us (6%)
  starting transfers between devices  8.1 us (3%)
  matrix products  7.48 us (3%)
    reduce_scatter x1, waiting for transfers between devices, shards(): lax.psum_scatter(jnp.dot(picked, weights, precision=lax.Precision.HIGHEST...  147 us
    ppermute x1, waiting for transfers between devices, with_halo(): before = lax.ppermute(last, axis, up)  25.6 us
    gather x1, local copies, waits for them, and re-layouts, shards(): picked = signal.reshape(slab_cells, time_local)[brain_voxels]  14.2 us
    add x2, other arithmetic, smooth_along(): summed + kernel[shift_k] * lax.slice_in_dim(padded, shift_k, shift_k + ex...  10.4 us
    dot_general x1, matrix products, shards(): jnp.dot(picked, weights, precision=lax.Precision.HIGHEST, preferred_eleme...  7.48 us
    add x1, other arithmetic, smooth_planes(): summed + kernel[shift_k] * padded[shift_k:shift_k + planes].astype(jnp.fl...  6.33 us
    ppermute x1, starting transfers between devices, with_halo(): after = lax.ppermute(initial, axis, down)  6.05 us
  transfers between devices with their start and end apart: 3, of which 2 were waited for; matrix products, arithmetic and copies ran while one was open for 2% of the time, Pallas kernels for 0%

commit v1 on v0

--- a/solution.py
+++ b/solution.py
@@ -1,9 +1,15 @@
+import functools
 import math
 
 import jax
 import jax.numpy as jnp
 from jax import lax
+from jax.experimental import pallas as pl
+from jax.experimental.pallas import tpu as pltpu
 from jax.sharding import PartitionSpec as P
+
+MESH = pl.DeviceIdType.MESH
+Z_RING = 16
 
 
 def with_halo(shard, sides, width):
@@ -46,6 +52,98 @@
     return summed
 
 
+def rs_kernel(nz, p_ref, o_ref, recv, send, fin, xrecv, send_sem, recv_sem, credit, xsem):
+    gz = lax.axis_index("gz")
+    ta = lax.axis_index("ta")
+    xl = ta // nz
+    zi = ta % nz
+    right = xl * nz + (zi + 1) % nz
+    left = xl * nz + (zi + nz - 1) % nz
+    partner = (1 - xl) * nz + zi
+
+    barrier = pltpu.get_barrier_semaphore()
+    for peer in (left, right, partner):
+        pl.semaphore_signal(barrier, 1, device_id=(gz, peer), device_id_type=MESH)
+    pl.semaphore_wait(barrier, 3)
+
+    dirs = (
+        (0, right, left, lambda s: (zi + 2 * nz - s - 1) % nz),
+        (1, left, right, lambda s: nz + (zi + s + 1) % nz),
+    )
+    copies = {}
+    for s in range(nz):
+        for d, dst, src_peer, chunk in dirs:
+            blk = chunk(s)
+            if s == 0:
+                src = p_ref.at[blk]
+            else:
+                copies[(d, s - 1)].wait_recv()
+                val = recv[d, (s - 1) % 2] + p_ref[blk]
+                if s < nz - 1:
+                    if s >= 2:
+                        copies[(d, s - 2)].wait_send()
+                    send[d, s % 2] = val
+                    src = send.at[d, s % 2]
+                    if s <= nz - 3:
+                        pl.semaphore_signal(credit.at[d], 1, device_id=(gz, src_peer), device_id_type=MESH)
+                else:
+                    fin[d] = val
+            if s < nz - 1:
+                if s >= 2:
+                    pl.semaphore_wait(credit.at[d], 1)
+                cp = pltpu.make_async_remote_copy(
+                    src_ref=src,
+                    dst_ref=recv.at[d, s % 2],
+                    send_sem=send_sem.at[d, s % 2],
+                    recv_sem=recv_sem.at[d, s % 2],
+                    device_id=(gz, dst),
+                    device_id_type=MESH,
+                )
+                cp.start()
+                copies[(d, s)] = cp
+
+    xcp = pltpu.make_async_remote_copy(
+        src_ref=fin.at[1 - xl],
+        dst_ref=xrecv,
+        send_sem=xsem.at[0],
+        recv_sem=xsem.at[1],
+        device_id=(gz, partner),
+        device_id_type=MESH,
+    )
+    xcp.start()
+    for d in range(2):
+        for s in (nz - 3, nz - 2):
+            copies[(d, s)].wait_send()
+    xcp.wait_recv()
+    o_ref[...] = fin[xl] + xrecv[...]
+    xcp.wait_send()
+
+
+def reduce_scatter_ta(partial, n_ta):
+    rows_all, cols = partial.shape
+    nz = Z_RING
+    assert n_ta == 2 * nz
+    rows = rows_all // n_ta
+    blocks = partial.reshape(n_ta, rows, cols)
+    return pl.pallas_call(
+        functools.partial(rs_kernel, nz),
+        out_shape=jax.ShapeDtypeStruct((rows, cols), jnp.float32),
+        in_specs=[pl.BlockSpec(memory_space=pltpu.VMEM)],
+        out_specs=pl.BlockSpec(memory_space=pltpu.VMEM),
+        scratch_shapes=[
+            pltpu.VMEM((2, 2, rows, cols), jnp.float32),
+            pltpu.VMEM((2, 2, rows, cols), jnp.float32),
+            pltpu.VMEM((2, rows, cols), jnp.float32),
+            pltpu.VMEM((rows, cols), jnp.float32),
+            pltpu.SemaphoreType.DMA((2, 2)),
+            pltpu.SemaphoreType.DMA((2, 2)),
+            pltpu.SemaphoreType.REGULAR((2,)),
+            pltpu.SemaphoreType.DMA((2,)),
+        ],
+        compiler_params=pltpu.CompilerParams(collective_id=0, has_side_effects=True),
+    )(blocks)
+
+
 def shards(volume, sketch_matrix, brain_voxels):
     kernel = kernel_taps()
     planes, width_x, width_y, time_local = volume.shape
@@ -56,14 +154,10 @@
     signal = smooth_along(signal, 1, kernel)
     signal = smooth_along(signal, 2, kernel)
     picked = signal.reshape(slab_cells, time_local)[brain_voxels]
-    return lax.psum_scatter(
-        jnp.dot(
-            picked, weights, precision=lax.Precision.HIGHEST, preferred_element_type=jnp.float32
-        ),
-        "ta",
-        scatter_dimension=0,
-        tiled=True,
+    partial = jnp.dot(
+        picked, weights, precision=lax.Precision.HIGHEST, preferred_element_type=jnp.float32
     )
+    return reduce_scatter_ta(partial, lax.axis_size("ta"))
 
 
 def solution(mesh):

time: 240 us -> 167 us (0.70)
  waiting for transfers between devices: 172 us -> 25.6 us
  Pallas kernels: 0 us -> 85.5 us
  between operations: 13.4 us -> 0.05 us
    reduce_scatter x1 -> x0, waiting for transfers between devices: 147 us -> none  [shards(): lax.psum_scatter(jnp.dot(picked, weights, precision=lax.Precision.HIGHEST...]
    pallas_call x0 -> x1, Pallas kernels: none -> 85.5 us  [reduce_scatter_ta(): pl.pallas_call(functools.partial(rs_kernel, nz), out_shape=jax.ShapeDtype...]
  transfers between devices with their start and end apart: 3 -> 2, of which waited for: 2 -> 1; matrix products, arithmetic and copies ran while one was open for 2% -> 3% of each run, Pallas kernels for 0% -> 0%
where the time goes in v1:
time: 167 us
  Pallas kernels  85.5 us (51%)
  waiting for transfers between devices  25.6 us (15%)
  local copies, waits for them, and re-layouts  22.4 us (13%)
  other arithmetic  17.4 us (10%)
  starting transfers between devices  8.1 us (5%)
  matrix products  7.49 us (4%)
    pallas_call x1, Pallas kernels, reduce_scatter_ta(): pl.pallas_call(functools.partial(rs_kernel, nz), out_shape=jax.ShapeDtype...  85.5 us
    ppermute x1, waiting for transfers between devices, with_halo(): before = lax.ppermute(last, axis, up)  25.6 us
    gather x1, local copies, waits for them, and re-layouts, shards(): picked = signal.reshape(slab_cells, time_local)[brain_voxels]  14.2 us
    add x2, other arithmetic, smooth_along(): summed + kernel[shift_k] * lax.slice_in_dim(padded, shift_k, shift_k + ex...  10.4 us
    dot_general x1, matrix products, shards(): jnp.dot(picked, weights, precision=lax.Precision.HIGHEST, preferred_eleme...  7.49 us
    add x1, other arithmetic, smooth_planes(): summed + kernel[shift_k] * padded[shift_k:shift_k + planes].astype(jnp.fl...  6.33 us
    ppermute x1, starting transfers between devices, with_halo(): after = lax.ppermute(initial, axis, down)  6.05 us
  transfers between devices with their start and end apart: 2, of which 1 were waited for; matrix products, arithmetic and copies ran while one was open for 3% of the time, Pallas kernels for 0%

profile of v1, /device:TPU:24, one launch (start us, length us, event | category | flops | bytes accessed | tf_op | source)
XLA Modules:
  0.0 166.6 jit_solution(4251299600167600810)
XLA Ops:
  0.0 0.0 copy-start
  0.0 0.0 copy-start.1
  0.0 2.3 %fusion.16 = (bf16[2,24,40,384]{3,2,1,0:T(8,128)(2,1)S(1)}, bf16[2,24,40,384]{3,2,1,0:T(8,128)(2,1)S(1)}) fusion(bf16[6,24,40,384]{3,2,1,0:T(8,128)(2,1)} %param.3), kind=kLoop, calls=%fused_computation.32 | loop fusion | bytes 5898240 | tf_op jit(solution)/shard_map/slice | solution.py:20
  2.3 2.1 %collective-permute-start = (bf16[2,24,40,384]{3,2,1,0:T(8,128)(2,1)S(1)}, bf16[2,24,40,384]{3,2,1,0:T(8,128)(2,1)S(1)}, u32[]{:S(2)}, u32[]{:S(2)}) collective-permute-start(bf16[2,24,40,384]{3,2,1,0:T(8,128)(2,1)S(1)} %get-tuple-element.7), channel_id=1, source_target_pairs={{0,32},{32,64},{64,96},{96,128},{128,160},{160,192},{192,224},{224... | collective-permute-start | bytes 4423688 | tf_op jit(solution)/shard_map/ppermute | solution.py:22
  4.3 6.0 %collective-permute-start.1 = (bf16[2,24,40,384]{3,2,1,0:T(8,128)(2,1)S(1)}, bf16[2,24,40,384]{3,2,1,0:T(8,128)(2,1)S(1)}, u32[]{:S(2)}, u32[]{:S(2)}) collective-permute-start(bf16[2,24,40,384]{3,2,1,0:T(8,128)(2,1)S(1)} %get-tuple-element.8), channel_id=1, source_target_pairs={{32,0},{64,32},{96,64},{128,96},{160,128},{192,160},{224,192},{256... | collective-permute-start | bytes 4423688 | tf_op jit(solution)/shard_map/ppermute | solution.py:23
  10.4 0.7 compare_select_fusion
  11.1 25.6 %collective-permute-done = bf16[2,24,40,384]{3,2,1,0:T(8,128)(2,1)S(1)} collective-permute-done((bf16[2,24,40,384]{3,2,1,0:T(8,128)(2,1)S(1)}, bf16[2,24,40,384]{3,2,1,0:T(8,128)(2,1)S(1)}, u32[]{:S(2)}, u32[]{:S(2)}) %collective-permute-start) | collective-permute-done | bytes 1474592 | tf_op jit(solution)/shard_map/ppermute | solution.py:22
  36.7 1.3 constant_dynamic-update-slice_fusion.1
  38.0 0.0 copy-done.1
  38.0 2.8 %constant_dynamic-update-slice_fusion = (bf16[8,24,40,384]{3,2,1,0:T(8,128)(2,1)}, bf16[8,24,40,384]{3,2,1,0:T(8,128)(2,1)S(1)}) fusion(bf16[8,24,40,384]{3,2,1,0:T(8,128)(2,1)} %constant_dynamic-update-slice_fusion.1, bf16[6,24,40,384]{3,2,1,0:T(8,128)(2,1)S(1)} %copy-done.1), kind=kLoop, calls=%fused_computation.28 | loop fusion | bytes 13271040 | tf_op jit(solution)/shard_map/concatenate | solution.py:24
  40.8 0.0 collective-permute-done.1
  40.8 0.3 constant_dynamic-update-slice_fusion.2
  41.1 6.3 %multiply_add_fusion = f32[6,24,40,384]{3,2,1,0:T(8,128)S(1)} fusion(bf16[6,24,40,384]{3,2,1,0:T(8,128)(2,1)S(1)} %copy-done.1, bf16[8,24,40,384]{3,2,1,0:T(8,128)(2,1)S(1)} %constant_dynamic-update-slice_fusion.2, bf16[8,24,40,384]{3,2,1,0:T(8,128)(2,1)} %get-tuple-element.5), kind=kLoop, calls=%fused_computation.25 | loop fusion | flops 30965760 | bytes 30965760 | tf_op jit(solution)/shard_map/add | solution.py:51
  47.5 3.6 %fusion.4 = f32[6,24,40,384]{3,2,1,0:T(8,128)S(1)} fusion(f32[6,24,40,384]{3,2,1,0:T(8,128)S(1)} %multiply_add_fusion), kind=kLoop, calls=%fused_computation.13 | loop fusion | flops 19906560 | bytes 17694720 | tf_op jit(solution)/shard_map/add | solution.py:42
  51.0 6.8 %fusion.12 = f32[6,24,40,384]{3,2,1,0:T(8,128)} fusion(f32[6,24,40,384]{3,2,1,0:T(8,128)S(1)} %fusion.4), kind=kLoop, calls=%fused_computation.21 | loop fusion | flops 19906560 | bytes 17694720 | tf_op jit(solution)/shard_map/add | solution.py:42
  57.8 14.2 %gather_fusion = f32[3584,384]{1,0:T(8,128)} fusion(f32[5760,384]{1,0:T(8,128)} %bitcast.4, s32[4096]{0:T(1024)S(1)} %pad_clamp_fusion), kind=kCustom, calls=%fused_computation | custom fusion | bytes 11024384 | tf_op jit(solution)/shard_map/gather | solution.py:156
  72.0 0.0 copy-done
  72.0 7.5 %fusion.17 = f32[3584,256]{1,0:T(8,128)} fusion(f32[3584,384]{1,0:T(8,128)} %gather_fusion, bf16[384,256]{1,0:T(8,128)(2,1)S(1)} %copy-done), kind=kOutput, calls=%fused_computation.33 | convolution fusion | flops 4227858432 | bytes 9371648 | tf_op jit(solution)/shard_map/dot_general | solution.py:157
  79.5 85.5 %shard_map.37 = f32[112,256]{1,0:T(8,128)} custom-call(f32[32,112,256]{2,1,0:T(8,128)} %bitcast.5), custom_call_target="tpu_custom_call" | custom-call | tf_op jit(solution)/shard_map/pallas_call | solution.py:128
  165.0 1.6 copy.7
  (1 shorter events, 0.0 us)
Async XLA Ops:
  0.0 72.0 %copy-start = (bf16[384,256]{1,0:T(8,128)(2,1)S(1)}, bf16[384,256]{1,0:T(8,128)(2,1)}, u32[]{:S(2)}) copy-start(bf16[384,256]{1,0:T(8,128)(2,1)} %param.4) | copy-start | bytes 589828
  0.0 38.0 %copy-start.1 = (bf16[6,24,40,384]{3,2,1,0:T(8,128)(2,1)S(1)}, bf16[6,24,40,384]{3,2,1,0:T(8,128)(2,1)}, u32[]{:S(2)}) copy-start(bf16[6,24,40,384]{3,2,1,0:T(8,128)(2,1)} %param.3) | copy-start | bytes 13271044
  2.3 34.4 %collective-permute-start = (bf16[2,24,40,384]{3,2,1,0:T(8,128)(2,1)S(1)}, bf16[2,24,40,384]{3,2,1,0:T(8,128)(2,1)S(1)}, u32[]{:S(2)}, u32[]{:S(2)}) collective-permute-start(bf16[2,24,40,384]{3,2,1,0:T(8,128)(2,1)S(1)} %get-tuple-element.7), channel_id=1, source_target_pairs={{0,32},{32,64},{64,96},{96,128},{128,160},{160,192},{192,224},{224... | collective-permute-start | bytes 4423688 | tf_op jit(solution)/shard_map/ppermute | solution.py:22
  4.3 36.5 %collective-permute-start.1 = (bf16[2,24,40,384]{3,2,1,0:T(8,128)(2,1)S(1)}, bf16[2,24,40,384]{3,2,1,0:T(8,128)(2,1)S(1)}, u32[]{:S(2)}, u32[]{:S(2)}) collective-permute-start(bf16[2,24,40,384]{3,2,1,0:T(8,128)(2,1)S(1)} %get-tuple-element.8), channel_id=1, source_target_pairs={{32,0},{64,32},{96,64},{128,96},{160,128},{192,160},{224,192},{256... | collective-permute-start | bytes 4423688 | tf_op jit(solution)/shard_map/ppermute | solution.py:23

commit v2 on v1

--- a/solution.py
+++ b/solution.py
@@ -148,15 +148,15 @@
     kernel = kernel_taps()
     planes, width_x, width_y, time_local = volume.shape
     slab_cells = planes * width_x * width_y
-    weights = sketch_matrix.astype(jnp.float32)
+    rank = sketch_matrix.shape[1]
     padded = with_halo(volume, (("gz", 0),), 2)
-    signal = smooth_planes(padded, planes, kernel)
+    projected = jnp.dot(
+        padded.reshape(-1, time_local), sketch_matrix, preferred_element_type=jnp.float32
+    ).reshape(planes + 4, width_x, width_y, rank)
+    signal = smooth_planes(projected, planes, kernel)
     signal = smooth_along(signal, 1, kernel)
     signal = smooth_along(signal, 2, kernel)
-    picked = signal.reshape(slab_cells, time_local)[brain_voxels]
-    partial = jnp.dot(
-        picked, weights, precision=lax.Precision.HIGHEST, preferred_element_type=jnp.float32
-    )
+    partial = signal.reshape(slab_cells, rank)[brain_voxels]
     return reduce_scatter_ta(partial, lax.axis_size("ta"))
 
 

time: 167 us -> 151 us (0.904)
  local copies, waits for them, and re-layouts: 22.4 us -> 15.9 us
  other arithmetic: 17.4 us -> 11.3 us
  matrix products: 7.49 us -> 2.71 us
  waiting for transfers between devices: 25.6 us -> 29 us
  Pallas kernels: 85.5 us -> 82.5 us
    dot_general x1, matrix products: 7.49 us -> 2.71 us  [shards(): jnp.dot(padded.reshape(-1, time_local), sketch_matrix, preferred_element_...]
    add x1, other arithmetic: 6.33 us -> 2.18 us  [smooth_planes(): summed + kernel[shift_k] * padded[shift_k:shift_k + planes].astype(jnp.fl...]
    concatenate x2 -> x0, local copies, waits for them, and re-layouts: 3.14 us -> none  [with_halo(): shard = jnp.concatenate([before, shard, after], axis=dim)]
    pallas_call x1, Pallas kernels: 85.5 us -> 82.5 us  [reduce_scatter_ta(): pl.pallas_call(functools.partial(rs_kernel, nz), out_shape=jax.ShapeDtype...]
    ppermute x1, waiting for transfers between devices: 0.01 us -> 2.73 us  [with_halo(): after = lax.ppermute(initial, axis, down)]
    add x2, other arithmetic: 10.4 us -> 7.99 us  [smooth_along(): summed + kernel[shift_k] * lax.slice_in_dim(padded, shift_k, shift_k + ex...]
    gather x1, local copies, waits for them, and re-layouts: 14.2 us -> 12.1 us  [shards(): partial = signal.reshape(slab_cells, rank)[brain_voxels]]
  transfers between devices with their start and end apart: 2 -> 2, of which waited for: 1 -> 2; matrix products, arithmetic and copies ran while one was open for 3% -> 0% of each run, Pallas kernels for 0% -> 0%
where the time goes in v2:
time: 151 us; the launch traced here: 150 us
  Pallas kernels  82.5 us (55%)
  waiting for transfers between devices  29 us (19%)
  local copies, waits for them, and re-layouts  15.9 us (11%)
  other arithmetic  11.3 us (7%)
  starting transfers between devices  8.1 us (5%)
  matrix products  2.71 us (2%)
    pallas_call x1, Pallas kernels, reduce_scatter_ta(): pl.pallas_call(functools.partial(rs_kernel, nz), out_shape=jax.ShapeDtype...  82.5 us
    ppermute x1, waiting for transfers between devices, with_halo(): before = lax.ppermute(last, axis, up)  26.3 us
    gather x1, local copies, waits for them, and re-layouts, shards(): partial = signal.reshape(slab_cells, rank)[brain_voxels]  12.1 us
    add x2, other arithmetic, smooth_along(): summed + kernel[shift_k] * lax.slice_in_dim(padded, shift_k, shift_k + ex...  7.99 us
    ppermute x1, starting transfers between devices, with_halo(): after = lax.ppermute(initial, axis, down)  6.05 us
  transfers between devices with their start and end apart: 2, of which 2 were waited for; matrix products, arithmetic and copies ran while one was open for 0% of the time, Pallas kernels for 0%

profile of v2, /device:TPU:24, one launch (start us, length us, event | category | flops | bytes accessed | tf_op | source)
XLA Modules:
  0.0 149.6 jit_solution(12368066848426016896)
XLA Ops:
  0.0 0.0 copy-start
  0.0 0.0 copy-start.1
  0.0 0.0 copy-start.2
  0.0 2.3 %fusion.20 = (bf16[2,24,40,384]{3,2,1,0:T(8,128)(2,1)S(1)}, bf16[2,24,40,384]{3,2,1,0:T(8,128)(2,1)S(1)}) fusion(bf16[6,24,40,384]{3,2,1,0:T(8,128)(2,1)} %param.3), kind=kLoop, calls=%fused_computation.37 | loop fusion | bytes 5898240 | tf_op jit(solution)/shard_map/slice | solution.py:20
  2.3 2.1 %collective-permute-start = (bf16[2,24,40,384]{3,2,1,0:T(8,128)(2,1)S(1)}, bf16[2,24,40,384]{3,2,1,0:T(8,128)(2,1)S(1)}, u32[]{:S(2)}, u32[]{:S(2)}) collective-permute-start(bf16[2,24,40,384]{3,2,1,0:T(8,128)(2,1)S(1)} %get-tuple-element.5), channel_id=1, source_target_pairs={{0,32},{32,64},{64,96},{96,128},{128,160},{160,192},{192,224},{224... | collective-permute-start | bytes 4423688 | tf_op jit(solution)/shard_map/ppermute | solution.py:22
  4.3 6.0 %collective-permute-start.1 = (bf16[2,24,40,384]{3,2,1,0:T(8,128)(2,1)S(1)}, bf16[2,24,40,384]{3,2,1,0:T(8,128)(2,1)S(1)}, u32[]{:S(2)}, u32[]{:S(2)}) collective-permute-start(bf16[2,24,40,384]{3,2,1,0:T(8,128)(2,1)S(1)} %get-tuple-element.6), channel_id=1, source_target_pairs={{32,0},{64,32},{96,64},{128,96},{160,128},{192,160},{224,192},{256... | collective-permute-start | bytes 4423688 | tf_op jit(solution)/shard_map/ppermute | solution.py:23
  10.4 0.0 copy-done.2
  10.4 26.3 %collective-permute-done = bf16[2,24,40,384]{3,2,1,0:T(8,128)(2,1)S(1)} collective-permute-done((bf16[2,24,40,384]{3,2,1,0:T(8,128)(2,1)S(1)}, bf16[2,24,40,384]{3,2,1,0:T(8,128)(2,1)S(1)}, u32[]{:S(2)}, u32[]{:S(2)}) %collective-permute-start) | collective-permute-done | bytes 1474592 | tf_op jit(solution)/shard_map/ppermute | solution.py:22
  36.7 2.7 %collective-permute-done.1 = bf16[2,24,40,384]{3,2,1,0:T(8,128)(2,1)S(1)} collective-permute-done((bf16[2,24,40,384]{3,2,1,0:T(8,128)(2,1)S(1)}, bf16[2,24,40,384]{3,2,1,0:T(8,128)(2,1)S(1)}, u32[]{:S(2)}, u32[]{:S(2)}) %collective-permute-start.1) | collective-permute-done | bytes 1474592 | tf_op jit(solution)/shard_map/ppermute | solution.py:23
  39.4 0.0 copy-done.1
  39.4 1.1 pad_maximum_fusion
  40.5 0.0 copy-done
  40.5 2.7 %fusion.21 = f32[9600,256]{1,0:T(8,128)S(1)} fusion(bf16[9600,384]{1,0:T(8,128)(2,1)S(1)} %bitcast.7, bf16[384,256]{1,0:T(8,128)(2,1)S(1)} %copy-done), kind=kOutput, calls=%fused_computation.38 | convolution fusion | flops 1887436800 | bytes 17399808 | tf_op jit(solution)/shard_map/dot_general | solution.py:153
  43.3 2.2 %fusion.16 = f32[5760,256]{1,0:T(8,128)S(1)} fusion(f32[9600,256]{1,0:T(8,128)S(1)} %fusion.21), kind=kLoop, calls=%fused_computation.27 | loop fusion | flops 13271040 | bytes 35389440 | tf_op jit(solution)/shard_map/add | solution.py:51
  45.5 2.8 %fusion.4 = f32[6,24,40,256]{3,2,1,0:T(8,128)S(1)} fusion(f32[6,24,40,256]{3,2,1,0:T(8,128)S(1)} %bitcast.8), kind=kLoop, calls=%fused_computation.14 | loop fusion | flops 13271040 | bytes 11796480 | tf_op jit(solution)/shard_map/add | solution.py:42
  48.2 5.2 %fusion.12 = f32[6,24,40,256]{3,2,1,0:T(8,128)} fusion(f32[6,24,40,256]{3,2,1,0:T(8,128)S(1)} %fusion.4), kind=kLoop, calls=%fused_computation.22 | loop fusion | flops 13271040 | bytes 11796480 | tf_op jit(solution)/shard_map/add | solution.py:42
  53.4 12.1 %gather_fusion = f32[3584,256]{1,0:T(8,128)} fusion(f32[5760,256]{1,0:T(8,128)} %bitcast.6, s32[4096]{0:T(1024)S(1)} %pad_clamp_fusion), kind=kCustom, calls=%fused_computation | custom fusion | bytes 7354368 | tf_op jit(solution)/shard_map/gather | solution.py:159
  65.6 82.5 %shard_map.37 = f32[112,256]{1,0:T(8,128)} custom-call(f32[32,112,256]{2,1,0:T(8,128)} %bitcast.9), custom_call_target="tpu_custom_call" | custom-call | tf_op jit(solution)/shard_map/pallas_call | solution.py:128
  148.0 1.6 %copy.5 = f32[112,256]{1,0:T(8,128)} copy(f32[112,256]{1,0:T(8,128)} %shard_map.37) | data formatting | bytes 229376
  (2 shorter events, 0.0 us)
Async XLA Ops:
  0.0 40.5 %copy-start = (bf16[384,256]{1,0:T(8,128)(2,1)S(1)}, bf16[384,256]{1,0:T(8,128)(2,1)}, u32[]{:S(2)}) copy-start(bf16[384,256]{1,0:T(8,128)(2,1)} %param.4) | copy-start | bytes 589828
  0.0 39.4 %copy-start.1 = (bf16[6,24,40,384]{3,2,1,0:T(8,128)(2,1)S(1)}, bf16[6,24,40,384]{3,2,1,0:T(8,128)(2,1)}, u32[]{:S(2)}) copy-start(bf16[6,24,40,384]{3,2,1,0:T(8,128)(2,1)} %param.3) | copy-start | bytes 13271044
  0.0 10.4 %copy-start.2 = (s32[3584]{0:T(1024)S(1)}, s32[3584]{0:T(1024)}, u32[]{:S(2)}) copy-start(s32[3584]{0:T(1024)} %param.5) | copy-start | bytes 43012
  2.3 34.4 %collective-permute-start = (bf16[2,24,40,384]{3,2,1,0:T(8,128)(2,1)S(1)}, bf16[2,24,40,384]{3,2,1,0:T(8,128)(2,1)S(1)}, u32[]{:S(2)}, u32[]{:S(2)}) collective-permute-start(bf16[2,24,40,384]{3,2,1,0:T(8,128)(2,1)S(1)} %get-tuple-element.5), channel_id=1, source_target_pairs={{0,32},{32,64},{64,96},{96,128},{128,160},{160,192},{192,224},{224... | collective-permute-start | bytes 4423688 | tf_op jit(solution)/shard_map/ppermute | solution.py:22
  4.3 35.1 %collective-permute-start.1 = (bf16[2,24,40,384]{3,2,1,0:T(8,128)(2,1)S(1)}, bf16[2,24,40,384]{3,2,1,0:T(8,128)(2,1)S(1)}, u32[]{:S(2)}, u32[]{:S(2)}) collective-permute-start(bf16[2,24,40,384]{3,2,1,0:T(8,128)(2,1)S(1)} %get-tuple-element.6), channel_id=1, source_target_pairs={{32,0},{64,32},{96,64},{128,96},{160,128},{192,160},{224,192},{256... | collective-permute-start | bytes 4423688 | tf_op jit(solution)/shard_map/ppermute | solution.py:23

commit v3 on v2

--- a/solution.py
+++ b/solution.py
@@ -52,7 +52,7 @@
     return summed
 
 
-def rs_kernel(nz, p_ref, o_ref, recv, send, fin, xrecv, send_sem, recv_sem, credit, xsem):
+def rs_kernel(nz, parts, p_ref, o_ref, recv, send, fin, xrecv, send_sem, recv_sem, credit, xsem):
     gz = lax.axis_index("gz")
     ta = lax.axis_index("ta")
     xl = ta // nz
@@ -60,6 +60,7 @@
     right = xl * nz + (zi + 1) % nz
     left = xl * nz + (zi + nz - 1) % nz
     partner = (1 - xl) * nz + zi
+    rk = recv.shape[3]
 
     barrier = pltpu.get_barrier_semaphore()
     for peer in (left, right, partner):
@@ -72,35 +73,39 @@
     )
     copies = {}
     for s in range(nz):
-        for d, dst, src_peer, chunk in dirs:
-            blk = chunk(s)
-            if s == 0:
-                src = p_ref.at[blk]
-            else:
-                copies[(d, s - 1)].wait_recv()
-                val = recv[d, (s - 1) % 2] + p_ref[blk]
+        for k in range(parts):
+            for d, dst, src_peer, chunk in dirs:
+                blk = chunk(s)
+                own = p_ref.at[blk, pl.ds(k * rk, rk)]
+                if s == 0:
+                    src = own
+                else:
+                    copies[(d, k, s - 1)].wait_recv()
+                    val = recv[d, k, (s - 1) % 2] + own[...]
+                    if s < nz - 1:
+                        if s >= 2:
+                            copies[(d, k, s - 2)].wait_send()
+                        send[d, k, s % 2] = val
+                        src = send.at[d, k, s % 2]
+                        if s <= nz - 3:
+                            pl.semaphore_signal(
+                                credit.at[d, k], 1, device_id=(gz, src_peer), device_id_type=MESH
+                            )
+                    else:
+                        fin[d, pl.ds(k * rk, rk)] = val
                 if s < nz - 1:
                     if s >= 2:
-                        copies[(d, s - 2)].wait_send()
-                    send[d, s % 2] = val
-                    src = send.at[d, s % 2]
-                    if s <= nz - 3:
-                        pl.semaphore_signal(credit.at[d], 1, device_id=(gz, src_peer), device_id_type=MESH)
-                else:
-                    fin[d] = val
-            if s < nz - 1:
-                if s >= 2:
-                    pl.semaphore_wait(credit.at[d], 1)
-                cp = pltpu.make_async_remote_copy(
-                    src_ref=src,
-                    dst_ref=recv.at[d, s % 2],
-                    send_sem=send_sem.at[d, s % 2],
-                    recv_sem=recv_sem.at[d, s % 2],
-                    device_id=(gz, dst),
-                    device_id_type=MESH,
-                )
-                cp.start()
-                copies[(d, s)] = cp
+                        pl.semaphore_wait(credit.at[d, k], 1)
+                    cp = pltpu.make_async_remote_copy(
+                        src_ref=src,
+                        dst_ref=recv.at[d, k, s % 2],
+                        send_sem=send_sem.at[d, k, s % 2],
+                        recv_sem=recv_sem.at[d, k, s % 2],
+                        device_id=(gz, dst),
+                        device_id_type=MESH,
+                    )
+                    cp.start()
+                    copies[(d, k, s)] = cp
 
     xcp = pltpu.make_async_remote_copy(
         src_ref=fin.at[1 - xl],
@@ -112,32 +117,34 @@
     )
     xcp.start()
     for d in range(2):
-        for s in (nz - 3, nz - 2):
-            copies[(d, s)].wait_send()
+        for k in range(parts):
+            for s in (nz - 3, nz - 2):
+                copies[(d, k, s)].wait_send()
     xcp.wait_recv()
     o_ref[...] = fin[xl] + xrecv[...]
     xcp.wait_send()
 
 
-def reduce_scatter_ta(partial, n_ta):
+def reduce_scatter_ta(partial, n_ta, parts=2):
     rows_all, cols = partial.shape
     nz = Z_RING
     assert n_ta == 2 * nz
     rows = rows_all // n_ta
+    rk = rows // parts
     blocks = partial.reshape(n_ta, rows, cols)
     return pl.pallas_call(
-        functools.partial(rs_kernel, nz),
+        functools.partial(rs_kernel, nz, parts),
         out_shape=jax.ShapeDtypeStruct((rows, cols), jnp.float32),
         in_specs=[pl.BlockSpec(memory_space=pltpu.VMEM)],
         out_specs=pl.BlockSpec(memory_space=pltpu.VMEM),
         scratch_shapes=[
-            pltpu.VMEM((2, 2, rows, cols), jnp.float32),
-            pltpu.VMEM((2, 2, rows, cols), jnp.float32),
+            pltpu.VMEM((2, parts, 2, rk, cols), jnp.float32),
+            pltpu.VMEM((2, parts, 2, rk, cols), jnp.float32),
             pltpu.VMEM((2, rows, cols), jnp.float32),
             pltpu.VMEM((rows, cols), jnp.float32),
-            pltpu.SemaphoreType.DMA((2, 2)),
-            pltpu.SemaphoreType.DMA((2, 2)),
-            pltpu.SemaphoreType.REGULAR((2,)),
+            pltpu.SemaphoreType.DMA((2, parts, 2)),
+            pltpu.SemaphoreType.DMA((2, parts, 2)),
+            pltpu.SemaphoreType.REGULAR((2, parts)),
             pltpu.SemaphoreType.DMA((2,)),
         ],
         compiler_params=pltpu.CompilerParams(collective_id=0, has_side_effects=True),

time: 151 us -> 141 us (0.934)
  Pallas kernels: 82.5 us -> 73.5 us
    pallas_call x1, Pallas kernels: 82.5 us -> 73.5 us  [reduce_scatter_ta(): pl.pallas_call(functools.partial(rs_kernel, nz, parts), out_shape=jax.Sha...]
where the time goes in v3:
time: 141 us
  Pallas kernels  73.5 us (52%)
  waiting for transfers between devices  29 us (21%)
  local copies, waits for them, and re-layouts  15.9 us (11%)
  other arithmetic  11.3 us (8%)
  starting transfers between devices  8.1 us (6%)
  matrix products  2.71 us (2%)
    pallas_call x1, Pallas kernels, reduce_scatter_ta(): pl.pallas_call(functools.partial(rs_kernel, nz, parts), out_shape=jax.Sha...  73.5 us
    ppermute x1, waiting for transfers between devices, with_halo(): before = lax.ppermute(last, axis, up)  26.3 us
    gather x1, local copies, waits for them, and re-layouts, shards(): partial = signal.reshape(slab_cells, rank)[brain_voxels]  12.1 us
    add x2, other arithmetic, smooth_along(): summed + kernel[shift_k] * lax.slice_in_dim(padded, shift_k, shift_k + ex...  7.99 us
    ppermute x1, starting transfers between devices, with_halo(): after = lax.ppermute(initial, axis, down)  6.05 us
  transfers between devices with their start and end apart: 2, of which 2 were waited for; matrix products, arithmetic and copies ran while one was open for 0% of the time, Pallas kernels for 0%

profile of v3, /device:TPU:24, one launch (start us, length us, event | category | flops | bytes accessed | tf_op | source)
XLA Modules:
  0.0 140.6 jit_solution(17175773150039926833)
XLA Ops:
  0.0 0.0 copy-start
  0.0 0.0 copy-start.1
  0.0 0.0 copy-start.2
  0.0 2.3 %fusion.20 = (bf16[2,24,40,384]{3,2,1,0:T(8,128)(2,1)S(1)}, bf16[2,24,40,384]{3,2,1,0:T(8,128)(2,1)S(1)}) fusion(bf16[6,24,40,384]{3,2,1,0:T(8,128)(2,1)} %param.3), kind=kLoop, calls=%fused_computation.37 | loop fusion | bytes 5898240 | tf_op jit(solution)/shard_map/slice | solution.py:20
  2.3 2.1 %collective-permute-start = (bf16[2,24,40,384]{3,2,1,0:T(8,128)(2,1)S(1)}, bf16[2,24,40,384]{3,2,1,0:T(8,128)(2,1)S(1)}, u32[]{:S(2)}, u32[]{:S(2)}) collective-permute-start(bf16[2,24,40,384]{3,2,1,0:T(8,128)(2,1)S(1)} %get-tuple-element.5), channel_id=1, source_target_pairs={{0,32},{32,64},{64,96},{96,128},{128,160},{160,192},{192,224},{224... | collective-permute-start | bytes 4423688 | tf_op jit(solution)/shard_map/ppermute | solution.py:22
  4.3 6.0 %collective-permute-start.1 = (bf16[2,24,40,384]{3,2,1,0:T(8,128)(2,1)S(1)}, bf16[2,24,40,384]{3,2,1,0:T(8,128)(2,1)S(1)}, u32[]{:S(2)}, u32[]{:S(2)}) collective-permute-start(bf16[2,24,40,384]{3,2,1,0:T(8,128)(2,1)S(1)} %get-tuple-element.6), channel_id=1, source_target_pairs={{32,0},{64,32},{96,64},{128,96},{160,128},{192,160},{224,192},{256... | collective-permute-start | bytes 4423688 | tf_op jit(solution)/shard_map/ppermute | solution.py:23
  10.4 0.0 copy-done.2
  10.4 26.3 %collective-permute-done = bf16[2,24,40,384]{3,2,1,0:T(8,128)(2,1)S(1)} collective-permute-done((bf16[2,24,40,384]{3,2,1,0:T(8,128)(2,1)S(1)}, bf16[2,24,40,384]{3,2,1,0:T(8,128)(2,1)S(1)}, u32[]{:S(2)}, u32[]{:S(2)}) %collective-permute-start) | collective-permute-done | bytes 1474592 | tf_op jit(solution)/shard_map/ppermute | solution.py:22
  36.7 2.7 %collective-permute-done.1 = bf16[2,24,40,384]{3,2,1,0:T(8,128)(2,1)S(1)} collective-permute-done((bf16[2,24,40,384]{3,2,1,0:T(8,128)(2,1)S(1)}, bf16[2,24,40,384]{3,2,1,0:T(8,128)(2,1)S(1)}, u32[]{:S(2)}, u32[]{:S(2)}) %collective-permute-start.1) | collective-permute-done | bytes 1474592 | tf_op jit(solution)/shard_map/ppermute | solution.py:23
  39.4 0.0 copy-done.1
  39.4 1.1 pad_maximum_fusion
  40.5 0.0 copy-done
  40.5 2.7 %fusion.21 = f32[9600,256]{1,0:T(8,128)S(1)} fusion(bf16[9600,384]{1,0:T(8,128)(2,1)S(1)} %bitcast.7, bf16[384,256]{1,0:T(8,128)(2,1)S(1)} %copy-done), kind=kOutput, calls=%fused_computation.38 | convolution fusion | flops 1887436800 | bytes 17399808 | tf_op jit(solution)/shard_map/dot_general | solution.py:160
  43.3 2.2 %fusion.16 = f32[5760,256]{1,0:T(8,128)S(1)} fusion(f32[9600,256]{1,0:T(8,128)S(1)} %fusion.21), kind=kLoop, calls=%fused_computation.27 | loop fusion | flops 13271040 | bytes 35389440 | tf_op jit(solution)/shard_map/add | solution.py:51
  45.5 2.8 %fusion.4 = f32[6,24,40,256]{3,2,1,0:T(8,128)S(1)} fusion(f32[6,24,40,256]{3,2,1,0:T(8,128)S(1)} %bitcast.8), kind=kLoop, calls=%fused_computation.14 | loop fusion | flops 13271040 | bytes 11796480 | tf_op jit(solution)/shard_map/add | solution.py:42
  48.2 5.2 %fusion.12 = f32[6,24,40,256]{3,2,1,0:T(8,128)} fusion(f32[6,24,40,256]{3,2,1,0:T(8,128)S(1)} %fusion.4), kind=kLoop, calls=%fused_computation.22 | loop fusion | flops 13271040 | bytes 11796480 | tf_op jit(solution)/shard_map/add | solution.py:42
  53.4 12.1 %gather_fusion = f32[3584,256]{1,0:T(8,128)} fusion(f32[5760,256]{1,0:T(8,128)} %bitcast.6, s32[4096]{0:T(1024)S(1)} %pad_clamp_fusion), kind=kCustom, calls=%fused_computation | custom fusion | bytes 7354368 | tf_op jit(solution)/shard_map/gather | solution.py:166
  65.6 73.5 %shard_map.37 = f32[112,256]{1,0:T(8,128)} custom-call(f32[32,112,256]{2,1,0:T(8,128)} %bitcast.9), custom_call_target="tpu_custom_call" | custom-call | tf_op jit(solution)/shard_map/pallas_call | solution.py:135
  139.0 1.6 %copy.5 = f32[112,256]{1,0:T(8,128)} copy(f32[112,256]{1,0:T(8,128)} %shard_map.37) | data formatting | bytes 229376
  (2 shorter events, 0.0 us)
Async XLA Ops:
  0.0 40.5 %copy-start = (bf16[384,256]{1,0:T(8,128)(2,1)S(1)}, bf16[384,256]{1,0:T(8,128)(2,1)}, u32[]{:S(2)}) copy-start(bf16[384,256]{1,0:T(8,128)(2,1)} %param.4) | copy-start | bytes 589828
  0.0 39.4 %copy-start.1 = (bf16[6,24,40,384]{3,2,1,0:T(8,128)(2,1)S(1)}, bf16[6,24,40,384]{3,2,1,0:T(8,128)(2,1)}, u32[]{:S(2)}) copy-start(bf16[6,24,40,384]{3,2,1,0:T(8,128)(2,1)} %param.3) | copy-start | bytes 13271044
  0.0 10.4 %copy-start.2 = (s32[3584]{0:T(1024)S(1)}, s32[3584]{0:T(1024)}, u32[]{:S(2)}) copy-start(s32[3584]{0:T(1024)} %param.5) | copy-start | bytes 43012
  2.3 34.4 %collective-permute-start = (bf16[2,24,40,384]{3,2,1,0:T(8,128)(2,1)S(1)}, bf16[2,24,40,384]{3,2,1,0:T(8,128)(2,1)S(1)}, u32[]{:S(2)}, u32[]{:S(2)}) collective-permute-start(bf16[2,24,40,384]{3,2,1,0:T(8,128)(2,1)S(1)} %get-tuple-element.5), channel_id=1, source_target_pairs={{0,32},{32,64},{64,96},{96,128},{128,160},{160,192},{192,224},{224... | collective-permute-start | bytes 4423688 | tf_op jit(solution)/shard_map/ppermute | solution.py:22
  4.3 35.1 %collective-permute-start.1 = (bf16[2,24,40,384]{3,2,1,0:T(8,128)(2,1)S(1)}, bf16[2,24,40,384]{3,2,1,0:T(8,128)(2,1)S(1)}, u32[]{:S(2)}, u32[]{:S(2)}) collective-permute-start(bf16[2,24,40,384]{3,2,1,0:T(8,128)(2,1)S(1)} %get-tuple-element.6), channel_id=1, source_target_pairs={{32,0},{64,32},{96,64},{128,96},{160,128},{192,160},{224,192},{256... | collective-permute-start | bytes 4423688 | tf_op jit(solution)/shard_map/ppermute | solution.py:23

commit v4 on v3

--- a/solution.py
+++ b/solution.py
@@ -10,19 +10,6 @@
 
 MESH = pl.DeviceIdType.MESH
 Z_RING = 16
-
-
-def with_halo(shard, sides, width):
-    for axis, dim in sides:
-        peers, length = (lax.axis_size(axis), shard.shape[dim])
-        up = [(i, (i + 1) % peers) for i in range(peers - 1)]
-        down = [(j, i) for i, j in up]
-        last = lax.slice_in_dim(shard, length - width, length, axis=dim)
-        initial = lax.slice_in_dim(shard, 0, width, axis=dim)
-        before = lax.ppermute(last, axis, up)
-        after = lax.ppermute(initial, axis, down)
-        shard = jnp.concatenate([before, shard, after], axis=dim)
-    return shard
 
 
 def kernel_taps():
@@ -151,18 +138,33 @@
     )(blocks)
 
 
+def exchange_halo(shard, axis, width):
+    peers, length = lax.axis_size(axis), shard.shape[0]
+    up = [(i, i + 1) for i in range(peers - 1)]
+    down = [(j, i) for i, j in up]
+    below = lax.ppermute(shard[length - width :], axis, up)
+    above = lax.ppermute(shard[:width], axis, down)
+    return below, above
+
+
+def project_smooth_xy(planes_bf16, sketch_matrix, kernel):
+    count, width_x, width_y, time_local = planes_bf16.shape
+    projected = jnp.dot(
+        planes_bf16.reshape(-1, time_local), sketch_matrix, preferred_element_type=jnp.float32
+    ).reshape(count, width_x, width_y, sketch_matrix.shape[1])
+    return smooth_along(smooth_along(projected, 1, kernel), 2, kernel)
+
+
 def shards(volume, sketch_matrix, brain_voxels):
     kernel = kernel_taps()
     planes, width_x, width_y, time_local = volume.shape
     slab_cells = planes * width_x * width_y
     rank = sketch_matrix.shape[1]
-    padded = with_halo(volume, (("gz", 0),), 2)
-    projected = jnp.dot(
-        padded.reshape(-1, time_local), sketch_matrix, preferred_element_type=jnp.float32
-    ).reshape(planes + 4, width_x, width_y, rank)
-    signal = smooth_planes(projected, planes, kernel)
-    signal = smooth_along(signal, 1, kernel)
-    signal = smooth_along(signal, 2, kernel)
+    below, above = exchange_halo(volume, "gz", 2)
+    local = project_smooth_xy(volume, sketch_matrix, kernel)
+    halo = project_smooth_xy(jnp.concatenate([below, above]), sketch_matrix, kernel)
+    padded = jnp.concatenate([halo[:2], local, halo[2:]])
+    signal = smooth_planes(padded, planes, kernel)
     partial = signal.reshape(slab_cells, rank)[brain_voxels]
     return reduce_scatter_ta(partial, lax.axis_size("ta"))
 

time: 141 us -> 138 us (0.979)
  waiting for transfers between devices: 29 us -> 21.2 us
  other arithmetic: 11.3 us -> 14.8 us
  local copies, waits for them, and re-layouts: 15.9 us -> 17.8 us
    ppermute x2, waiting for transfers between devices: 29 us -> 21.2 us  [the longest x1 18.4 us: exchange_halo(): below = lax.ppermute(shard[length - width:], axis, up)]
    add x2 -> x4, other arithmetic: 7.99 us -> 10.7 us  [smooth_along(): summed + kernel[shift_k] * lax.slice_in_dim(padded, shift_k, shift_k + ex...]
    add x1, other arithmetic: 2.18 us -> 4.12 us  [smooth_planes(): summed + kernel[shift_k] * padded[shift_k:shift_k + planes].astype(jnp.fl...]
    slice x1 -> x2, local copies, waits for them, and re-layouts: 2.27 us -> 4.11 us  [the longest x1 3.86 us: exchange_halo(): below = lax.ppermute(shard[length - width:], axis, up)]
    dot_general x1 -> x2, matrix products: 2.71 us -> 2.92 us  [project_smooth_xy(): jnp.dot(planes_bf16.reshape(-1, time_local), sketch_matrix, preferred_ele...]
  transfers between devices with their start and end apart: 2 -> 2, of which waited for: 2 -> 2; matrix products, arithmetic and copies ran while one was open for 0% -> 6% of each run, Pallas kernels for 0% -> 0%
where the time goes in v4:
time: 138 us
  Pallas kernels  72.7 us (53%)
  waiting for transfers between devices  21.2 us (15%)
  local copies, waits for them, and re-layouts  17.8 us (13%)
  other arithmetic  14.8 us (11%)
  starting transfers between devices  8.08 us (6%)
  matrix products  2.92 us (2%)
    pallas_call x1, Pallas kernels, reduce_scatter_ta(): pl.pallas_call(functools.partial(rs_kernel, nz, parts), out_shape=jax.Sha...  72.7 us
    ppermute x1, waiting for transfers between devices, exchange_halo(): below = lax.ppermute(shard[length - width:], axis, up)  18.4 us
    gather x1, local copies, waits for them, and re-layouts, shards(): partial = signal.reshape(slab_cells, rank)[brain_voxels]  12.1 us
    add x4, other arithmetic, smooth_along(): summed + kernel[shift_k] * lax.slice_in_dim(padded, shift_k, shift_k + ex...  10.7 us
    ppermute x1, starting transfers between devices, exchange_halo(): above = lax.ppermute(shard[:width], axis, down)  6.04 us
    add x1, other arithmetic, smooth_planes(): summed + kernel[shift_k] * padded[shift_k:shift_k + planes].astype(jnp.fl...  4.12 us
    slice x1, local copies, waits for them, and re-layouts, exchange_halo(): below = lax.ppermute(shard[length - width:], axis, up)  3.86 us
    dot_general x2, matrix products, project_smooth_xy(): jnp.dot(planes_bf16.reshape(-1, time_local), sketch_matrix, preferred_ele...  2.92 us
  transfers between devices with their start and end apart: 2, of which 2 were waited for; matrix products, arithmetic and copies ran while one was open for 6% of the time, Pallas kernels for 0%

profile of v4, /device:TPU:24, one launch (start us, length us, event | category | flops | bytes accessed | tf_op | source)
XLA Modules:
  0.0 137.7 jit_solution(2314763504883697755)
XLA Ops:
  0.0 0.0 copy-start
  0.0 0.0 copy-start.1
  0.0 3.9 %fusion.50 = (bf16[2,24,40,384]{3,2,1,0:T(8,128)(2,1)}, bf16[2,24,40,384]{3,2,1,0:T(8,128)(2,1)}) fusion(bf16[6,24,40,384]{3,2,1,0:T(8,128)(2,1)} %param.3), kind=kLoop, calls=%fused_computation.75 | loop fusion | bytes 5898240 | tf_op jit(solution)/shard_map/slice | solution.py:145
  3.9 0.0 copy-start.2
  3.9 2.0 %collective-permute-start = (bf16[2,24,40,384]{3,2,1,0:T(8,128)(2,1)}, bf16[2,24,40,384]{3,2,1,0:T(8,128)(2,1)S(1)}, u32[]{:S(2)}, u32[]{:S(2)}) collective-permute-start(bf16[2,24,40,384]{3,2,1,0:T(8,128)(2,1)} %get-tuple-element.5), channel_id=1, source_target_pairs={{0,32},{32,64},{64,96},{96,128},{128,160},{160,192},{192,224},{224... | collective-permute-start | bytes 4423688 | tf_op jit(solution)/shard_map/ppermute | solution.py:145
  5.9 6.0 %collective-permute-start.1 = (bf16[2,24,40,384]{3,2,1,0:T(8,128)(2,1)}, bf16[2,24,40,384]{3,2,1,0:T(8,128)(2,1)S(1)}, u32[]{:S(2)}, u32[]{:S(2)}) collective-permute-start(bf16[2,24,40,384]{3,2,1,0:T(8,128)(2,1)} %get-tuple-element.6), channel_id=1, source_target_pairs={{32,0},{64,32},{96,64},{128,96},{160,128},{192,160},{224,192},{256... | collective-permute-start | bytes 4423688 | tf_op jit(solution)/shard_map/ppermute | solution.py:146
  12.0 0.0 copy-done
  12.0 0.0 copy-done.1
  12.0 1.7 %fusion.46 = f32[6,24,40,256]{3,2,1,0:T(8,128)S(1)} fusion(bf16[6,24,40,384]{3,2,1,0:T(8,128)(2,1)S(1)} %copy-done.1, bf16[384,256]{1,0:T(8,128)(2,1)S(1)} %copy-done), kind=kOutput, calls=%fused_computation.69 | convolution fusion | flops 1132462080 | bytes 10518528 | tf_op jit(solution)/shard_map/dot_general | solution.py:152
  13.7 0.0 copy-done.2
  13.7 2.8 %fusion.4 = f32[6,24,40,256]{3,2,1,0:T(8,128)S(1)} fusion(f32[6,24,40,256]{3,2,1,0:T(8,128)S(1)} %fusion.46), kind=kLoop, calls=%fused_computation.17 | loop fusion | flops 13271040 | bytes 11796480 | tf_op jit(solution)/shard_map/add | solution.py:29
  16.5 3.6 %fusion.12 = f32[6,24,40,256]{3,2,1,0:T(8,128)S(1)} fusion(f32[6,24,40,256]{3,2,1,0:T(8,128)S(1)} %fusion.4), kind=kLoop, calls=%fused_computation.25 | loop fusion | flops 13271040 | bytes 11796480 | tf_op jit(solution)/shard_map/add | solution.py:29
  20.1 18.4 %collective-permute-done = bf16[2,24,40,384]{3,2,1,0:T(8,128)(2,1)S(1)} collective-permute-done((bf16[2,24,40,384]{3,2,1,0:T(8,128)(2,1)}, bf16[2,24,40,384]{3,2,1,0:T(8,128)(2,1)S(1)}, u32[]{:S(2)}, u32[]{:S(2)}) %collective-permute-start) | collective-permute-done | bytes 1474592 | tf_op jit(solution)/shard_map/ppermute | solution.py:145
  38.5 2.8 %collective-permute-done.1 = bf16[2,24,40,384]{3,2,1,0:T(8,128)(2,1)S(1)} collective-permute-done((bf16[2,24,40,384]{3,2,1,0:T(8,128)(2,1)}, bf16[2,24,40,384]{3,2,1,0:T(8,128)(2,1)S(1)}, u32[]{:S(2)}, u32[]{:S(2)}) %collective-permute-start.1) | collective-permute-done | bytes 1474592 | tf_op jit(solution)/shard_map/ppermute | solution.py:146
  41.3 1.2 fusion.42
  42.5 2.0 %fusion.30 = f32[4,24,40,256]{3,2,1,0:T(8,128)S(1)} fusion(f32[4,24,40,256]{3,2,1,0:T(8,128)S(1)} %fusion.42), kind=kLoop, calls=%fused_computation.53 | loop fusion | flops 8847360 | bytes 7864320 | tf_op jit(solution)/shard_map/add | solution.py:29
  44.5 2.3 %fusion.38 = f32[4,24,40,256]{3,2,1,0:T(8,128)S(1)} fusion(f32[4,24,40,256]{3,2,1,0:T(8,128)S(1)} %fusion.30), kind=kLoop, calls=%fused_computation.61 | loop fusion | flops 8847360 | bytes 7864320 | tf_op jit(solution)/shard_map/add | solution.py:29
  46.9 0.3 fusion.51
  47.1 4.1 %fusion.19 = f32[6,24,40,256]{3,2,1,0:T(8,128)} fusion(f32[6,24,40,256]{3,2,1,0:T(8,128)S(1)} %fusion.12, f32[2,24,40,256]{3,2,1,0:T(8,128)S(1)} %get-tuple-element.8, f32[2,24,40,256]{3,2,1,0:T(8,128)S(1)} %get-tuple-element.7), kind=kLoop, calls=%fused_computation.32 | loop fusion | flops 19169280 | bytes 15728640 | tf_op jit(solution)/shard_map/add | solution.py:38
  51.3 12.1 %gather_fusion = f32[3584,256]{1,0:T(8,128)} fusion(f32[5760,256]{1,0:T(8,128)} %bitcast.10, s32[4096]{0:T(1024)S(1)} %pad_clamp_fusion), kind=kCustom, calls=%fused_computation | custom fusion | bytes 7354368 | tf_op jit(solution)/shard_map/gather | solution.py:168
  63.4 72.7 %shard_map.37 = f32[112,256]{1,0:T(8,128)} custom-call(f32[32,112,256]{2,1,0:T(8,128)} %bitcast.11), custom_call_target="tpu_custom_call" | custom-call | tf_op jit(solution)/shard_map/pallas_call | solution.py:122
  136.1 1.6 %copy.6 = f32[112,256]{1,0:T(8,128)} copy(f32[112,256]{1,0:T(8,128)} %shard_map.37) | data formatting | bytes 229376
  (2 shorter events, 0.0 us)
Async XLA Ops:
  0.0 12.0 %copy-start = (bf16[384,256]{1,0:T(8,128)(2,1)S(1)}, bf16[384,256]{1,0:T(8,128)(2,1)}, u32[]{:S(2)}) copy-start(bf16[384,256]{1,0:T(8,128)(2,1)} %param.4) | copy-start | bytes 589828
  0.0 12.0 %copy-start.1 = (bf16[6,24,40,384]{3,2,1,0:T(8,128)(2,1)S(1)}, bf16[6,24,40,384]{3,2,1,0:T(8,128)(2,1)}, u32[]{:S(2)}) copy-start(bf16[6,24,40,384]{3,2,1,0:T(8,128)(2,1)} %param.3) | copy-start | bytes 13271044
  3.9 9.8 %copy-start.2 = (s32[3584]{0:T(1024)S(1)}, s32[3584]{0:T(1024)}, u32[]{:S(2)}) copy-start(s32[3584]{0:T(1024)} %param.5) | copy-start | bytes 43012
  3.9 34.6 %collective-permute-start = (bf16[2,24,40,384]{3,2,1,0:T(8,128)(2,1)}, bf16[2,24,40,384]{3,2,1,0:T(8,128)(2,1)S(1)}, u32[]{:S(2)}, u32[]{:S(2)}) collective-permute-start(bf16[2,24,40,384]{3,2,1,0:T(8,128)(2,1)} %get-tuple-element.5), channel_id=1, source_target_pairs={{0,32},{32,64},{64,96},{96,128},{128,160},{160,192},{192,224},{224... | collective-permute-start | bytes 4423688 | tf_op jit(solution)/shard_map/ppermute | solution.py:145
  5.9 35.4 %collective-permute-start.1 = (bf16[2,24,40,384]{3,2,1,0:T(8,128)(2,1)}, bf16[2,24,40,384]{3,2,1,0:T(8,128)(2,1)S(1)}, u32[]{:S(2)}, u32[]{:S(2)}) collective-permute-start(bf16[2,24,40,384]{3,2,1,0:T(8,128)(2,1)} %get-tuple-element.6), channel_id=1, source_target_pairs={{32,0},{64,32},{96,64},{128,96},{160,128},{192,160},{224,192},{256... | collective-permute-start | bytes 4423688 | tf_op jit(solution)/shard_map/ppermute | solution.py:146

commit v5 on v4

--- a/solution.py
+++ b/solution.py
@@ -112,7 +112,7 @@
     xcp.wait_send()
 
 
-def reduce_scatter_ta(partial, n_ta, parts=2):
+def reduce_scatter_ta(partial, n_ta, parts=7):
     rows_all, cols = partial.shape
     nz = Z_RING
     assert n_ta == 2 * nz

time: 138 us -> 133 us (0.964)
  Pallas kernels: 72.7 us -> 67.4 us
    pallas_call x1, Pallas kernels: 72.7 us -> 67.4 us  [reduce_scatter_ta(): pl.pallas_call(functools.partial(rs_kernel, nz, parts), out_shape=jax.Sha...]
where the time goes in v5:
time: 133 us; the launch traced here: 132 us
  Pallas kernels  67.4 us (51%)
  waiting for transfers between devices  21 us (16%)
  local copies, waits for them, and re-layouts  17.8 us (13%)
  other arithmetic  15 us (11%)
  starting transfers between devices  8.08 us (6%)
  matrix products  2.92 us (2%)
    pallas_call x1, Pallas kernels, reduce_scatter_ta(): pl.pallas_call(functools.partial(rs_kernel, nz, parts), out_shape=jax.Sha...  67.4 us
    ppermute x1, waiting for transfers between devices, exchange_halo(): below = lax.ppermute(shard[length - width:], axis, up)  18.2 us
    gather x1, local copies, waits for them, and re-layouts, shards(): partial = signal.reshape(slab_cells, rank)[brain_voxels]  12.1 us
    add x4, other arithmetic, smooth_along(): summed + kernel[shift_k] * lax.slice_in_dim(padded, shift_k, shift_k + ex...  10.9 us
    ppermute x1, starting transfers between devices, exchange_halo(): above = lax.ppermute(shard[:width], axis, down)  6.04 us
    add x1, other arithmetic, smooth_planes(): summed + kernel[shift_k] * padded[shift_k:shift_k + planes].astype(jnp.fl...  4.12 us
    slice x1, local copies, waits for them, and re-layouts, exchange_halo(): below = lax.ppermute(shard[length - width:], axis, up)  3.86 us
    dot_general x2, matrix products, project_smooth_xy(): jnp.dot(planes_bf16.reshape(-1, time_local), sketch_matrix, preferred_ele...  2.92 us
  transfers between devices with their start and end apart: 2, of which 2 were waited for; matrix products, arithmetic and copies ran while one was open for 6% of the time, Pallas kernels for 0%

profile of v5, /device:TPU:24, one launch (start us, length us, event | category | flops | bytes accessed | tf_op | source)
XLA Modules:
  0.0 132.3 jit_solution(16672696880894696297)
XLA Ops:
  0.0 0.0 copy-start
  0.0 0.0 copy-start.1
  0.0 3.9 %fusion.50 = (bf16[2,24,40,384]{3,2,1,0:T(8,128)(2,1)}, bf16[2,24,40,384]{3,2,1,0:T(8,128)(2,1)}) fusion(bf16[6,24,40,384]{3,2,1,0:T(8,128)(2,1)} %param.3), kind=kLoop, calls=%fused_computation.75 | loop fusion | bytes 5898240 | tf_op jit(solution)/shard_map/slice | solution.py:145
  3.9 0.0 copy-start.2
  3.9 2.0 %collective-permute-start = (bf16[2,24,40,384]{3,2,1,0:T(8,128)(2,1)}, bf16[2,24,40,384]{3,2,1,0:T(8,128)(2,1)S(1)}, u32[]{:S(2)}, u32[]{:S(2)}) collective-permute-start(bf16[2,24,40,384]{3,2,1,0:T(8,128)(2,1)} %get-tuple-element.5), channel_id=1, source_target_pairs={{0,32},{32,64},{64,96},{96,128},{128,160},{160,192},{192,224},{224... | collective-permute-start | bytes 4423688 | tf_op jit(solution)/shard_map/ppermute | solution.py:145
  5.9 6.0 %collective-permute-start.1 = (bf16[2,24,40,384]{3,2,1,0:T(8,128)(2,1)}, bf16[2,24,40,384]{3,2,1,0:T(8,128)(2,1)S(1)}, u32[]{:S(2)}, u32[]{:S(2)}) collective-permute-start(bf16[2,24,40,384]{3,2,1,0:T(8,128)(2,1)} %get-tuple-element.6), channel_id=1, source_target_pairs={{32,0},{64,32},{96,64},{128,96},{160,128},{192,160},{224,192},{256... | collective-permute-start | bytes 4423688 | tf_op jit(solution)/shard_map/ppermute | solution.py:146
  12.0 0.0 copy-done
  12.0 0.0 copy-done.1
  12.0 1.7 %fusion.46 = f32[6,24,40,256]{3,2,1,0:T(8,128)S(1)} fusion(bf16[6,24,40,384]{3,2,1,0:T(8,128)(2,1)S(1)} %copy-done.1, bf16[384,256]{1,0:T(8,128)(2,1)S(1)} %copy-done), kind=kOutput, calls=%fused_computation.69 | convolution fusion | flops 1132462080 | bytes 10518528 | tf_op jit(solution)/shard_map/dot_general | solution.py:152
  13.7 0.0 copy-done.2
  13.7 3.0 %fusion.4 = f32[6,24,40,256]{3,2,1,0:T(8,128)S(1)} fusion(f32[6,24,40,256]{3,2,1,0:T(8,128)S(1)} %fusion.46), kind=kLoop, calls=%fused_computation.17 | loop fusion | flops 13271040 | bytes 11796480 | tf_op jit(solution)/shard_map/add | solution.py:29
  16.7 3.6 %fusion.12 = f32[6,24,40,256]{3,2,1,0:T(8,128)S(1)} fusion(f32[6,24,40,256]{3,2,1,0:T(8,128)S(1)} %fusion.4), kind=kLoop, calls=%fused_computation.25 | loop fusion | flops 13271040 | bytes 11796480 | tf_op jit(solution)/shard_map/add | solution.py:29
  20.3 18.2 %collective-permute-done = bf16[2,24,40,384]{3,2,1,0:T(8,128)(2,1)S(1)} collective-permute-done((bf16[2,24,40,384]{3,2,1,0:T(8,128)(2,1)}, bf16[2,24,40,384]{3,2,1,0:T(8,128)(2,1)S(1)}, u32[]{:S(2)}, u32[]{:S(2)}) %collective-permute-start) | collective-permute-done | bytes 1474592 | tf_op jit(solution)/shard_map/ppermute | solution.py:145
  38.5 2.8 %collective-permute-done.1 = bf16[2,24,40,384]{3,2,1,0:T(8,128)(2,1)S(1)} collective-permute-done((bf16[2,24,40,384]{3,2,1,0:T(8,128)(2,1)}, bf16[2,24,40,384]{3,2,1,0:T(8,128)(2,1)S(1)}, u32[]{:S(2)}, u32[]{:S(2)}) %collective-permute-start.1) | collective-permute-done | bytes 1474592 | tf_op jit(solution)/shard_map/ppermute | solution.py:146
  41.3 1.2 fusion.42
  42.5 2.0 %fusion.30 = f32[4,24,40,256]{3,2,1,0:T(8,128)S(1)} fusion(f32[4,24,40,256]{3,2,1,0:T(8,128)S(1)} %fusion.42), kind=kLoop, calls=%fused_computation.53 | loop fusion | flops 8847360 | bytes 7864320 | tf_op jit(solution)/shard_map/add | solution.py:29
  44.5 2.3 %fusion.38 = f32[4,24,40,256]{3,2,1,0:T(8,128)S(1)} fusion(f32[4,24,40,256]{3,2,1,0:T(8,128)S(1)} %fusion.30), kind=kLoop, calls=%fused_computation.61 | loop fusion | flops 8847360 | bytes 7864320 | tf_op jit(solution)/shard_map/add | solution.py:29
  46.9 0.3 fusion.51
  47.1 4.1 %fusion.19 = f32[6,24,40,256]{3,2,1,0:T(8,128)} fusion(f32[6,24,40,256]{3,2,1,0:T(8,128)S(1)} %fusion.12, f32[2,24,40,256]{3,2,1,0:T(8,128)S(1)} %get-tuple-element.8, f32[2,24,40,256]{3,2,1,0:T(8,128)S(1)} %get-tuple-element.7), kind=kLoop, calls=%fused_computation.32 | loop fusion | flops 19169280 | bytes 15728640 | tf_op jit(solution)/shard_map/add | solution.py:38
  51.3 12.1 %gather_fusion = f32[3584,256]{1,0:T(8,128)} fusion(f32[5760,256]{1,0:T(8,128)} %bitcast.10, s32[4096]{0:T(1024)S(1)} %pad_clamp_fusion), kind=kCustom, calls=%fused_computation | custom fusion | bytes 7354368 | tf_op jit(solution)/shard_map/gather | solution.py:168
  63.4 67.4 %shard_map.37 = f32[112,256]{1,0:T(8,128)} custom-call(f32[32,112,256]{2,1,0:T(8,128)} %bitcast.11), custom_call_target="tpu_custom_call" | custom-call | tf_op jit(solution)/shard_map/pallas_call | solution.py:122
  130.8 1.6 %copy.6 = f32[112,256]{1,0:T(8,128)} copy(f32[112,256]{1,0:T(8,128)} %shard_map.37) | data formatting | bytes 229376
  (2 shorter events, 0.0 us)
Async XLA Ops:
  0.0 12.0 %copy-start = (bf16[384,256]{1,0:T(8,128)(2,1)S(1)}, bf16[384,256]{1,0:T(8,128)(2,1)}, u32[]{:S(2)}) copy-start(bf16[384,256]{1,0:T(8,128)(2,1)} %param.4) | copy-start | bytes 589828
  0.0 12.0 %copy-start.1 = (bf16[6,24,40,384]{3,2,1,0:T(8,128)(2,1)S(1)}, bf16[6,24,40,384]{3,2,1,0:T(8,128)(2,1)}, u32[]{:S(2)}) copy-start(bf16[6,24,40,384]{3,2,1,0:T(8,128)(2,1)} %param.3) | copy-start | bytes 13271044
  3.9 9.8 %copy-start.2 = (s32[3584]{0:T(1024)S(1)}, s32[3584]{0:T(1024)}, u32[]{:S(2)}) copy-start(s32[3584]{0:T(1024)} %param.5) | copy-start | bytes 43012
  3.9 34.6 %collective-permute-start = (bf16[2,24,40,384]{3,2,1,0:T(8,128)(2,1)}, bf16[2,24,40,384]{3,2,1,0:T(8,128)(2,1)S(1)}, u32[]{:S(2)}, u32[]{:S(2)}) collective-permute-start(bf16[2,24,40,384]{3,2,1,0:T(8,128)(2,1)} %get-tuple-element.5), channel_id=1, source_target_pairs={{0,32},{32,64},{64,96},{96,128},{128,160},{160,192},{192,224},{224... | collective-permute-start | bytes 4423688 | tf_op jit(solution)/shard_map/ppermute | solution.py:145
  5.9 35.4 %collective-permute-start.1 = (bf16[2,24,40,384]{3,2,1,0:T(8,128)(2,1)}, bf16[2,24,40,384]{3,2,1,0:T(8,128)(2,1)S(1)}, u32[]{:S(2)}, u32[]{:S(2)}) collective-permute-start(bf16[2,24,40,384]{3,2,1,0:T(8,128)(2,1)} %get-tuple-element.6), channel_id=1, source_target_pairs={{32,0},{64,32},{96,64},{128,96},{160,128},{192,160},{224,192},{256... | collective-permute-start | bytes 4423688 | tf_op jit(solution)/shard_map/ppermute | solution.py:146

commit v6 on v5

--- a/solution.py
+++ b/solution.py
@@ -138,12 +138,53 @@
     )(blocks)
 
 
-def exchange_halo(shard, axis, width):
-    peers, length = lax.axis_size(axis), shard.shape[0]
-    up = [(i, i + 1) for i in range(peers - 1)]
-    down = [(j, i) for i, j in up]
-    below = lax.ppermute(shard[length - width :], axis, up)
-    above = lax.ppermute(shard[:width], axis, down)
+Y_SIZE, X_SIZE = 4, 4
+
+
+def _coords(lin, n_ta):
+    gz, ta = divmod(lin, n_ta)
+    y, x_hi, core = gz // 4, (gz // 2) % 2, gz % 2
+    x_lo, z = divmod(ta, Z_RING)
+    return y, x_hi * 2 + x_lo, z, core
+
+
+def _lin(y, x, z, core, n_ta):
+    gz = (y * 2 + x // 2) * 2 + core
+    return gz * n_ta + (x % 2) * Z_RING + z
+
+
+def halo_routes(n_gz, n_ta):
+    onchip, first, second = [], ([], []), ([], [])
+    for lin in range(n_gz * n_ta):
+        gz = lin // n_ta
+        y, x, z, core = _coords(lin, n_ta)
+        onchip.append((lin, _lin(y, x, z, 1 - core, n_ta)))
+        dest_gz = gz + 1 if core == 1 else gz - 1
+        if not 0 <= dest_gz < n_gz:
+            continue
+        dest = dest_gz * n_ta + lin % n_ta
+        for half, step in enumerate((1, -1)):
+            relay = _lin(y, (x + step) % X_SIZE, z, core, n_ta)
+            first[half].append((lin, relay))
+            second[half].append((relay, dest))
+    return onchip, first, second
+
+
+def exchange_halo(shard, width):
+    n_gz, n_ta = lax.axis_size("gz"), lax.axis_size("ta")
+    onchip, first, second = halo_routes(n_gz, n_ta)
+    axes = ("gz", "ta")
+    core = lax.axis_index("gz") % 2
+    length, width_x = shard.shape[0], shard.shape[1]
+    top, bottom = shard[length - width :], shard[:width]
+    near = lax.ppermute(jnp.where(core == 0, top, bottom), axes, onchip)
+    far_out = jnp.where(core == 1, top, bottom)
+    cut = width_x // 2
+    halves = (far_out[:, :cut], far_out[:, cut:])
+    relayed = [lax.ppermute(h, axes, p) for h, p in zip(halves, first)]
+    far = jnp.concatenate([lax.ppermute(h, axes, p) for h, p in zip(relayed, second)], axis=1)
+    below = jnp.where(core == 0, far, near)
+    above = jnp.where(core == 0, near, far)
     return below, above
 
 
@@ -160,7 +201,7 @@
     planes, width_x, width_y, time_local = volume.shape
     slab_cells = planes * width_x * width_y
     rank = sketch_matrix.shape[1]
-    below, above = exchange_halo(volume, "gz", 2)
+    below, above = exchange_halo(volume, 2)
     local = project_smooth_xy(volume, sketch_matrix, kernel)
     halo = project_smooth_xy(jnp.concatenate([below, above]), sketch_matrix, kernel)
     padded = jnp.concatenate([halo[:2], local, halo[2:]])

time: 133 us -> 141 us (1.060)
  starting transfers between devices: 8.08 us -> 14.8 us
  local copies, waits for them, and re-layouts: 17.8 us -> 15.4 us
  other arithmetic: 15 us -> 17.3 us
  waiting for transfers between devices: 21 us -> 22.7 us
    ppermute x2 -> x5, starting transfers between devices: 8.08 us -> 14.8 us  [the longest x2 7.06 us: exchange_halo(): relayed = [lax.ppermute(h, axes, p) for h, p in zip(halves, first)]]
    slice x1, local copies, waits for them, and re-layouts: 3.86 us -> 0.15 us  [exchange_halo(): halves = (far_out[:, :cut], far_out[:, cut:])]
    select_n x0 -> x2, other arithmetic: none -> 2.52 us  [the longest x1 2.24 us: exchange_halo(): far_out = jnp.where(core == 1, top, bottom)]
    ppermute x2 -> x5, waiting for transfers between devices: 21 us -> 22.7 us  [the longest x2 15.2 us: exchange_halo(): lax.ppermute(h, axes, p)]
  transfers between devices with their start and end apart: 2 -> 5, of which waited for: 2 -> 4; matrix products, arithmetic and copies ran while one was open for 6% -> 7% of each run, Pallas kernels for 0% -> 0%
where the time goes in v6:
time: 141 us; the launch traced here: 140 us
  Pallas kernels  67 us (48%)
  waiting for transfers between devices  22.7 us (16%)
  other arithmetic  17.3 us (12%)
  local copies, waits for them, and re-layouts  15.4 us (11%)
  starting transfers between devices  14.8 us (10%)
  matrix products  2.92 us (2%)
    pallas_call x1, Pallas kernels, reduce_scatter_ta(): pl.pallas_call(functools.partial(rs_kernel, nz, parts), out_shape=jax.Sha...  67 us
    ppermute x2, waiting for transfers between devices, exchange_halo(): lax.ppermute(h, axes, p)  15.2 us
    gather x1, local copies, waits for them, and re-layouts, shards(): partial = signal.reshape(slab_cells, rank)[brain_voxels]  12.1 us
    add x4, other arithmetic, smooth_along(): summed + kernel[shift_k] * lax.slice_in_dim(padded, shift_k, shift_k + ex...  10.7 us
    ppermute x2, waiting for transfers between devices, exchange_halo(): relayed = [lax.ppermute(h, axes, p) for h, p in zip(halves, first)]  7.58 us
    ppermute x2, starting transfers between devices, exchange_halo(): relayed = [lax.ppermute(h, axes, p) for h, p in zip(halves, first)]  7.06 us
    ppermute x2, starting transfers between devices, exchange_halo(): lax.ppermute(h, axes, p)  5.81 us
    add x1, other arithmetic, smooth_planes(): summed + kernel[shift_k] * padded[shift_k:shift_k + planes].astype(jnp.fl...  4.06 us
  transfers between devices with their start and end apart: 5, of which 4 were waited for; matrix products, arithmetic and copies ran while one was open for 7% of the time, Pallas kernels for 0%

profile of v6, /device:TPU:24, one launch (start us, length us, event | category | flops | bytes accessed | tf_op | source)
XLA Modules:
  0.0 140.4 jit_solution(4787409206176940688)
XLA Ops:
  0.0 0.0 copy-start
  0.0 0.0 slice-start
  0.0 0.0 slice-start.1
  0.0 2.2 %broadcast_select_fusion = (bf16[2,24,40,384]{3,2,1,0:T(8,128)(2,1)S(1)}, bf16[2,24,40,384]{3,2,1,0:T(8,128)(2,1)S(1)}) fusion(pred[]{:T(512)S(6)} %eq.11, bf16[6,24,40,384]{3,2,1,0:T(8,128)(2,1)} %param.3, pred[]{:T(512)S(6)} %eq.10), kind=kLoop, calls=%fused_computation.69 | loop fusion | flops 1474560 | bytes 5898242 | tf_op jit(solution)/shard_map/jit(_where)/select_n | solution.py:181
  2.3 0.1 fusion.51
  2.4 3.4 %collective-permute-start = (bf16[2,12,40,384]{3,2,1,0:T(8,128)(2,1)S(1)}, bf16[2,12,40,384]{3,2,1,0:T(8,128)(2,1)}, u32[]{:S(2)}, u32[]{:S(2)}) collective-permute-start(bf16[2,12,40,384]{3,2,1,0:T(8,128)(2,1)S(1)} %get-tuple-element.12), channel_id=1, source_target_pairs={{32,48},{33,49},{34,50},{35,51},{36,52},{37,53},{38,54},{39,55},{4... | collective-permute-start | bytes 2211848 | tf_op jit(solution)/shard_map/ppermute | solution.py:184
  5.8 3.7 %collective-permute-start.2 = (bf16[2,12,40,384]{3,2,1,0:T(8,128)(2,1)S(1)}, bf16[2,12,40,384]{3,2,1,0:T(8,128)(2,1)}, u32[]{:S(2)}, u32[]{:S(2)}) collective-permute-start(bf16[2,12,40,384]{3,2,1,0:T(8,128)(2,1)S(1)} %get-tuple-element.11), channel_id=1, source_target_pairs={{32,112},{33,113},{34,114},{35,115},{36,116},{37,117},{38,118},{39... | collective-permute-start | bytes 2211848 | tf_op jit(solution)/shard_map/ppermute | solution.py:184
  9.5 0.0 copy-start.1
  9.5 1.9 %collective-permute-start.4 = (bf16[2,24,40,384]{3,2,1,0:T(8,128)(2,1)S(1)}, bf16[2,24,40,384]{3,2,1,0:T(8,128)(2,1)S(1)}, u32[]{:S(2)}, u32[]{:S(2)}) collective-permute-start(bf16[2,24,40,384]{3,2,1,0:T(8,128)(2,1)S(1)} %get-tuple-element.6), channel_id=1, source_target_pairs={{0,32},{1,33},{2,34},{3,35},{4,36},{5,37},{6,38},{7,39},{8,40},{9,... | collective-permute-start | bytes 4423688 | tf_op jit(solution)/shard_map/ppermute | solution.py:180
  11.4 0.0 copy-done
  11.4 0.0 slice-done
  11.4 0.0 slice-done.1
  11.5 1.7 %fusion.46 = f32[6,24,40,256]{3,2,1,0:T(8,128)S(1)} fusion(bf16[6,24,40,384]{3,2,1,0:T(8,128)(2,1)S(1)} %bitcast.13, bf16[384,256]{1,0:T(8,128)(2,1)S(1)} %copy-done), kind=kOutput, calls=%fused_computation.73 | convolution fusion | flops 1132462080 | bytes 10518528 | tf_op jit(solution)/shard_map/dot_general | solution.py:193
  13.2 0.0 copy-done.1
  13.2 2.8 %fusion.4 = f32[6,24,40,256]{3,2,1,0:T(8,128)S(1)} fusion(f32[6,24,40,256]{3,2,1,0:T(8,128)S(1)} %fusion.46), kind=kLoop, calls=%fused_computation.17 | loop fusion | flops 13271040 | bytes 11796480 | tf_op jit(solution)/shard_map/add | solution.py:29
  16.0 5.5 %collective-permute-done = bf16[2,12,40,384]{3,2,1,0:T(8,128)(2,1)} collective-permute-done((bf16[2,12,40,384]{3,2,1,0:T(8,128)(2,1)S(1)}, bf16[2,12,40,384]{3,2,1,0:T(8,128)(2,1)}, u32[]{:S(2)}, u32[]{:S(2)}) %collective-permute-start) | collective-permute-done | bytes 737312 | tf_op jit(solution)/shard_map/ppermute | solution.py:184
  21.5 3.1 %collective-permute-start.1 = (bf16[2,12,40,384]{3,2,1,0:T(8,128)(2,1)}, bf16[2,12,40,384]{3,2,1,0:T(8,128)(2,1)S(1)}, u32[]{:S(2)}, u32[]{:S(2)}) collective-permute-start(bf16[2,12,40,384]{3,2,1,0:T(8,128)(2,1)} %collective-permute-done), channel_id=1, source_target_pairs={{48,64},{49,65},{50,66},{51,67},{52,68},{53,69},{54,70},{55,71},{5... | collective-permute-start | bytes 2211848 | tf_op jit(solution)/shard_map/ppermute | solution.py:185
  24.6 2.0 %collective-permute-done.2 = bf16[2,12,40,384]{3,2,1,0:T(8,128)(2,1)} collective-permute-done((bf16[2,12,40,384]{3,2,1,0:T(8,128)(2,1)S(1)}, bf16[2,12,40,384]{3,2,1,0:T(8,128)(2,1)}, u32[]{:S(2)}, u32[]{:S(2)}) %collective-permute-start.2) | collective-permute-done | bytes 737312 | tf_op jit(solution)/shard_map/ppermute | solution.py:184
  26.6 2.8 %collective-permute-start.3 = (bf16[2,12,40,384]{3,2,1,0:T(8,128)(2,1)}, bf16[2,12,40,384]{3,2,1,0:T(8,128)(2,1)}, u32[]{:S(2)}, u32[]{:S(2)}) collective-permute-start(bf16[2,12,40,384]{3,2,1,0:T(8,128)(2,1)} %collective-permute-done.2), channel_id=1, source_target_pairs={{112,64},{113,65},{114,66},{115,67},{116,68},{117,69},{118,70},{11... | collective-permute-start | bytes 2211848 | tf_op jit(solution)/shard_map/ppermute | solution.py:185
  29.4 3.6 %fusion.12 = f32[6,24,40,256]{3,2,1,0:T(8,128)S(1)} fusion(f32[6,24,40,256]{3,2,1,0:T(8,128)S(1)} %fusion.4), kind=kLoop, calls=%fused_computation.25 | loop fusion | flops 13271040 | bytes 11796480 | tf_op jit(solution)/shard_map/add | solution.py:29
  33.0 10.8 %collective-permute-done.1 = bf16[2,12,40,384]{3,2,1,0:T(8,128)(2,1)S(1)} collective-permute-done((bf16[2,12,40,384]{3,2,1,0:T(8,128)(2,1)}, bf16[2,12,40,384]{3,2,1,0:T(8,128)(2,1)S(1)}, u32[]{:S(2)}, u32[]{:S(2)}) %collective-permute-start.1) | collective-permute-done | bytes 737312 | tf_op jit(solution)/shard_map/ppermute | solution.py:185
  43.8 0.1 constant_dynamic-update-slice_fusion.1
  43.9 4.3 %collective-permute-done.3 = bf16[2,12,40,384]{3,2,1,0:T(8,128)(2,1)} collective-permute-done((bf16[2,12,40,384]{3,2,1,0:T(8,128)(2,1)}, bf16[2,12,40,384]{3,2,1,0:T(8,128)(2,1)}, u32[]{:S(2)}, u32[]{:S(2)}) %collective-permute-start.3) | collective-permute-done | bytes 737312 | tf_op jit(solution)/shard_map/ppermute | solution.py:185
  48.2 1.3 constant_dynamic-update-slice_fusion
  49.5 0.0 collective-permute-done.4
  49.5 0.3 broadcast_select_fusion.2
  49.8 1.2 fusion.42
  51.0 2.0 %fusion.30 = f32[4,24,40,256]{3,2,1,0:T(8,128)S(1)} fusion(f32[4,24,40,256]{3,2,1,0:T(8,128)S(1)} %fusion.42), kind=kLoop, calls=%fused_computation.53 | loop fusion | flops 8847360 | bytes 7864320 | tf_op jit(solution)/shard_map/add | solution.py:29
  53.0 2.3 %fusion.38 = f32[4,24,40,256]{3,2,1,0:T(8,128)S(1)} fusion(f32[4,24,40,256]{3,2,1,0:T(8,128)S(1)} %fusion.30), kind=kLoop, calls=%fused_computation.61 | loop fusion | flops 8847360 | bytes 7864320 | tf_op jit(solution)/shard_map/add | solution.py:29
  55.4 0.3 fusion.50
  55.6 4.1 %fusion.19 = f32[6,24,40,256]{3,2,1,0:T(8,128)} fusion(f32[6,24,40,256]{3,2,1,0:T(8,128)S(1)} %fusion.12, f32[2,24,40,256]{3,2,1,0:T(8,128)S(1)} %get-tuple-element.8, f32[2,24,40,256]{3,2,1,0:T(8,128)S(1)} %get-tuple-element.7), kind=kLoop, calls=%fused_computation.32 | loop fusion | flops 19169280 | bytes 15728640 | tf_op jit(solution)/shard_map/add | solution.py:38
  59.7 12.1 %gather_fusion = f32[3584,256]{1,0:T(8,128)} fusion(f32[5760,256]{1,0:T(8,128)} %bitcast.10, s32[4096]{0:T(1024)S(1)} %pad_clamp_fusion), kind=kCustom, calls=%fused_computation | custom fusion | bytes 7354368 | tf_op jit(solution)/shard_map/gather | solution.py:209
  71.8 67.0 %shard_map.37 = f32[112,256]{1,0:T(8,128)} custom-call(f32[32,112,256]{2,1,0:T(8,128)} %bitcast.11), custom_call_target="tpu_custom_call" | custom-call | tf_op jit(solution)/shard_map/pallas_call | solution.py:122
  138.8 1.6 %copy.7 = f32[112,256]{1,0:T(8,128)} copy(f32[112,256]{1,0:T(8,128)} %shard_map.37) | data formatting | bytes 229376
  (3 shorter events, 0.0 us)
Async XLA Ops:
  0.0 11.4 %copy-start = (bf16[384,256]{1,0:T(8,128)(2,1)S(1)}, bf16[384,256]{1,0:T(8,128)(2,1)}, u32[]{:S(2)}) copy-start(bf16[384,256]{1,0:T(8,128)(2,1)} %param.4) | copy-start | bytes 589828
  0.0 11.4 %slice-start = ((s8[4423680]{0:T(1024)(128)(4,1)}), s8[229376]{0:T(1024)(128)(4,1)S(1)}, s32[]{:S(2)}) async-start(s8[4423680]{0:T(1024)(128)(4,1)} %bitcast.12), calls=%async_computation | async-start | bytes 458752
  0.0 11.4 %slice-start.1 = ((s8[4423680]{0:T(1024)(128)(4,1)}), s8[4194304]{0:T(1024)(128)(4,1)S(1)}, s32[]{:S(2)}) async-start(s8[4423680]{0:T(1024)(128)(4,1)} %bitcast.12), calls=%async_computation.1 | async-start | bytes 8388608
  2.4 19.1 %collective-permute-start = (bf16[2,12,40,384]{3,2,1,0:T(8,128)(2,1)S(1)}, bf16[2,12,40,384]{3,2,1,0:T(8,128)(2,1)}, u32[]{:S(2)}, u32[]{:S(2)}) collective-permute-start(bf16[2,12,40,384]{3,2,1,0:T(8,128)(2,1)S(1)} %get-tuple-element.12), channel_id=1, source_target_pairs={{32,48},{33,49},{34,50},{35,51},{36,52},{37,53},{38,54},{39,55},{4... | collective-permute-start | bytes 2211848 | tf_op jit(solution)/shard_map/ppermute | solution.py:184
  5.8 20.8 %collective-permute-start.2 = (bf16[2,12,40,384]{3,2,1,0:T(8,128)(2,1)S(1)}, bf16[2,12,40,384]{3,2,1,0:T(8,128)(2,1)}, u32[]{:S(2)}, u32[]{:S(2)}) collective-permute-start(bf16[2,12,40,384]{3,2,1,0:T(8,128)(2,1)S(1)} %get-tuple-element.11), channel_id=1, source_target_pairs={{32,112},{33,113},{34,114},{35,115},{36,116},{37,117},{38,118},{39... | collective-permute-start | bytes 2211848 | tf_op jit(solution)/shard_map/ppermute | solution.py:184
  9.5 3.7 %copy-start.1 = (s32[3584]{0:T(1024)S(1)}, s32[3584]{0:T(1024)}, u32[]{:S(2)}) copy-start(s32[3584]{0:T(1024)} %param.5) | copy-start | bytes 43012
  9.5 40.0 %collective-permute-start.4 = (bf16[2,24,40,384]{3,2,1,0:T(8,128)(2,1)S(1)}, bf16[2,24,40,384]{3,2,1,0:T(8,128)(2,1)S(1)}, u32[]{:S(2)}, u32[]{:S(2)}) collective-permute-start(bf16[2,24,40,384]{3,2,1,0:T(8,128)(2,1)S(1)} %get-tuple-element.6), channel_id=1, source_target_pairs={{0,32},{1,33},{2,34},{3,35},{4,36},{5,37},{6,38},{7,39},{8,40},{9,... | collective-permute-start | bytes 4423688 | tf_op jit(solution)/shard_map/ppermute | solution.py:180
  21.5 22.3 %collective-permute-start.1 = (bf16[2,12,40,384]{3,2,1,0:T(8,128)(2,1)}, bf16[2,12,40,384]{3,2,1,0:T(8,128)(2,1)S(1)}, u32[]{:S(2)}, u32[]{:S(2)}) collective-permute-start(bf16[2,12,40,384]{3,2,1,0:T(8,128)(2,1)} %collective-permute-done), channel_id=1, source_target_pairs={{48,64},{49,65},{50,66},{51,67},{52,68},{53,69},{54,70},{55,71},{5... | collective-permute-start | bytes 2211848 | tf_op jit(solution)/shard_map/ppermute | solution.py:185
  26.6 21.6 %collective-permute-start.3 = (bf16[2,12,40,384]{3,2,1,0:T(8,128)(2,1)}, bf16[2,12,40,384]{3,2,1,0:T(8,128)(2,1)}, u32[]{:S(2)}, u32[]{:S(2)}) collective-permute-start(bf16[2,12,40,384]{3,2,1,0:T(8,128)(2,1)} %collective-permute-done.2), channel_id=1, source_target_pairs={{112,64},{113,65},{114,66},{115,67},{116,68},{117,69},{118,70},{11... | collective-permute-start | bytes 2211848 | tf_op jit(solution)/shard_map/ppermute | solution.py:185

commit v7 on v5

--- a/solution.py
+++ b/solution.py
@@ -93,26 +93,30 @@
                     )
                     cp.start()
                     copies[(d, k, s)] = cp
+            if s == nz - 1:
+                xcp = pltpu.make_async_remote_copy(
+                    src_ref=fin.at[1 - xl, pl.ds(k * rk, rk)],
+                    dst_ref=xrecv.at[pl.ds(k * rk, rk)],
+                    send_sem=xsem.at[0, k],
+                    recv_sem=xsem.at[1, k],
+                    device_id=(gz, partner),
+                    device_id_type=MESH,
+                )
+                xcp.start()
+                copies[("x", k)] = xcp
 
-    xcp = pltpu.make_async_remote_copy(
-        src_ref=fin.at[1 - xl],
-        dst_ref=xrecv,
-        send_sem=xsem.at[0],
-        recv_sem=xsem.at[1],
-        device_id=(gz, partner),
-        device_id_type=MESH,
-    )
-    xcp.start()
     for d in range(2):
         for k in range(parts):
             for s in (nz - 3, nz - 2):
                 copies[(d, k, s)].wait_send()
-    xcp.wait_recv()
+    for k in range(parts):
+        copies[("x", k)].wait_recv()
     o_ref[...] = fin[xl] + xrecv[...]
-    xcp.wait_send()
+    for k in range(parts):
+        copies[("x", k)].wait_send()
 
 
-def reduce_scatter_ta(partial, n_ta, parts=7):
+def reduce_scatter_ta(partial, n_ta, parts=14):
     rows_all, cols = partial.shape
     nz = Z_RING
     assert n_ta == 2 * nz
@@ -132,7 +136,7 @@
             pltpu.SemaphoreType.DMA((2, parts, 2)),
             pltpu.SemaphoreType.DMA((2, parts, 2)),
             pltpu.SemaphoreType.REGULAR((2, parts)),
-            pltpu.SemaphoreType.DMA((2,)),
+            pltpu.SemaphoreType.DMA((2, parts)),
         ],
         compiler_params=pltpu.CompilerParams(collective_id=0, has_side_effects=True),
     )(blocks)

time: 133 us -> 132 us (level)
  no operation moved by 1% of the time
where the time goes in v7:
time: 132 us
  Pallas kernels  66.8 us (51%)
  waiting for transfers between devices  21.2 us (16%)
  local copies, waits for them, and re-layouts  17.8 us (13%)
  other arithmetic  14.8 us (11%)
  starting transfers between devices  8.08 us (6%)
  matrix products  2.92 us (2%)
    pallas_call x1, Pallas kernels, reduce_scatter_ta(): pl.pallas_call(functools.partial(rs_kernel, nz, parts), out_shape=jax.Sha...  66.8 us
    ppermute x1, waiting for transfers between devices, exchange_halo(): below = lax.ppermute(shard[length - width:], axis, up)  18.4 us
    gather x1, local copies, waits for them, and re-layouts, shards(): partial = signal.reshape(slab_cells, rank)[brain_voxels]  12.1 us
    add x4, other arithmetic, smooth_along(): summed + kernel[shift_k] * lax.slice_in_dim(padded, shift_k, shift_k + ex...  10.7 us
    ppermute x1, starting transfers between devices, exchange_halo(): above = lax.ppermute(shard[:width], axis, down)  6.04 us
    add x1, other arithmetic, smooth_planes(): summed + kernel[shift_k] * padded[shift_k:shift_k + planes].astype(jnp.fl...  4.12 us
    slice x1, local copies, waits for them, and re-layouts, exchange_halo(): below = lax.ppermute(shard[length - width:], axis, up)  3.86 us
    dot_general x2, matrix products, project_smooth_xy(): jnp.dot(planes_bf16.reshape(-1, time_local), sketch_matrix, preferred_ele...  2.92 us
  transfers between devices with their start and end apart: 2, of which 2 were waited for; matrix products, arithmetic and copies ran while one was open for 6% of the time, Pallas kernels for 0%

profile of v7, /device:TPU:24, one launch (start us, length us, event | category | flops | bytes accessed | tf_op | source)
XLA Modules:
  0.0 131.8 jit_solution(3165220426530637414)
XLA Ops:
  0.0 0.0 copy-start
  0.0 0.0 copy-start.1
  0.0 3.9 %fusion.50 = (bf16[2,24,40,384]{3,2,1,0:T(8,128)(2,1)}, bf16[2,24,40,384]{3,2,1,0:T(8,128)(2,1)}) fusion(bf16[6,24,40,384]{3,2,1,0:T(8,128)(2,1)} %param.3), kind=kLoop, calls=%fused_computation.75 | loop fusion | bytes 5898240 | tf_op jit(solution)/shard_map/slice | solution.py:149
  3.9 0.0 copy-start.2
  3.9 2.0 %collective-permute-start = (bf16[2,24,40,384]{3,2,1,0:T(8,128)(2,1)}, bf16[2,24,40,384]{3,2,1,0:T(8,128)(2,1)S(1)}, u32[]{:S(2)}, u32[]{:S(2)}) collective-permute-start(bf16[2,24,40,384]{3,2,1,0:T(8,128)(2,1)} %get-tuple-element.5), channel_id=1, source_target_pairs={{0,32},{32,64},{64,96},{96,128},{128,160},{160,192},{192,224},{224... | collective-permute-start | bytes 4423688 | tf_op jit(solution)/shard_map/ppermute | solution.py:149
  5.9 6.0 %collective-permute-start.1 = (bf16[2,24,40,384]{3,2,1,0:T(8,128)(2,1)}, bf16[2,24,40,384]{3,2,1,0:T(8,128)(2,1)S(1)}, u32[]{:S(2)}, u32[]{:S(2)}) collective-permute-start(bf16[2,24,40,384]{3,2,1,0:T(8,128)(2,1)} %get-tuple-element.6), channel_id=1, source_target_pairs={{32,0},{64,32},{96,64},{128,96},{160,128},{192,160},{224,192},{256... | collective-permute-start | bytes 4423688 | tf_op jit(solution)/shard_map/ppermute | solution.py:150
  12.0 0.0 copy-done
  12.0 0.0 copy-done.1
  12.0 1.7 %fusion.46 = f32[6,24,40,256]{3,2,1,0:T(8,128)S(1)} fusion(bf16[6,24,40,384]{3,2,1,0:T(8,128)(2,1)S(1)} %copy-done.1, bf16[384,256]{1,0:T(8,128)(2,1)S(1)} %copy-done), kind=kOutput, calls=%fused_computation.69 | convolution fusion | flops 1132462080 | bytes 10518528 | tf_op jit(solution)/shard_map/dot_general | solution.py:156
  13.7 0.0 copy-done.2
  13.7 2.8 %fusion.4 = f32[6,24,40,256]{3,2,1,0:T(8,128)S(1)} fusion(f32[6,24,40,256]{3,2,1,0:T(8,128)S(1)} %fusion.46), kind=kLoop, calls=%fused_computation.17 | loop fusion | flops 13271040 | bytes 11796480 | tf_op jit(solution)/shard_map/add | solution.py:29
  16.5 3.6 %fusion.12 = f32[6,24,40,256]{3,2,1,0:T(8,128)S(1)} fusion(f32[6,24,40,256]{3,2,1,0:T(8,128)S(1)} %fusion.4), kind=kLoop, calls=%fused_computation.25 | loop fusion | flops 13271040 | bytes 11796480 | tf_op jit(solution)/shard_map/add | solution.py:29
  20.1 18.4 %collective-permute-done = bf16[2,24,40,384]{3,2,1,0:T(8,128)(2,1)S(1)} collective-permute-done((bf16[2,24,40,384]{3,2,1,0:T(8,128)(2,1)}, bf16[2,24,40,384]{3,2,1,0:T(8,128)(2,1)S(1)}, u32[]{:S(2)}, u32[]{:S(2)}) %collective-permute-start) | collective-permute-done | bytes 1474592 | tf_op jit(solution)/shard_map/ppermute | solution.py:149
  38.5 2.8 %collective-permute-done.1 = bf16[2,24,40,384]{3,2,1,0:T(8,128)(2,1)S(1)} collective-permute-done((bf16[2,24,40,384]{3,2,1,0:T(8,128)(2,1)}, bf16[2,24,40,384]{3,2,1,0:T(8,128)(2,1)S(1)}, u32[]{:S(2)}, u32[]{:S(2)}) %collective-permute-start.1) | collective-permute-done | bytes 1474592 | tf_op jit(solution)/shard_map/ppermute | solution.py:150
  41.3 1.2 fusion.42
  42.5 2.0 %fusion.30 = f32[4,24,40,256]{3,2,1,0:T(8,128)S(1)} fusion(f32[4,24,40,256]{3,2,1,0:T(8,128)S(1)} %fusion.42), kind=kLoop, calls=%fused_computation.53 | loop fusion | flops 8847360 | bytes 7864320 | tf_op jit(solution)/shard_map/add | solution.py:29
  44.5 2.3 %fusion.38 = f32[4,24,40,256]{3,2,1,0:T(8,128)S(1)} fusion(f32[4,24,40,256]{3,2,1,0:T(8,128)S(1)} %fusion.30), kind=kLoop, calls=%fused_computation.61 | loop fusion | flops 8847360 | bytes 7864320 | tf_op jit(solution)/shard_map/add | solution.py:29
  46.9 0.3 fusion.51
  47.1 4.1 %fusion.19 = f32[6,24,40,256]{3,2,1,0:T(8,128)} fusion(f32[6,24,40,256]{3,2,1,0:T(8,128)S(1)} %fusion.12, f32[2,24,40,256]{3,2,1,0:T(8,128)S(1)} %get-tuple-element.8, f32[2,24,40,256]{3,2,1,0:T(8,128)S(1)} %get-tuple-element.7), kind=kLoop, calls=%fused_computation.32 | loop fusion | flops 19169280 | bytes 15728640 | tf_op jit(solution)/shard_map/add | solution.py:38
  51.3 12.1 %gather_fusion = f32[3584,256]{1,0:T(8,128)} fusion(f32[5760,256]{1,0:T(8,128)} %bitcast.10, s32[4096]{0:T(1024)S(1)} %pad_clamp_fusion), kind=kCustom, calls=%fused_computation | custom fusion | bytes 7354368 | tf_op jit(solution)/shard_map/gather | solution.py:172
  63.4 66.8 %shard_map.37 = f32[112,256]{1,0:T(8,128)} custom-call(f32[32,112,256]{2,1,0:T(8,128)} %bitcast.11), custom_call_target="tpu_custom_call" | custom-call | tf_op jit(solution)/shard_map/pallas_call | solution.py:126
  130.2 1.6 %copy.6 = f32[112,256]{1,0:T(8,128)} copy(f32[112,256]{1,0:T(8,128)} %shard_map.37) | data formatting | bytes 229376
  (2 shorter events, 0.0 us)
Async XLA Ops:
  0.0 12.0 %copy-start = (bf16[384,256]{1,0:T(8,128)(2,1)S(1)}, bf16[384,256]{1,0:T(8,128)(2,1)}, u32[]{:S(2)}) copy-start(bf16[384,256]{1,0:T(8,128)(2,1)} %param.4) | copy-start | bytes 589828
  0.0 12.0 %copy-start.1 = (bf16[6,24,40,384]{3,2,1,0:T(8,128)(2,1)S(1)}, bf16[6,24,40,384]{3,2,1,0:T(8,128)(2,1)}, u32[]{:S(2)}) copy-start(bf16[6,24,40,384]{3,2,1,0:T(8,128)(2,1)} %param.3) | copy-start | bytes 13271044
  3.9 9.8 %copy-start.2 = (s32[3584]{0:T(1024)S(1)}, s32[3584]{0:T(1024)}, u32[]{:S(2)}) copy-start(s32[3584]{0:T(1024)} %param.5) | copy-start | bytes 43012
  3.9 34.6 %collective-permute-start = (bf16[2,24,40,384]{3,2,1,0:T(8,128)(2,1)}, bf16[2,24,40,384]{3,2,1,0:T(8,128)(2,1)S(1)}, u32[]{:S(2)}, u32[]{:S(2)}) collective-permute-start(bf16[2,24,40,384]{3,2,1,0:T(8,128)(2,1)} %get-tuple-element.5), channel_id=1, source_target_pairs={{0,32},{32,64},{64,96},{96,128},{128,160},{160,192},{192,224},{224... | collective-permute-start | bytes 4423688 | tf_op jit(solution)/shard_map/ppermute | solution.py:149
  5.9 35.4 %collective-permute-start.1 = (bf16[2,24,40,384]{3,2,1,0:T(8,128)(2,1)}, bf16[2,24,40,384]{3,2,1,0:T(8,128)(2,1)S(1)}, u32[]{:S(2)}, u32[]{:S(2)}) collective-permute-start(bf16[2,24,40,384]{3,2,1,0:T(8,128)(2,1)} %get-tuple-element.6), channel_id=1, source_target_pairs={{32,0},{64,32},{96,64},{128,96},{160,128},{192,160},{224,192},{256... | collective-permute-start | bytes 4423688 | tf_op jit(solution)/shard_map/ppermute | solution.py:150

commit v8 on v7

--- a/solution.py
+++ b/solution.py
@@ -142,13 +142,127 @@
     )(blocks)
 
 
-def exchange_halo(shard, axis, width):
-    peers, length = lax.axis_size(axis), shard.shape[0]
-    up = [(i, i + 1) for i in range(peers - 1)]
-    down = [(j, i) for i, j in up]
-    below = lax.ppermute(shard[length - width :], axis, up)
-    above = lax.ppermute(shard[:width], axis, down)
-    return below, above
+def halo_kernel(nz, n_gz, vol_ref, o_ref, relay, halo, sems):
+    gz = lax.axis_index("gz")
+    ta = lax.axis_index("ta")
+    length, width_x = vol_ref.shape[0], vol_ref.shape[1]
+    width = halo.shape[1]
+    cut = width_x // 2
+    y, core = gz // 4, gz % 2
+    x = ((gz // 2) % 2) * 2 + ta // nz
+    zi = ta % nz
+
+    def dev(yy, xx):
+        return ((yy * 2 + xx // 2) * 2 + core, (xx % 2) * nz + zi)
+
+    def flows(g):
+        return jnp.logical_or(
+            jnp.logical_and(core == 1, g < n_gz - 1), jnp.logical_and(core == 0, g > 0)
+        )
+
+    step = 2 * core - 1
+    partner = (gz - step, ta)
+    near = ((y, (x + 1) % 4), (y, (x + 3) % 4))
+    sources = (dev(*near[1]), dev(*near[0]))
+    src_gz = gz + step
+    has_src = jnp.logical_and(src_gz >= 0, src_gz < n_gz)
+    src_y, src_x = src_gz // 4, ((src_gz // 2) % 2) * 2 + ta // nz
+    src_relays = (
+        (src_y, (src_x + 1) % 4),
+        (src_y, (src_x + 3) % 4),
+    )
+
+    barrier = pltpu.get_barrier_semaphore()
+
+    def signal(target):
+        pl.semaphore_signal(barrier, 1, device_id=target, device_id_type=MESH)
+
+    signal(partner)
+    for rel in near:
+        signal(dev(*rel))
+    relays_for = []
+    for h in range(2):
+        s_gz, s_ta = sources[h]
+        live = flows(s_gz)
+        relays_for.append(live)
+        pl.when(live)(functools.partial(signal, (s_gz + step, s_ta)))
+    for h in range(2):
+        ry, rx = src_relays[h]
+        pl.when(has_src)(functools.partial(signal, ((ry * 2 + rx // 2) * 2 + (1 - core), (rx % 2) * nz + zi)))
+    count = 3 + relays_for[0].astype(jnp.int32) + relays_for[1].astype(jnp.int32) + 2 * has_src.astype(jnp.int32)
+    pl.semaphore_wait(barrier, count)
+
+    def copy(src, dst, i, target):
+        return pltpu.make_async_remote_copy(
+            src_ref=src, dst_ref=dst, send_sem=sems.at[0, i], recv_sem=sems.at[1, i],
+            device_id=target, device_id_type=MESH,
+        )
+
+    near_copy = copy(vol_ref.at[pl.ds((1 - core) * (length - width), width)], halo.at[core], 0, partner)
+    near_copy.start()
+    mine = flows(gz)
+    first = [
+        copy(vol_ref.at[pl.ds(core * (length - width), width), pl.ds(h * cut, cut)], relay.at[h], 1 + h,
+             dev(*near[h]))
+        for h in range(2)
+    ]
+    second = [
+        copy(relay.at[h], halo.at[1 - core, :, pl.ds(h * cut, cut)], 3 + h,
+             (sources[h][0] + step, sources[h][1]))
+        for h in range(2)
+    ]
+
+    @pl.when(mine)
+    def _():
+        for h in range(2):
+            first[h].start()
+
+    for h in range(2):
+        @pl.when(relays_for[h])
+        def _():
+            first[h].wait_recv()
+            second[h].start()
+
+    @pl.when(jnp.logical_not(has_src))
+    def _():
+        halo[core] = jnp.zeros(halo.shape[1:], halo.dtype)
+
+    near_copy.wait_recv()
+    near_copy.wait_send()
+
+    @pl.when(has_src)
+    def _():
+        for h in range(2):
+            second[h].wait_recv()
+
+    @pl.when(mine)
+    def _():
+        for h in range(2):
+            first[h].wait_send()
+
+    for h in range(2):
+        @pl.when(relays_for[h])
+        def _():
+            second[h].wait_send()
+
+    o_ref[...] = halo[...]
+
+
+def exchange_halo(shard, width, nz=Z_RING):
+    length, width_x, width_y, time_local = shard.shape
+    halo = pl.pallas_call(
+        functools.partial(halo_kernel, nz, lax.axis_size("gz")),
+        out_shape=jax.ShapeDtypeStruct((2, width, width_x, width_y, time_local), shard.dtype),
+        in_specs=[pl.BlockSpec(memory_space=pltpu.VMEM)],
+        out_specs=pl.BlockSpec(memory_space=pltpu.VMEM),
+        scratch_shapes=[
+            pltpu.VMEM((2, width, width_x // 2, width_y, time_local), shard.dtype),
+            pltpu.VMEM((2, width, width_x, width_y, time_local), shard.dtype),
+            pltpu.SemaphoreType.DMA((2, 5)),
+        ],
+        compiler_params=pltpu.CompilerParams(collective_id=1, has_side_effects=True),
+    )(shard)
+    return halo[0], halo[1]
 
 
 def project_smooth_xy(planes_bf16, sketch_matrix, kernel):
@@ -164,7 +278,7 @@
     planes, width_x, width_y, time_local = volume.shape
     slab_cells = planes * width_x * width_y
     rank = sketch_matrix.shape[1]
-    below, above = exchange_halo(volume, "gz", 2)
+    below, above = exchange_halo(volume, 2)
     local = project_smooth_xy(volume, sketch_matrix, kernel)
     halo = project_smooth_xy(jnp.concatenate([below, above]), sketch_matrix, kernel)
     padded = jnp.concatenate([halo[:2], local, halo[2:]])

time: 132 us -> 147 us (1.11)
  Pallas kernels: 66.8 us -> 111 us
  waiting for transfers between devices: 21.2 us -> 0 us
  starting transfers between devices: 8.08 us -> 0 us
    pallas_call x0 -> x1, Pallas kernels: none -> 43.7 us  [exchange_halo(): pl.pallas_call(functools.partial(halo_kernel, nz, lax.axis_size('gz')), o...]
    ppermute x2 -> x0, waiting for transfers between devices: 21.2 us -> none  [the longest x1 18.4 us: exchange_halo(): below = lax.ppermute(shard[length - width:], axis, up)]
    ppermute x2 -> x0, starting transfers between devices: 8.08 us -> none  [the longest x1 6.04 us: exchange_halo(): above = lax.ppermute(shard[:width], axis, down)]
    slice x1 -> x0, local copies, waits for them, and re-layouts: 3.86 us -> none  [exchange_halo(): below = lax.ppermute(shard[length - width:], axis, up)]
    squeeze x0 -> x1, local copies, waits for them, and re-layouts: none -> 2.11 us  [exchange_halo(): return (halo[0], halo[1])]
    unnamed x7 -> x9, local copies, waits for them, and re-layouts: 1.56 us -> 3.44 us
  transfers between devices with their start and end apart: 2 -> 0, of which waited for: 2 -> 0; matrix products, arithmetic and copies ran while one was open for 6% -> 0% of each run, Pallas kernels for 0% -> 0%
where the time goes in v8:
time: 147 us; the launch traced here: 146 us
  Pallas kernels  111 us (76%)
  local copies, waits for them, and re-layouts  17.9 us (12%)
  other arithmetic  14.8 us (10%)
  matrix products  2.92 us (2%)
    pallas_call x1, Pallas kernels, reduce_scatter_ta(): pl.pallas_call(functools.partial(rs_kernel, nz, parts), out_shape=jax.Sha...  66.9 us
    pallas_call x1, Pallas kernels, exchange_halo(): pl.pallas_call(functools.partial(halo_kernel, nz, lax.axis_size('gz')), o...  43.7 us
    gather x1, local copies, waits for them, and re-layouts, shards(): partial = signal.reshape(slab_cells, rank)[brain_voxels]  12.1 us
    add x4, other arithmetic, smooth_along(): summed + kernel[shift_k] * lax.slice_in_dim(padded, shift_k, shift_k + ex...  10.7 us
    add x1, other arithmetic, smooth_planes(): summed + kernel[shift_k] * padded[shift_k:shift_k + planes].astype(jnp.fl...  4.13 us
    unnamed x9, local copies, waits for them, and re-layouts  3.44 us

profile of v8, /device:TPU:24, one launch (start us, length us, event | category | flops | bytes accessed | tf_op | source)
XLA Modules:
  0.0 146.5 jit_solution(11132930063162246822)
XLA Ops:
  0.0 0.0 copy-start
  0.0 43.7 %shard_map.37 = bf16[2,2,24,40,384]{4,3,2,1,0:T(8,128)(2,1)} custom-call(bf16[6,24,40,384]{3,2,1,0:T(8,128)(2,1)} %vol_ref.1), custom_call_target="tpu_custom_call" | custom-call | tf_op jit(solution)/shard_map/pallas_call | solution.py:253
  43.8 2.1 %slice_bitcast_fusion.1 = (bf16[2,24,40,384]{3,2,1,0:T(8,128)(2,1)S(1)}, bf16[2,24,40,384]{3,2,1,0:T(8,128)(2,1)S(1)}) fusion(bf16[2,2,24,40,384]{4,3,2,1,0:T(8,128)(2,1)} %shard_map.37), kind=kLoop, calls=%fused_computation.70 | loop fusion | bytes 5898240 | tf_op jit(solution)/shard_map/squeeze | solution.py:265
  45.9 0.0 copy-done
  45.9 1.2 fusion.42
  47.1 2.0 %fusion.30 = f32[4,24,40,256]{3,2,1,0:T(8,128)S(1)} fusion(f32[4,24,40,256]{3,2,1,0:T(8,128)S(1)} %fusion.42), kind=kLoop, calls=%fused_computation.53 | loop fusion | flops 8847360 | bytes 7864320 | tf_op jit(solution)/shard_map/add | solution.py:29
  49.1 0.0 slice-start
  49.1 2.3 %fusion.38 = f32[4,24,40,256]{3,2,1,0:T(8,128)S(1)} fusion(f32[4,24,40,256]{3,2,1,0:T(8,128)S(1)} %fusion.30), kind=kLoop, calls=%fused_computation.61 | loop fusion | flops 8847360 | bytes 7864320 | tf_op jit(solution)/shard_map/add | solution.py:29
  51.5 0.0 slice-start.1
  51.5 0.3 fusion.50
  51.8 0.0 slice-done
  51.8 1.9 %slice-done.1 = s8[4194304]{0:T(1024)(128)(4,1)S(1)} async-done(((s8[4423680]{0:T(1024)(128)(4,1)}), s8[4194304]{0:T(1024)(128)(4,1)S(1)}, s32[]{:S(2)}) %slice-start.1) | async-done | bytes 4194328
  53.7 1.7 %fusion.46 = f32[6,24,40,256]{3,2,1,0:T(8,128)S(1)} fusion(bf16[6,24,40,384]{3,2,1,0:T(8,128)(2,1)S(1)} %bitcast.16, bf16[384,256]{1,0:T(8,128)(2,1)S(1)} %copy-done), kind=kOutput, calls=%fused_computation.71 | convolution fusion | flops 1132462080 | bytes 10518528 | tf_op jit(solution)/shard_map/dot_general | solution.py:270
  55.4 2.8 %fusion.4 = f32[6,24,40,256]{3,2,1,0:T(8,128)S(1)} fusion(f32[6,24,40,256]{3,2,1,0:T(8,128)S(1)} %fusion.46), kind=kLoop, calls=%fused_computation.17 | loop fusion | flops 13271040 | bytes 11796480 | tf_op jit(solution)/shard_map/add | solution.py:29
  58.2 3.6 %fusion.12 = f32[6,24,40,256]{3,2,1,0:T(8,128)S(1)} fusion(f32[6,24,40,256]{3,2,1,0:T(8,128)S(1)} %fusion.4), kind=kLoop, calls=%fused_computation.25 | loop fusion | flops 13271040 | bytes 11796480 | tf_op jit(solution)/shard_map/add | solution.py:29
  61.7 0.0 copy-start.1
  61.8 4.1 %fusion.19 = f32[6,24,40,256]{3,2,1,0:T(8,128)} fusion(f32[6,24,40,256]{3,2,1,0:T(8,128)S(1)} %fusion.12, f32[2,24,40,256]{3,2,1,0:T(8,128)S(1)} %get-tuple-element.6, f32[2,24,40,256]{3,2,1,0:T(8,128)S(1)} %get-tuple-element.5), kind=kLoop, calls=%fused_computation.32 | loop fusion | flops 19169280 | bytes 15728640 | tf_op jit(solution)/shard_map/add | solution.py:38
  65.9 0.0 copy-done.1
  65.9 12.1 %gather_fusion = f32[3584,256]{1,0:T(8,128)} fusion(f32[5760,256]{1,0:T(8,128)} %bitcast.14, s32[4096]{0:T(1024)S(1)} %pad_clamp_fusion), kind=kCustom, calls=%fused_computation | custom fusion | bytes 7354368 | tf_op jit(solution)/shard_map/gather | solution.py:286
  78.0 66.9 %shard_map.38 = f32[112,256]{1,0:T(8,128)} custom-call(f32[32,112,256]{2,1,0:T(8,128)} %bitcast.17), custom_call_target="tpu_custom_call" | custom-call | tf_op jit(solution)/shard_map/pallas_call | solution.py:126
  144.9 1.6 %copy.6 = f32[112,256]{1,0:T(8,128)} copy(f32[112,256]{1,0:T(8,128)} %shard_map.38) | data formatting | bytes 229376
  (3 shorter events, 0.0 us)
Async XLA Ops:
  0.0 45.9 %copy-start = (bf16[384,256]{1,0:T(8,128)(2,1)S(1)}, bf16[384,256]{1,0:T(8,128)(2,1)}, u32[]{:S(2)}) copy-start(bf16[384,256]{1,0:T(8,128)(2,1)} %param.4) | copy-start | bytes 589828
  49.1 2.7 %slice-start = ((s8[4423680]{0:T(1024)(128)(4,1)}), s8[229376]{0:T(1024)(128)(4,1)S(1)}, s32[]{:S(2)}) async-start(s8[4423680]{0:T(1024)(128)(4,1)} %bitcast.15), calls=%async_computation | async-start | bytes 458752
  51.5 2.2 %slice-start.1 = ((s8[4423680]{0:T(1024)(128)(4,1)}), s8[4194304]{0:T(1024)(128)(4,1)S(1)}, s32[]{:S(2)}) async-start(s8[4423680]{0:T(1024)(128)(4,1)} %bitcast.15), calls=%async_computation.1 | async-start | bytes 8388608
  61.7 4.1 %copy-start.1 = (s32[3584]{0:T(1024)S(1)}, s32[3584]{0:T(1024)}, u32[]{:S(2)}) copy-start(s32[3584]{0:T(1024)} %param.5) | copy-start | bytes 43012

commit v9 on v7

--- a/solution.py
+++ b/solution.py
@@ -10,6 +10,7 @@
 
 MESH = pl.DeviceIdType.MESH
 Z_RING = 16
+SLOTS = 3
 
 
 def kernel_taps():
@@ -68,26 +69,26 @@
                     src = own
                 else:
                     copies[(d, k, s - 1)].wait_recv()
-                    val = recv[d, k, (s - 1) % 2] + own[...]
+                    val = recv[d, k, (s - 1) % SLOTS] + own[...]
                     if s < nz - 1:
-                        if s >= 2:
-                            copies[(d, k, s - 2)].wait_send()
-                        send[d, k, s % 2] = val
-                        src = send.at[d, k, s % 2]
-                        if s <= nz - 3:
+                        if s >= SLOTS:
+                            copies[(d, k, s - SLOTS)].wait_send()
+                        send[d, k, s % SLOTS] = val
+                        src = send.at[d, k, s % SLOTS]
+                        if s <= nz - 1 - SLOTS:
                             pl.semaphore_signal(
                                 credit.at[d, k], 1, device_id=(gz, src_peer), device_id_type=MESH
                             )
                     else:
                         fin[d, pl.ds(k * rk, rk)] = val
                 if s < nz - 1:
-                    if s >= 2:
+                    if s >= SLOTS:
                         pl.semaphore_wait(credit.at[d, k], 1)
                     cp = pltpu.make_async_remote_copy(
                         src_ref=src,
-                        dst_ref=recv.at[d, k, s % 2],
-                        send_sem=send_sem.at[d, k, s % 2],
-                        recv_sem=recv_sem.at[d, k, s % 2],
+                        dst_ref=recv.at[d, k, s % SLOTS],
+                        send_sem=send_sem.at[d, k, s % SLOTS],
+                        recv_sem=recv_sem.at[d, k, s % SLOTS],
                         device_id=(gz, dst),
                         device_id_type=MESH,
                     )
@@ -107,7 +108,7 @@
 
     for d in range(2):
         for k in range(parts):
-            for s in (nz - 3, nz - 2):
+            for s in range(nz - 1 - SLOTS, nz - 1):
                 copies[(d, k, s)].wait_send()
     for k in range(parts):
         copies[("x", k)].wait_recv()
@@ -129,12 +130,12 @@
         in_specs=[pl.BlockSpec(memory_space=pltpu.VMEM)],
         out_specs=pl.BlockSpec(memory_space=pltpu.VMEM),
         scratch_shapes=[
-            pltpu.VMEM((2, parts, 2, rk, cols), jnp.float32),
-            pltpu.VMEM((2, parts, 2, rk, cols), jnp.float32),
+            pltpu.VMEM((2, parts, SLOTS, rk, cols), jnp.float32),
+            pltpu.VMEM((2, parts, SLOTS, rk, cols), jnp.float32),
             pltpu.VMEM((2, rows, cols), jnp.float32),
             pltpu.VMEM((rows, cols), jnp.float32),
-            pltpu.SemaphoreType.DMA((2, parts, 2)),
-            pltpu.SemaphoreType.DMA((2, parts, 2)),
+            pltpu.SemaphoreType.DMA((2, parts, SLOTS)),
+            pltpu.SemaphoreType.DMA((2, parts, SLOTS)),
             pltpu.SemaphoreType.REGULAR((2, parts)),
             pltpu.SemaphoreType.DMA((2, parts)),
         ],

time: 132 us -> 133 us (level)
  no operation moved by 1% of the time
where the time goes in v9:
time: 133 us; the launch traced here: 132 us
  Pallas kernels  67.4 us (51%)
  waiting for transfers between devices  21.2 us (16%)
  local copies, waits for them, and re-layouts  17.8 us (13%)
  other arithmetic  14.8 us (11%)
  starting transfers between devices  8.08 us (6%)
  matrix products  2.92 us (2%)
    pallas_call x1, Pallas kernels, reduce_scatter_ta(): pl.pallas_call(functools.partial(rs_kernel, nz, parts), out_shape=jax.Sha...  67.4 us
    ppermute x1, waiting for transfers between devices, exchange_halo(): below = lax.ppermute(shard[length - width:], axis, up)  18.4 us
    gather x1, local copies, waits for them, and re-layouts, shards(): partial = signal.reshape(slab_cells, rank)[brain_voxels]  12.1 us
    add x4, other arithmetic, smooth_along(): summed + kernel[shift_k] * lax.slice_in_dim(padded, shift_k, shift_k + ex...  10.7 us
    ppermute x1, starting transfers between devices, exchange_halo(): above = lax.ppermute(shard[:width], axis, down)  6.04 us
    add x1, other arithmetic, smooth_planes(): summed + kernel[shift_k] * padded[shift_k:shift_k + planes].astype(jnp.fl...  4.12 us
    slice x1, local copies, waits for them, and re-layouts, exchange_halo(): below = lax.ppermute(shard[length - width:], axis, up)  3.86 us
    dot_general x2, matrix products, project_smooth_xy(): jnp.dot(planes_bf16.reshape(-1, time_local), sketch_matrix, preferred_ele...  2.92 us
  transfers between devices with their start and end apart: 2, of which 2 were waited for; matrix products, arithmetic and copies ran while one was open for 6% of the time, Pallas kernels for 0%

profile of v9, /device:TPU:24, one launch (start us, length us, event | category | flops | bytes accessed | tf_op | source)
XLA Modules:
  0.0 132.3 jit_solution(7117808555121284064)
XLA Ops:
  0.0 0.0 copy-start
  0.0 0.0 copy-start.1
  0.0 3.9 %fusion.50 = (bf16[2,24,40,384]{3,2,1,0:T(8,128)(2,1)}, bf16[2,24,40,384]{3,2,1,0:T(8,128)(2,1)}) fusion(bf16[6,24,40,384]{3,2,1,0:T(8,128)(2,1)} %param.3), kind=kLoop, calls=%fused_computation.75 | loop fusion | bytes 5898240 | tf_op jit(solution)/shard_map/slice | solution.py:150
  3.9 0.0 copy-start.2
  3.9 2.0 %collective-permute-start = (bf16[2,24,40,384]{3,2,1,0:T(8,128)(2,1)}, bf16[2,24,40,384]{3,2,1,0:T(8,128)(2,1)S(1)}, u32[]{:S(2)}, u32[]{:S(2)}) collective-permute-start(bf16[2,24,40,384]{3,2,1,0:T(8,128)(2,1)} %get-tuple-element.5), channel_id=1, source_target_pairs={{0,32},{32,64},{64,96},{96,128},{128,160},{160,192},{192,224},{224... | collective-permute-start | bytes 4423688 | tf_op jit(solution)/shard_map/ppermute | solution.py:150
  5.9 6.0 %collective-permute-start.1 = (bf16[2,24,40,384]{3,2,1,0:T(8,128)(2,1)}, bf16[2,24,40,384]{3,2,1,0:T(8,128)(2,1)S(1)}, u32[]{:S(2)}, u32[]{:S(2)}) collective-permute-start(bf16[2,24,40,384]{3,2,1,0:T(8,128)(2,1)} %get-tuple-element.6), channel_id=1, source_target_pairs={{32,0},{64,32},{96,64},{128,96},{160,128},{192,160},{224,192},{256... | collective-permute-start | bytes 4423688 | tf_op jit(solution)/shard_map/ppermute | solution.py:151
  12.0 0.0 copy-done
  12.0 0.0 copy-done.1
  12.0 1.7 %fusion.46 = f32[6,24,40,256]{3,2,1,0:T(8,128)S(1)} fusion(bf16[6,24,40,384]{3,2,1,0:T(8,128)(2,1)S(1)} %copy-done.1, bf16[384,256]{1,0:T(8,128)(2,1)S(1)} %copy-done), kind=kOutput, calls=%fused_computation.69 | convolution fusion | flops 1132462080 | bytes 10518528 | tf_op jit(solution)/shard_map/dot_general | solution.py:157
  13.7 0.0 copy-done.2
  13.7 2.8 %fusion.4 = f32[6,24,40,256]{3,2,1,0:T(8,128)S(1)} fusion(f32[6,24,40,256]{3,2,1,0:T(8,128)S(1)} %fusion.46), kind=kLoop, calls=%fused_computation.17 | loop fusion | flops 13271040 | bytes 11796480 | tf_op jit(solution)/shard_map/add | solution.py:30
  16.5 3.6 %fusion.12 = f32[6,24,40,256]{3,2,1,0:T(8,128)S(1)} fusion(f32[6,24,40,256]{3,2,1,0:T(8,128)S(1)} %fusion.4), kind=kLoop, calls=%fused_computation.25 | loop fusion | flops 13271040 | bytes 11796480 | tf_op jit(solution)/shard_map/add | solution.py:30
  20.1 18.4 %collective-permute-done = bf16[2,24,40,384]{3,2,1,0:T(8,128)(2,1)S(1)} collective-permute-done((bf16[2,24,40,384]{3,2,1,0:T(8,128)(2,1)}, bf16[2,24,40,384]{3,2,1,0:T(8,128)(2,1)S(1)}, u32[]{:S(2)}, u32[]{:S(2)}) %collective-permute-start) | collective-permute-done | bytes 1474592 | tf_op jit(solution)/shard_map/ppermute | solution.py:150
  38.5 2.8 %collective-permute-done.1 = bf16[2,24,40,384]{3,2,1,0:T(8,128)(2,1)S(1)} collective-permute-done((bf16[2,24,40,384]{3,2,1,0:T(8,128)(2,1)}, bf16[2,24,40,384]{3,2,1,0:T(8,128)(2,1)S(1)}, u32[]{:S(2)}, u32[]{:S(2)}) %collective-permute-start.1) | collective-permute-done | bytes 1474592 | tf_op jit(solution)/shard_map/ppermute | solution.py:151
  41.3 1.2 fusion.42
  42.5 2.0 %fusion.30 = f32[4,24,40,256]{3,2,1,0:T(8,128)S(1)} fusion(f32[4,24,40,256]{3,2,1,0:T(8,128)S(1)} %fusion.42), kind=kLoop, calls=%fused_computation.53 | loop fusion | flops 8847360 | bytes 7864320 | tf_op jit(solution)/shard_map/add | solution.py:30
  44.5 2.3 %fusion.38 = f32[4,24,40,256]{3,2,1,0:T(8,128)S(1)} fusion(f32[4,24,40,256]{3,2,1,0:T(8,128)S(1)} %fusion.30), kind=kLoop, calls=%fused_computation.61 | loop fusion | flops 8847360 | bytes 7864320 | tf_op jit(solution)/shard_map/add | solution.py:30
  46.9 0.3 fusion.51
  47.1 4.1 %fusion.19 = f32[6,24,40,256]{3,2,1,0:T(8,128)} fusion(f32[6,24,40,256]{3,2,1,0:T(8,128)S(1)} %fusion.12, f32[2,24,40,256]{3,2,1,0:T(8,128)S(1)} %get-tuple-element.8, f32[2,24,40,256]{3,2,1,0:T(8,128)S(1)} %get-tuple-element.7), kind=kLoop, calls=%fused_computation.32 | loop fusion | flops 19169280 | bytes 15728640 | tf_op jit(solution)/shard_map/add | solution.py:39
  51.3 12.1 %gather_fusion = f32[3584,256]{1,0:T(8,128)} fusion(f32[5760,256]{1,0:T(8,128)} %bitcast.10, s32[4096]{0:T(1024)S(1)} %pad_clamp_fusion), kind=kCustom, calls=%fused_computation | custom fusion | bytes 7354368 | tf_op jit(solution)/shard_map/gather | solution.py:173
  63.4 67.4 %shard_map.37 = f32[112,256]{1,0:T(8,128)} custom-call(f32[32,112,256]{2,1,0:T(8,128)} %bitcast.11), custom_call_target="tpu_custom_call" | custom-call | tf_op jit(solution)/shard_map/pallas_call | solution.py:127
  130.7 1.6 %copy.6 = f32[112,256]{1,0:T(8,128)} copy(f32[112,256]{1,0:T(8,128)} %shard_map.37) | data formatting | bytes 229376
  (2 shorter events, 0.0 us)
Async XLA Ops:
  0.0 12.0 %copy-start = (bf16[384,256]{1,0:T(8,128)(2,1)S(1)}, bf16[384,256]{1,0:T(8,128)(2,1)}, u32[]{:S(2)}) copy-start(bf16[384,256]{1,0:T(8,128)(2,1)} %param.4) | copy-start | bytes 589828
  0.0 12.0 %copy-start.1 = (bf16[6,24,40,384]{3,2,1,0:T(8,128)(2,1)S(1)}, bf16[6,24,40,384]{3,2,1,0:T(8,128)(2,1)}, u32[]{:S(2)}) copy-start(bf16[6,24,40,384]{3,2,1,0:T(8,128)(2,1)} %param.3) | copy-start | bytes 13271044
  3.9 9.8 %copy-start.2 = (s32[3584]{0:T(1024)S(1)}, s32[3584]{0:T(1024)}, u32[]{:S(2)}) copy-start(s32[3584]{0:T(1024)} %param.5) | copy-start | bytes 43012
  3.9 34.6 %collective-permute-start = (bf16[2,24,40,384]{3,2,1,0:T(8,128)(2,1)}, bf16[2,24,40,384]{3,2,1,0:T(8,128)(2,1)S(1)}, u32[]{:S(2)}, u32[]{:S(2)}) collective-permute-start(bf16[2,24,40,384]{3,2,1,0:T(8,128)(2,1)} %get-tuple-element.5), channel_id=1, source_target_pairs={{0,32},{32,64},{64,96},{96,128},{128,160},{160,192},{192,224},{224... | collective-permute-start | bytes 4423688 | tf_op jit(solution)/shard_map/ppermute | solution.py:150
  5.9 35.4 %collective-permute-start.1 = (bf16[2,24,40,384]{3,2,1,0:T(8,128)(2,1)}, bf16[2,24,40,384]{3,2,1,0:T(8,128)(2,1)S(1)}, u32[]{:S(2)}, u32[]{:S(2)}) collective-permute-start(bf16[2,24,40,384]{3,2,1,0:T(8,128)(2,1)} %get-tuple-element.6), channel_id=1, source_target_pairs={{32,0},{64,32},{96,64},{128,96},{160,128},{192,160},{224,192},{256... | collective-permute-start | bytes 4423688 | tf_op jit(solution)/shard_map/ppermute | solution.py:151

commit v10 on v7

--- a/solution.py
+++ b/solution.py
@@ -167,8 +167,10 @@
     below, above = exchange_halo(volume, "gz", 2)
     local = project_smooth_xy(volume, sketch_matrix, kernel)
     halo = project_smooth_xy(jnp.concatenate([below, above]), sketch_matrix, kernel)
-    padded = jnp.concatenate([halo[:2], local, halo[2:]])
-    signal = smooth_planes(padded, planes, kernel)
+    sources = [halo[0], halo[1]] + [local[p] for p in range(planes)] + [halo[2], halo[3]]
+    signal = jnp.stack(
+        [sum(kernel[k] * sources[p + k] for k in range(5)) for p in range(planes)]
+    )
     partial = signal.reshape(slab_cells, rank)[brain_voxels]
     return reduce_scatter_ta(partial, lax.axis_size("ta"))
 

time: 132 us -> 136 us (1.030)
  other arithmetic: 14.8 us -> 18.7 us
    unnamed x0 -> x5, other arithmetic: none -> 6.62 us
    add x1 -> x0, other arithmetic: 4.12 us -> none  [smooth_planes(): summed + kernel[shift_k] * padded[shift_k:shift_k + planes].astype(jnp.fl...]
where the time goes in v10:
time: 136 us; the launch traced here: 135 us
  Pallas kernels  66.9 us (49%)
  waiting for transfers between devices  21.2 us (16%)
  other arithmetic  18.7 us (14%)
  local copies, waits for them, and re-layouts  17.5 us (13%)
  starting transfers between devices  7.95 us (6%)
  matrix products  2.92 us (2%)
    pallas_call x1, Pallas kernels, reduce_scatter_ta(): pl.pallas_call(functools.partial(rs_kernel, nz, parts), out_shape=jax.Sha...  66.9 us
    ppermute x1, waiting for transfers between devices, exchange_halo(): below = lax.ppermute(shard[length - width:], axis, up)  18.4 us
    gather x1, local copies, waits for them, and re-layouts, shards(): partial = signal.reshape(slab_cells, rank)[brain_voxels]  12.1 us
    add x4, other arithmetic, smooth_along(): summed + kernel[shift_k] * lax.slice_in_dim(padded, shift_k, shift_k + ex...  10.7 us
    unnamed x5, other arithmetic  6.62 us
    ppermute x1, starting transfers between devices, exchange_halo(): above = lax.ppermute(shard[:width], axis, down)  6.04 us
    slice x1, local copies, waits for them, and re-layouts, exchange_halo(): below = lax.ppermute(shard[length - width:], axis, up)  3.86 us
    dot_general x2, matrix products, project_smooth_xy(): jnp.dot(planes_bf16.reshape(-1, time_local), sketch_matrix, preferred_ele...  2.92 us
  transfers between devices with their start and end apart: 2, of which 2 were waited for; matrix products, arithmetic and copies ran while one was open for 6% of the time, Pallas kernels for 0%

profile of v10, /device:TPU:24, one launch (start us, length us, event | category | flops | bytes accessed | tf_op | source)
XLA Modules:
  0.0 135.3 jit_solution(16265726146825211548)
XLA Ops:
  0.0 0.0 copy-start
  0.0 0.0 copy-start.1
  0.0 3.9 %fusion.47 = (bf16[2,24,40,384]{3,2,1,0:T(8,128)(2,1)}, bf16[2,24,40,384]{3,2,1,0:T(8,128)(2,1)}) fusion(bf16[6,24,40,384]{3,2,1,0:T(8,128)(2,1)} %param.3), kind=kLoop, calls=%fused_computation.72 | loop fusion | bytes 5898240 | tf_op jit(solution)/shard_map/slice | solution.py:149
  3.9 1.9 %collective-permute-start = (bf16[2,24,40,384]{3,2,1,0:T(8,128)(2,1)}, bf16[2,24,40,384]{3,2,1,0:T(8,128)(2,1)S(1)}, u32[]{:S(2)}, u32[]{:S(2)}) collective-permute-start(bf16[2,24,40,384]{3,2,1,0:T(8,128)(2,1)} %get-tuple-element.5), channel_id=1, source_target_pairs={{0,32},{32,64},{64,96},{96,128},{128,160},{160,192},{192,224},{224... | collective-permute-start | bytes 4423688 | tf_op jit(solution)/shard_map/ppermute | solution.py:149
  5.8 0.0 copy-start.2
  5.8 6.0 %collective-permute-start.1 = (bf16[2,24,40,384]{3,2,1,0:T(8,128)(2,1)}, bf16[2,24,40,384]{3,2,1,0:T(8,128)(2,1)S(1)}, u32[]{:S(2)}, u32[]{:S(2)}) collective-permute-start(bf16[2,24,40,384]{3,2,1,0:T(8,128)(2,1)} %get-tuple-element.6), channel_id=1, source_target_pairs={{32,0},{64,32},{96,64},{128,96},{160,128},{192,160},{224,192},{256... | collective-permute-start | bytes 4423688 | tf_op jit(solution)/shard_map/ppermute | solution.py:150
  11.8 0.0 copy-done
  11.9 0.0 copy-done.1
  11.9 1.7 %fusion.43 = f32[6,24,40,256]{3,2,1,0:T(8,128)S(1)} fusion(bf16[6,24,40,384]{3,2,1,0:T(8,128)(2,1)S(1)} %copy-done.1, bf16[384,256]{1,0:T(8,128)(2,1)S(1)} %copy-done), kind=kOutput, calls=%fused_computation.66 | convolution fusion | flops 1132462080 | bytes 10518528 | tf_op jit(solution)/shard_map/dot_general | solution.py:156
  13.6 0.0 copy-done.2
  13.6 2.8 %fusion.4 = f32[6,24,40,256]{3,2,1,0:T(8,128)S(1)} fusion(f32[6,24,40,256]{3,2,1,0:T(8,128)S(1)} %fusion.43), kind=kLoop, calls=%fused_computation.13 | loop fusion | flops 13271040 | bytes 11796480 | tf_op jit(solution)/shard_map/add | solution.py:29
  16.4 3.6 %fusion.12 = f32[6,24,40,256]{3,2,1,0:T(8,128)S(1)} fusion(f32[6,24,40,256]{3,2,1,0:T(8,128)S(1)} %fusion.4), kind=kLoop, calls=%fused_computation.21 | loop fusion | flops 13271040 | bytes 11796480 | tf_op jit(solution)/shard_map/add | solution.py:29
  20.0 18.4 %collective-permute-done = bf16[2,24,40,384]{3,2,1,0:T(8,128)(2,1)S(1)} collective-permute-done((bf16[2,24,40,384]{3,2,1,0:T(8,128)(2,1)}, bf16[2,24,40,384]{3,2,1,0:T(8,128)(2,1)S(1)}, u32[]{:S(2)}, u32[]{:S(2)}) %collective-permute-start) | collective-permute-done | bytes 1474592 | tf_op jit(solution)/shard_map/ppermute | solution.py:149
  38.4 2.8 %collective-permute-done.1 = bf16[2,24,40,384]{3,2,1,0:T(8,128)(2,1)S(1)} collective-permute-done((bf16[2,24,40,384]{3,2,1,0:T(8,128)(2,1)}, bf16[2,24,40,384]{3,2,1,0:T(8,128)(2,1)S(1)}, u32[]{:S(2)}, u32[]{:S(2)}) %collective-permute-start.1) | collective-permute-done | bytes 1474592 | tf_op jit(solution)/shard_map/ppermute | solution.py:150
  41.2 1.2 fusion.32
  42.4 2.0 %fusion.20 = f32[4,24,40,256]{3,2,1,0:T(8,128)S(1)} fusion(f32[4,24,40,256]{3,2,1,0:T(8,128)S(1)} %fusion.32), kind=kLoop, calls=%fused_computation.37 | loop fusion | flops 8847360 | bytes 7864320 | tf_op jit(solution)/shard_map/add | solution.py:29
  44.4 2.3 %fusion.28 = f32[4,24,40,256]{3,2,1,0:T(8,128)S(1)} fusion(f32[4,24,40,256]{3,2,1,0:T(8,128)S(1)} %fusion.20), kind=kLoop, calls=%fused_computation.45 | loop fusion | flops 8847360 | bytes 7864320 | tf_op jit(solution)/shard_map/add | solution.py:29
  46.8 1.3 fusion.42
  48.1 1.4 %add_dynamic-update-slice_fusion.3 = f32[6,24,40,256]{3,2,1,0:T(8,128)} fusion(f32[6,24,40,256]{3,2,1,0:T(8,128)} %fusion.42, f32[4,24,40,256]{3,2,1,0:T(8,128)S(1)} %fusion.28, f32[6,24,40,256]{3,2,1,0:T(8,128)S(1)} %fusion.12), kind=kLoop, calls=%fused_computation.65 | loop fusion | flops 2211840 | bytes 5898240
  49.4 1.3 add_dynamic-update-slice_fusion.2
  50.8 1.3 add_dynamic-update-slice_fusion.1
  52.1 1.3 add_dynamic-update-slice_fusion
  53.4 1.3 fusion.37
  54.7 12.1 %gather_fusion = f32[3584,256]{1,0:T(8,128)} fusion(f32[5760,256]{1,0:T(8,128)} %bitcast.3, s32[4096]{0:T(1024)S(1)} %pad_clamp_fusion), kind=kCustom, calls=%fused_computation | custom fusion | bytes 7354368 | tf_op jit(solution)/shard_map/gather | solution.py:174
  66.8 66.9 %shard_map.37 = f32[112,256]{1,0:T(8,128)} custom-call(f32[32,112,256]{2,1,0:T(8,128)} %bitcast.10), custom_call_target="tpu_custom_call" | custom-call | tf_op jit(solution)/shard_map/pallas_call | solution.py:126
  133.7 1.6 %copy.11 = f32[112,256]{1,0:T(8,128)} copy(f32[112,256]{1,0:T(8,128)} %shard_map.37) | data formatting | bytes 229376
  (2 shorter events, 0.0 us)
Async XLA Ops:
  0.0 11.8 %copy-start = (bf16[384,256]{1,0:T(8,128)(2,1)S(1)}, bf16[384,256]{1,0:T(8,128)(2,1)}, u32[]{:S(2)}) copy-start(bf16[384,256]{1,0:T(8,128)(2,1)} %param.4) | copy-start | bytes 589828
  0.0 11.9 %copy-start.1 = (bf16[6,24,40,384]{3,2,1,0:T(8,128)(2,1)S(1)}, bf16[6,24,40,384]{3,2,1,0:T(8,128)(2,1)}, u32[]{:S(2)}) copy-start(bf16[6,24,40,384]{3,2,1,0:T(8,128)(2,1)} %param.3) | copy-start | bytes 13271044
  3.9 34.5 %collective-permute-start = (bf16[2,24,40,384]{3,2,1,0:T(8,128)(2,1)}, bf16[2,24,40,384]{3,2,1,0:T(8,128)(2,1)S(1)}, u32[]{:S(2)}, u32[]{:S(2)}) collective-permute-start(bf16[2,24,40,384]{3,2,1,0:T(8,128)(2,1)} %get-tuple-element.5), channel_id=1, source_target_pairs={{0,32},{32,64},{64,96},{96,128},{128,160},{160,192},{192,224},{224... | collective-permute-start | bytes 4423688 | tf_op jit(solution)/shard_map/ppermute | solution.py:149
  5.8 7.8 %copy-start.2 = (s32[3584]{0:T(1024)S(1)}, s32[3584]{0:T(1024)}, u32[]{:S(2)}) copy-start(s32[3584]{0:T(1024)} %param.5) | copy-start | bytes 43012
  5.8 35.4 %collective-permute-start.1 = (bf16[2,24,40,384]{3,2,1,0:T(8,128)(2,1)}, bf16[2,24,40,384]{3,2,1,0:T(8,128)(2,1)S(1)}, u32[]{:S(2)}, u32[]{:S(2)}) collective-permute-start(bf16[2,24,40,384]{3,2,1,0:T(8,128)(2,1)} %get-tuple-element.6), channel_id=1, source_target_pairs={{32,0},{64,32},{96,64},{128,96},{160,128},{192,160},{224,192},{256... | collective-permute-start | bytes 4423688 | tf_op jit(solution)/shard_map/ppermute | solution.py:150

commit v11 on v7

--- a/solution.py
+++ b/solution.py
@@ -60,8 +60,8 @@
     )
     copies = {}
     for s in range(nz):
-        for k in range(parts):
-            for d, dst, src_peer, chunk in dirs:
+        for d, dst, src_peer, chunk in dirs:
+            for k in range(parts):
                 blk = chunk(s)
                 own = p_ref.at[blk, pl.ds(k * rk, rk)]
                 if s == 0:
@@ -93,7 +93,8 @@
                     )
                     cp.start()
                     copies[(d, k, s)] = cp
-            if s == nz - 1:
+        if s == nz - 1:
+            for k in range(parts):
                 xcp = pltpu.make_async_remote_copy(
                     src_ref=fin.at[1 - xl, pl.ds(k * rk, rk)],
                     dst_ref=xrecv.at[pl.ds(k * rk, rk)],

time: 132 us -> 135 us (1.023)
  Pallas kernels: 66.8 us -> 69.2 us
    pallas_call x1, Pallas kernels: 66.8 us -> 69.2 us  [reduce_scatter_ta(): pl.pallas_call(functools.partial(rs_kernel, nz, parts), out_shape=jax.Sha...]
where the time goes in v11:
time: 135 us; the launch traced here: 134 us
  Pallas kernels  69.2 us (51%)
  waiting for transfers between devices  21.2 us (16%)
  local copies, waits for them, and re-layouts  17.8 us (13%)
  other arithmetic  14.8 us (11%)
  starting transfers between devices  8.08 us (6%)
  matrix products  2.92 us (2%)
    pallas_call x1, Pallas kernels, reduce_scatter_ta(): pl.pallas_call(functools.partial(rs_kernel, nz, parts), out_shape=jax.Sha...  69.2 us
    ppermute x1, waiting for transfers between devices, exchange_halo(): below = lax.ppermute(shard[length - width:], axis, up)  18.4 us
    gather x1, local copies, waits for them, and re-layouts, shards(): partial = signal.reshape(slab_cells, rank)[brain_voxels]  12.1 us
    add x4, other arithmetic, smooth_along(): summed + kernel[shift_k] * lax.slice_in_dim(padded, shift_k, shift_k + ex...  10.7 us
    ppermute x1, starting transfers between devices, exchange_halo(): above = lax.ppermute(shard[:width], axis, down)  6.04 us
    add x1, other arithmetic, smooth_planes(): summed + kernel[shift_k] * padded[shift_k:shift_k + planes].astype(jnp.fl...  4.12 us
    slice x1, local copies, waits for them, and re-layouts, exchange_halo(): below = lax.ppermute(shard[length - width:], axis, up)  3.86 us
    dot_general x2, matrix products, project_smooth_xy(): jnp.dot(planes_bf16.reshape(-1, time_local), sketch_matrix, preferred_ele...  2.92 us
  transfers between devices with their start and end apart: 2, of which 2 were waited for; matrix products, arithmetic and copies ran while one was open for 6% of the time, Pallas kernels for 0%

profile of v11, /device:TPU:24, one launch (start us, length us, event | category | flops | bytes accessed | tf_op | source)
XLA Modules:
  0.0 134.1 jit_solution(3407552368486142996)
XLA Ops:
  0.0 0.0 copy-start
  0.0 0.0 copy-start.1
  0.0 3.9 %fusion.50 = (bf16[2,24,40,384]{3,2,1,0:T(8,128)(2,1)}, bf16[2,24,40,384]{3,2,1,0:T(8,128)(2,1)}) fusion(bf16[6,24,40,384]{3,2,1,0:T(8,128)(2,1)} %param.3), kind=kLoop, calls=%fused_computation.75 | loop fusion | bytes 5898240 | tf_op jit(solution)/shard_map/slice | solution.py:150
  3.9 0.0 copy-start.2
  3.9 2.0 %collective-permute-start = (bf16[2,24,40,384]{3,2,1,0:T(8,128)(2,1)}, bf16[2,24,40,384]{3,2,1,0:T(8,128)(2,1)S(1)}, u32[]{:S(2)}, u32[]{:S(2)}) collective-permute-start(bf16[2,24,40,384]{3,2,1,0:T(8,128)(2,1)} %get-tuple-element.5), channel_id=1, source_target_pairs={{0,32},{32,64},{64,96},{96,128},{128,160},{160,192},{192,224},{224... | collective-permute-start | bytes 4423688 | tf_op jit(solution)/shard_map/ppermute | solution.py:150
  5.9 6.0 %collective-permute-start.1 = (bf16[2,24,40,384]{3,2,1,0:T(8,128)(2,1)}, bf16[2,24,40,384]{3,2,1,0:T(8,128)(2,1)S(1)}, u32[]{:S(2)}, u32[]{:S(2)}) collective-permute-start(bf16[2,24,40,384]{3,2,1,0:T(8,128)(2,1)} %get-tuple-element.6), channel_id=1, source_target_pairs={{32,0},{64,32},{96,64},{128,96},{160,128},{192,160},{224,192},{256... | collective-permute-start | bytes 4423688 | tf_op jit(solution)/shard_map/ppermute | solution.py:151
  12.0 0.0 copy-done
  12.0 0.0 copy-done.1
  12.0 1.7 %fusion.46 = f32[6,24,40,256]{3,2,1,0:T(8,128)S(1)} fusion(bf16[6,24,40,384]{3,2,1,0:T(8,128)(2,1)S(1)} %copy-done.1, bf16[384,256]{1,0:T(8,128)(2,1)S(1)} %copy-done), kind=kOutput, calls=%fused_computation.69 | convolution fusion | flops 1132462080 | bytes 10518528 | tf_op jit(solution)/shard_map/dot_general | solution.py:157
  13.7 0.0 copy-done.2
  13.7 2.8 %fusion.4 = f32[6,24,40,256]{3,2,1,0:T(8,128)S(1)} fusion(f32[6,24,40,256]{3,2,1,0:T(8,128)S(1)} %fusion.46), kind=kLoop, calls=%fused_computation.17 | loop fusion | flops 13271040 | bytes 11796480 | tf_op jit(solution)/shard_map/add | solution.py:29
  16.5 3.6 %fusion.12 = f32[6,24,40,256]{3,2,1,0:T(8,128)S(1)} fusion(f32[6,24,40,256]{3,2,1,0:T(8,128)S(1)} %fusion.4), kind=kLoop, calls=%fused_computation.25 | loop fusion | flops 13271040 | bytes 11796480 | tf_op jit(solution)/shard_map/add | solution.py:29
  20.1 18.4 %collective-permute-done = bf16[2,24,40,384]{3,2,1,0:T(8,128)(2,1)S(1)} collective-permute-done((bf16[2,24,40,384]{3,2,1,0:T(8,128)(2,1)}, bf16[2,24,40,384]{3,2,1,0:T(8,128)(2,1)S(1)}, u32[]{:S(2)}, u32[]{:S(2)}) %collective-permute-start) | collective-permute-done | bytes 1474592 | tf_op jit(solution)/shard_map/ppermute | solution.py:150
  38.5 2.8 %collective-permute-done.1 = bf16[2,24,40,384]{3,2,1,0:T(8,128)(2,1)S(1)} collective-permute-done((bf16[2,24,40,384]{3,2,1,0:T(8,128)(2,1)}, bf16[2,24,40,384]{3,2,1,0:T(8,128)(2,1)S(1)}, u32[]{:S(2)}, u32[]{:S(2)}) %collective-permute-start.1) | collective-permute-done | bytes 1474592 | tf_op jit(solution)/shard_map/ppermute | solution.py:151
  41.3 1.2 fusion.42
  42.5 2.0 %fusion.30 = f32[4,24,40,256]{3,2,1,0:T(8,128)S(1)} fusion(f32[4,24,40,256]{3,2,1,0:T(8,128)S(1)} %fusion.42), kind=kLoop, calls=%fused_computation.53 | loop fusion | flops 8847360 | bytes 7864320 | tf_op jit(solution)/shard_map/add | solution.py:29
  44.5 2.3 %fusion.38 = f32[4,24,40,256]{3,2,1,0:T(8,128)S(1)} fusion(f32[4,24,40,256]{3,2,1,0:T(8,128)S(1)} %fusion.30), kind=kLoop, calls=%fused_computation.61 | loop fusion | flops 8847360 | bytes 7864320 | tf_op jit(solution)/shard_map/add | solution.py:29
  46.9 0.3 fusion.51
  47.1 4.1 %fusion.19 = f32[6,24,40,256]{3,2,1,0:T(8,128)} fusion(f32[6,24,40,256]{3,2,1,0:T(8,128)S(1)} %fusion.12, f32[2,24,40,256]{3,2,1,0:T(8,128)S(1)} %get-tuple-element.8, f32[2,24,40,256]{3,2,1,0:T(8,128)S(1)} %get-tuple-element.7), kind=kLoop, calls=%fused_computation.32 | loop fusion | flops 19169280 | bytes 15728640 | tf_op jit(solution)/shard_map/add | solution.py:38
  51.3 12.1 %gather_fusion = f32[3584,256]{1,0:T(8,128)} fusion(f32[5760,256]{1,0:T(8,128)} %bitcast.10, s32[4096]{0:T(1024)S(1)} %pad_clamp_fusion), kind=kCustom, calls=%fused_computation | custom fusion | bytes 7354368 | tf_op jit(solution)/shard_map/gather | solution.py:173
  63.4 69.2 %shard_map.37 = f32[112,256]{1,0:T(8,128)} custom-call(f32[32,112,256]{2,1,0:T(8,128)} %bitcast.11), custom_call_target="tpu_custom_call" | custom-call | tf_op jit(solution)/shard_map/pallas_call | solution.py:127
  132.6 1.6 %copy.6 = f32[112,256]{1,0:T(8,128)} copy(f32[112,256]{1,0:T(8,128)} %shard_map.37) | data formatting | bytes 229376
  (2 shorter events, 0.0 us)
Async XLA Ops:
  0.0 12.0 %copy-start = (bf16[384,256]{1,0:T(8,128)(2,1)S(1)}, bf16[384,256]{1,0:T(8,128)(2,1)}, u32[]{:S(2)}) copy-start(bf16[384,256]{1,0:T(8,128)(2,1)} %param.4) | copy-start | bytes 589828
  0.0 12.0 %copy-start.1 = (bf16[6,24,40,384]{3,2,1,0:T(8,128)(2,1)S(1)}, bf16[6,24,40,384]{3,2,1,0:T(8,128)(2,1)}, u32[]{:S(2)}) copy-start(bf16[6,24,40,384]{3,2,1,0:T(8,128)(2,1)} %param.3) | copy-start | bytes 13271044
  3.9 9.8 %copy-start.2 = (s32[3584]{0:T(1024)S(1)}, s32[3584]{0:T(1024)}, u32[]{:S(2)}) copy-start(s32[3584]{0:T(1024)} %param.5) | copy-start | bytes 43012
  3.9 34.6 %collective-permute-start = (bf16[2,24,40,384]{3,2,1,0:T(8,128)(2,1)}, bf16[2,24,40,384]{3,2,1,0:T(8,128)(2,1)S(1)}, u32[]{:S(2)}, u32[]{:S(2)}) collective-permute-start(bf16[2,24,40,384]{3,2,1,0:T(8,128)(2,1)} %get-tuple-element.5), channel_id=1, source_target_pairs={{0,32},{32,64},{64,96},{96,128},{128,160},{160,192},{192,224},{224... | collective-permute-start | bytes 4423688 | tf_op jit(solution)/shard_map/ppermute | solution.py:150
  5.9 35.4 %collective-permute-start.1 = (bf16[2,24,40,384]{3,2,1,0:T(8,128)(2,1)}, bf16[2,24,40,384]{3,2,1,0:T(8,128)(2,1)S(1)}, u32[]{:S(2)}, u32[]{:S(2)}) collective-permute-start(bf16[2,24,40,384]{3,2,1,0:T(8,128)(2,1)} %get-tuple-element.6), channel_id=1, source_target_pairs={{32,0},{64,32},{96,64},{128,96},{160,128},{192,160},{224,192},{256... | collective-permute-start | bytes 4423688 | tf_op jit(solution)/shard_map/ppermute | solution.py:151

commit v12 on v7

--- a/solution.py
+++ b/solution.py
@@ -166,9 +166,13 @@
     rank = sketch_matrix.shape[1]
     below, above = exchange_halo(volume, "gz", 2)
     local = project_smooth_xy(volume, sketch_matrix, kernel)
+    zero = jnp.zeros((2,) + local.shape[1:], local.dtype)
+    signal = smooth_planes(jnp.concatenate([zero, local, zero]), planes, kernel)
     halo = project_smooth_xy(jnp.concatenate([below, above]), sketch_matrix, kernel)
-    padded = jnp.concatenate([halo[:2], local, halo[2:]])
-    signal = smooth_planes(padded, planes, kernel)
+    signal = signal.at[0].add(kernel[0] * halo[0] + kernel[1] * halo[1])
+    signal = signal.at[1].add(kernel[0] * halo[1])
+    signal = signal.at[planes - 2].add(kernel[4] * halo[2])
+    signal = signal.at[planes - 1].add(kernel[3] * halo[2] + kernel[4] * halo[3])
     partial = signal.reshape(slab_cells, rank)[brain_voxels]
     return reduce_scatter_ta(partial, lax.axis_size("ta"))
 

time: 132 us -> 137 us (1.038)
  other arithmetic: 14.8 us -> 23.5 us
  waiting for transfers between devices: 21.2 us -> 17.8 us
    scatter-add x0 -> x4, other arithmetic: none -> 9.36 us  [the longest x1 2.38 us: shards(): signal.at[planes - 1].add(kernel[3] * halo[2] + kernel[4] * halo[3])]
    ppermute x1, waiting for transfers between devices: 18.4 us -> 15 us  [exchange_halo(): below = lax.ppermute(shard[length - width:], axis, up)]
  transfers between devices with their start and end apart: 2 -> 2, of which waited for: 2 -> 2; matrix products, arithmetic and copies ran while one was open for 6% -> 8% of each run, Pallas kernels for 0% -> 0%
where the time goes in v12:
time: 137 us
  Pallas kernels  66.8 us (49%)
  other arithmetic  23.5 us (17%)
  waiting for transfers between devices  17.8 us (13%)
  local copies, waits for them, and re-layouts  17.6 us (13%)
  starting transfers between devices  7.95 us (6%)
  matrix products  2.92 us (2%)
    pallas_call x1, Pallas kernels, reduce_scatter_ta(): pl.pallas_call(functools.partial(rs_kernel, nz, parts), out_shape=jax.Sha...  66.8 us
    ppermute x1, waiting for transfers between devices, exchange_halo(): below = lax.ppermute(shard[length - width:], axis, up)  15 us
    gather x1, local copies, waits for them, and re-layouts, shards(): partial = signal.reshape(slab_cells, rank)[brain_voxels]  12.1 us
    add x4, other arithmetic, smooth_along(): summed + kernel[shift_k] * lax.slice_in_dim(padded, shift_k, shift_k + ex...  10.7 us
    ppermute x1, starting transfers between devices, exchange_halo(): above = lax.ppermute(shard[:width], axis, down)  6.04 us
    slice x1, local copies, waits for them, and re-layouts, exchange_halo(): below = lax.ppermute(shard[length - width:], axis, up)  3.92 us
    add x1, other arithmetic, smooth_planes(): summed + kernel[shift_k] * padded[shift_k:shift_k + planes].astype(jnp.fl...  3.41 us
    dot_general x2, matrix products, project_smooth_xy(): jnp.dot(planes_bf16.reshape(-1, time_local), sketch_matrix, preferred_ele...  2.92 us
  transfers between devices with their start and end apart: 2, of which 2 were waited for; matrix products, arithmetic and copies ran while one was open for 8% of the time, Pallas kernels for 0%

profile of v12, /device:TPU:24, one launch (start us, length us, event | category | flops | bytes accessed | tf_op | source)
XLA Modules:
  0.0 136.7 jit_solution(3975786870273497916)
XLA Ops:
  0.0 0.0 copy-start
  0.0 0.0 copy-start.1
  0.0 3.9 %fusion.56 = (bf16[2,24,40,384]{3,2,1,0:T(8,128)(2,1)}, bf16[2,24,40,384]{3,2,1,0:T(8,128)(2,1)}) fusion(bf16[6,24,40,384]{3,2,1,0:T(8,128)(2,1)} %param.11), kind=kLoop, calls=%fused_computation.83 | loop fusion | bytes 5898240 | tf_op jit(solution)/shard_map/slice | solution.py:149
  3.9 1.9 %collective-permute-start = (bf16[2,24,40,384]{3,2,1,0:T(8,128)(2,1)}, bf16[2,24,40,384]{3,2,1,0:T(8,128)(2,1)S(1)}, u32[]{:S(2)}, u32[]{:S(2)}) collective-permute-start(bf16[2,24,40,384]{3,2,1,0:T(8,128)(2,1)} %get-tuple-element.53), channel_id=1, source_target_pairs={{0,32},{32,64},{64,96},{96,128},{128,160},{160,192},{192,224},{224... | collective-permute-start | bytes 4423688 | tf_op jit(solution)/shard_map/ppermute | solution.py:149
  5.8 6.0 %collective-permute-start.1 = (bf16[2,24,40,384]{3,2,1,0:T(8,128)(2,1)}, bf16[2,24,40,384]{3,2,1,0:T(8,128)(2,1)S(1)}, u32[]{:S(2)}, u32[]{:S(2)}) collective-permute-start(bf16[2,24,40,384]{3,2,1,0:T(8,128)(2,1)} %get-tuple-element.54), channel_id=1, source_target_pairs={{32,0},{64,32},{96,64},{128,96},{160,128},{192,160},{224,192},{256... | collective-permute-start | bytes 4423688 | tf_op jit(solution)/shard_map/ppermute | solution.py:150
  11.9 0.0 copy-done
  11.9 0.0 copy-done.1
  11.9 1.7 %fusion.53 = f32[6,24,40,256]{3,2,1,0:T(8,128)S(1)} fusion(bf16[6,24,40,384]{3,2,1,0:T(8,128)(2,1)S(1)} %copy-done.1, bf16[384,256]{1,0:T(8,128)(2,1)S(1)} %copy-done), kind=kOutput, calls=%fused_computation.78 | convolution fusion | flops 1132462080 | bytes 10518528 | tf_op jit(solution)/shard_map/dot_general | solution.py:156
  13.6 0.0 copy-start.2
  13.6 2.8 %fusion.4 = f32[6,24,40,256]{3,2,1,0:T(8,128)S(1)} fusion(f32[6,24,40,256]{3,2,1,0:T(8,128)S(1)} %fusion.53), kind=kLoop, calls=%fused_computation.17 | loop fusion | flops 13271040 | bytes 11796480 | tf_op jit(solution)/shard_map/add | solution.py:29
  16.4 0.0 copy-done.2
  16.5 3.6 %fusion.12 = f32[6,24,40,256]{3,2,1,0:T(8,128)S(1)} fusion(f32[6,24,40,256]{3,2,1,0:T(8,128)S(1)} %fusion.4), kind=kLoop, calls=%fused_computation.25 | loop fusion | flops 13271040 | bytes 11796480 | tf_op jit(solution)/shard_map/add | solution.py:29
  20.1 3.4 %fusion.20 = f32[6,24,40,256]{3,2,1,0:T(8,128)} fusion(f32[6,24,40,256]{3,2,1,0:T(8,128)S(1)} %fusion.12), kind=kLoop, calls=%fused_computation.33 | loop fusion | flops 13271040 | bytes 11796480 | tf_op jit(solution)/shard_map/add | solution.py:38
  23.5 15.0 %collective-permute-done = bf16[2,24,40,384]{3,2,1,0:T(8,128)(2,1)S(1)} collective-permute-done((bf16[2,24,40,384]{3,2,1,0:T(8,128)(2,1)}, bf16[2,24,40,384]{3,2,1,0:T(8,128)(2,1)S(1)}, u32[]{:S(2)}, u32[]{:S(2)}) %collective-permute-start) | collective-permute-done | bytes 1474592 | tf_op jit(solution)/shard_map/ppermute | solution.py:149
  38.4 2.8 %collective-permute-done.1 = bf16[2,24,40,384]{3,2,1,0:T(8,128)(2,1)S(1)} collective-permute-done((bf16[2,24,40,384]{3,2,1,0:T(8,128)(2,1)}, bf16[2,24,40,384]{3,2,1,0:T(8,128)(2,1)S(1)}, u32[]{:S(2)}, u32[]{:S(2)}) %collective-permute-start.1) | collective-permute-done | bytes 1474592 | tf_op jit(solution)/shard_map/ppermute | solution.py:150
  41.2 1.2 fusion.40
  42.5 2.0 %fusion.28 = f32[4,24,40,256]{3,2,1,0:T(8,128)S(1)} fusion(f32[4,24,40,256]{3,2,1,0:T(8,128)S(1)} %fusion.40), kind=kLoop, calls=%fused_computation.49 | loop fusion | flops 8847360 | bytes 7864320 | tf_op jit(solution)/shard_map/add | solution.py:29
  44.5 2.3 %fusion.36 = f32[4,24,40,256]{3,2,1,0:T(8,128)S(1)} fusion(f32[4,24,40,256]{3,2,1,0:T(8,128)S(1)} %fusion.28), kind=kLoop, calls=%fused_computation.57 | loop fusion | flops 8847360 | bytes 7864320 | tf_op jit(solution)/shard_map/add | solution.py:29
  46.8 2.4 %fusion.51 = f32[6,24,40,256]{3,2,1,0:T(8,128)} fusion(f32[6,24,40,256]{3,2,1,0:T(8,128)} %fusion.20, f32[4,24,40,256]{3,2,1,0:T(8,128)S(1)} %fusion.36), kind=kLoop, calls=%fused_computation.76 | loop fusion | flops 983040 | bytes 3932160 | tf_op jit(solution)/shard_map/scatter-add | solution.py:172
  49.2 2.3 %fusion.48 = f32[6,24,40,256]{3,2,1,0:T(8,128)} fusion(f32[6,24,40,256]{3,2,1,0:T(8,128)} %fusion.51, f32[4,24,40,256]{3,2,1,0:T(8,128)S(1)} %fusion.36), kind=kLoop, calls=%fused_computation.72 | loop fusion | flops 491520 | bytes 2949120 | tf_op jit(solution)/shard_map/scatter-add | solution.py:173
  51.5 2.3 %fusion.47 = f32[6,24,40,256]{3,2,1,0:T(8,128)} fusion(f32[6,24,40,256]{3,2,1,0:T(8,128)} %fusion.48, f32[4,24,40,256]{3,2,1,0:T(8,128)S(1)} %fusion.36), kind=kLoop, calls=%fused_computation.70 | loop fusion | flops 491520 | bytes 2949120 | tf_op jit(solution)/shard_map/scatter-add | solution.py:174
  53.8 2.4 %fusion.46 = f32[6,24,40,256]{3,2,1,0:T(8,128)} fusion(f32[6,24,40,256]{3,2,1,0:T(8,128)} %fusion.47, f32[4,24,40,256]{3,2,1,0:T(8,128)S(1)} %fusion.36), kind=kLoop, calls=%fused_computation.68 | loop fusion | flops 983040 | bytes 3932160 | tf_op jit(solution)/shard_map/scatter-add | solution.py:175
  56.2 12.1 %gather_fusion = f32[3584,256]{1,0:T(8,128)} fusion(f32[5760,256]{1,0:T(8,128)} %bitcast.3, s32[4096]{0:T(1024)S(1)} %pad_clamp_fusion), kind=kCustom, calls=%fused_computation | custom fusion | bytes 7354368 | tf_op jit(solution)/shard_map/gather | solution.py:176
  68.3 66.8 %shard_map.37 = f32[112,256]{1,0:T(8,128)} custom-call(f32[32,112,256]{2,1,0:T(8,128)} %bitcast.10), custom_call_target="tpu_custom_call" | custom-call | tf_op jit(solution)/shard_map/pallas_call | solution.py:126
  135.1 1.6 %copy.10 = f32[112,256]{1,0:T(8,128)} copy(f32[112,256]{1,0:T(8,128)} %shard_map.37) | data formatting | bytes 229376
  (2 shorter events, 0.0 us)
Async XLA Ops:
  0.0 11.9 %copy-start = (bf16[384,256]{1,0:T(8,128)(2,1)S(1)}, bf16[384,256]{1,0:T(8,128)(2,1)}, u32[]{:S(2)}) copy-start(bf16[384,256]{1,0:T(8,128)(2,1)} %param.12) | copy-start | bytes 589828
  0.0 11.9 %copy-start.1 = (bf16[6,24,40,384]{3,2,1,0:T(8,128)(2,1)S(1)}, bf16[6,24,40,384]{3,2,1,0:T(8,128)(2,1)}, u32[]{:S(2)}) copy-start(bf16[6,24,40,384]{3,2,1,0:T(8,128)(2,1)} %param.11) | copy-start | bytes 13271044
  3.9 34.5 %collective-permute-start = (bf16[2,24,40,384]{3,2,1,0:T(8,128)(2,1)}, bf16[2,24,40,384]{3,2,1,0:T(8,128)(2,1)S(1)}, u32[]{:S(2)}, u32[]{:S(2)}) collective-permute-start(bf16[2,24,40,384]{3,2,1,0:T(8,128)(2,1)} %get-tuple-element.53), channel_id=1, source_target_pairs={{0,32},{32,64},{64,96},{96,128},{128,160},{160,192},{192,224},{224... | collective-permute-start | bytes 4423688 | tf_op jit(solution)/shard_map/ppermute | solution.py:149
  5.8 35.4 %collective-permute-start.1 = (bf16[2,24,40,384]{3,2,1,0:T(8,128)(2,1)}, bf16[2,24,40,384]{3,2,1,0:T(8,128)(2,1)S(1)}, u32[]{:S(2)}, u32[]{:S(2)}) collective-permute-start(bf16[2,24,40,384]{3,2,1,0:T(8,128)(2,1)} %get-tuple-element.54), channel_id=1, source_target_pairs={{32,0},{64,32},{96,64},{128,96},{160,128},{192,160},{224,192},{256... | collective-permute-start | bytes 4423688 | tf_op jit(solution)/shard_map/ppermute | solution.py:150
  13.6 2.8 %copy-start.2 = (s32[3584]{0:T(1024)S(1)}, s32[3584]{0:T(1024)}, u32[]{:S(2)}) copy-start(s32[3584]{0:T(1024)} %param.13) | copy-start | bytes 43012

commit v13 on v7

--- a/solution.py
+++ b/solution.py
@@ -166,8 +166,9 @@
     rank = sketch_matrix.shape[1]
     below, above = exchange_halo(volume, "gz", 2)
     local = project_smooth_xy(volume, sketch_matrix, kernel)
-    halo = project_smooth_xy(jnp.concatenate([below, above]), sketch_matrix, kernel)
-    padded = jnp.concatenate([halo[:2], local, halo[2:]])
+    lower = project_smooth_xy(below, sketch_matrix, kernel)
+    upper = project_smooth_xy(above, sketch_matrix, kernel)
+    padded = jnp.concatenate([lower, local, upper])
     signal = smooth_planes(padded, planes, kernel)
     partial = signal.reshape(slab_cells, rank)[brain_voxels]
     return reduce_scatter_ta(partial, lax.axis_size("ta"))

time: 132 us -> 130 us (0.985)
    add x4 -> x5, other arithmetic: 10.7 us -> 9.62 us  [smooth_along(): summed + kernel[shift_k] * lax.slice_in_dim(padded, shift_k, shift_k + ex...]
    dot_general x2 -> x3, matrix products: 2.92 us -> 3.06 us  [project_smooth_xy(): jnp.dot(planes_bf16.reshape(-1, time_local), sketch_matrix, preferred_ele...]
  transfers between devices with their start and end apart: 2 -> 2, of which waited for: 2 -> 2; matrix products, arithmetic and copies ran while one was open for 6% -> 7% of each run, Pallas kernels for 0% -> 0%
where the time goes in v13:
time: 130 us; the launch traced here: 129 us
  Pallas kernels  66.9 us (51%)
  waiting for transfers between devices  20.1 us (15%)
  local copies, waits for them, and re-layouts  17.5 us (13%)
  other arithmetic  13.7 us (11%)
  starting transfers between devices  7.95 us (6%)
  matrix products  3.06 us (2%)
    pallas_call x1, Pallas kernels, reduce_scatter_ta(): pl.pallas_call(functools.partial(rs_kernel, nz, parts), out_shape=jax.Sha...  66.9 us
    ppermute x1, waiting for transfers between devices, exchange_halo(): below = lax.ppermute(shard[length - width:], axis, up)  18.4 us
    gather x1, local copies, waits for them, and re-layouts, shards(): partial = signal.reshape(slab_cells, rank)[brain_voxels]  12.1 us
    add x5, other arithmetic, smooth_along(): summed + kernel[shift_k] * lax.slice_in_dim(padded, shift_k, shift_k + ex...  9.62 us
    ppermute x1, starting transfers between devices, exchange_halo(): above = lax.ppermute(shard[:width], axis, down)  6.04 us
    add x1, other arithmetic, smooth_planes(): summed + kernel[shift_k] * padded[shift_k:shift_k + planes].astype(jnp.fl...  4.12 us
    slice x1, local copies, waits for them, and re-layouts, exchange_halo(): below = lax.ppermute(shard[length - width:], axis, up)  3.86 us
    dot_general x3, matrix products, project_smooth_xy(): jnp.dot(planes_bf16.reshape(-1, time_local), sketch_matrix, preferred_ele...  3.06 us
  transfers between devices with their start and end apart: 2, of which 2 were waited for; matrix products, arithmetic and copies ran while one was open for 7% of the time, Pallas kernels for 0%

profile of v13, /device:TPU:24, one launch (start us, length us, event | category | flops | bytes accessed | tf_op | source)
XLA Modules:
  0.0 129.4 jit_solution(3045029336880716080)
XLA Ops:
  0.0 0.0 copy-start
  0.0 0.0 copy-start.1
  0.0 3.9 %fusion.64 = (bf16[2,24,40,384]{3,2,1,0:T(8,128)(2,1)}, bf16[2,24,40,384]{3,2,1,0:T(8,128)(2,1)}) fusion(bf16[6,24,40,384]{3,2,1,0:T(8,128)(2,1)} %param.3), kind=kLoop, calls=%fused_computation.97 | loop fusion | bytes 5898240 | tf_op jit(solution)/shard_map/slice | solution.py:149
  3.9 1.9 %collective-permute-start = (bf16[2,24,40,384]{3,2,1,0:T(8,128)(2,1)}, bf16[2,24,40,384]{3,2,1,0:T(8,128)(2,1)S(1)}, u32[]{:S(2)}, u32[]{:S(2)}) collective-permute-start(bf16[2,24,40,384]{3,2,1,0:T(8,128)(2,1)} %get-tuple-element.5), channel_id=1, source_target_pairs={{0,32},{32,64},{64,96},{96,128},{128,160},{160,192},{192,224},{224... | collective-permute-start | bytes 4423688 | tf_op jit(solution)/shard_map/ppermute | solution.py:149
  5.8 0.0 copy-start.2
  5.8 6.0 %collective-permute-start.1 = (bf16[2,24,40,384]{3,2,1,0:T(8,128)(2,1)}, bf16[2,24,40,384]{3,2,1,0:T(8,128)(2,1)S(1)}, u32[]{:S(2)}, u32[]{:S(2)}) collective-permute-start(bf16[2,24,40,384]{3,2,1,0:T(8,128)(2,1)} %get-tuple-element.6), channel_id=1, source_target_pairs={{32,0},{64,32},{96,64},{128,96},{160,128},{192,160},{224,192},{256... | collective-permute-start | bytes 4423688 | tf_op jit(solution)/shard_map/ppermute | solution.py:150
  11.8 0.0 copy-done
  11.9 0.0 copy-done.1
  11.9 1.7 %fusion.60 = f32[6,24,40,256]{3,2,1,0:T(8,128)S(1)} fusion(bf16[6,24,40,384]{3,2,1,0:T(8,128)(2,1)S(1)} %copy-done.1, bf16[384,256]{1,0:T(8,128)(2,1)S(1)} %copy-done), kind=kOutput, calls=%fused_computation.91 | convolution fusion | flops 1132462080 | bytes 10518528 | tf_op jit(solution)/shard_map/dot_general | solution.py:156
  13.6 0.0 copy-done.2
  13.6 2.8 %fusion.4 = f32[6,24,40,256]{3,2,1,0:T(8,128)S(1)} fusion(f32[6,24,40,256]{3,2,1,0:T(8,128)S(1)} %fusion.60), kind=kLoop, calls=%fused_computation.17 | loop fusion | flops 13271040 | bytes 11796480 | tf_op jit(solution)/shard_map/add | solution.py:29
  16.4 3.6 %fusion.12 = f32[6,24,40,256]{3,2,1,0:T(8,128)S(1)} fusion(f32[6,24,40,256]{3,2,1,0:T(8,128)S(1)} %fusion.4), kind=kLoop, calls=%fused_computation.25 | loop fusion | flops 13271040 | bytes 11796480 | tf_op jit(solution)/shard_map/add | solution.py:29
  20.0 18.4 %collective-permute-done = bf16[2,24,40,384]{3,2,1,0:T(8,128)(2,1)S(1)} collective-permute-done((bf16[2,24,40,384]{3,2,1,0:T(8,128)(2,1)}, bf16[2,24,40,384]{3,2,1,0:T(8,128)(2,1)S(1)}, u32[]{:S(2)}, u32[]{:S(2)}) %collective-permute-start) | collective-permute-done | bytes 1474592 | tf_op jit(solution)/shard_map/ppermute | solution.py:149
  38.3 0.7 fusion.62
  39.0 0.4 fusion.30
  39.5 1.7 %collective-permute-done.1 = bf16[2,24,40,384]{3,2,1,0:T(8,128)(2,1)S(1)} collective-permute-done((bf16[2,24,40,384]{3,2,1,0:T(8,128)(2,1)}, bf16[2,24,40,384]{3,2,1,0:T(8,128)(2,1)S(1)}, u32[]{:S(2)}, u32[]{:S(2)}) %collective-permute-start.1) | collective-permute-done | bytes 1474592 | tf_op jit(solution)/shard_map/ppermute | solution.py:150
  41.2 0.7 fusion.58
  41.9 0.4 fusion.38
  42.3 2.4 %fusion.46 = (f32[2,24,40,256]{3,2,1,0:T(8,128)S(1)}, f32[2,24,40,256]{3,2,1,0:T(8,128)S(1)}) fusion(f32[2,24,40,256]{3,2,1,0:T(8,128)S(1)} %fusion.30, f32[2,24,40,256]{3,2,1,0:T(8,128)S(1)} %fusion.38), kind=kLoop, calls=%fused_computation.77 | loop fusion | flops 8847360 | bytes 7864320 | tf_op jit(solution)/shard_map/add | solution.py:29
  44.7 4.1 %fusion.19 = f32[6,24,40,256]{3,2,1,0:T(8,128)} fusion(f32[6,24,40,256]{3,2,1,0:T(8,128)S(1)} %fusion.12, f32[2,24,40,256]{3,2,1,0:T(8,128)S(1)} %get-tuple-element.8, f32[2,24,40,256]{3,2,1,0:T(8,128)S(1)} %get-tuple-element.7), kind=kLoop, calls=%fused_computation.32 | loop fusion | flops 19169280 | bytes 15728640 | tf_op jit(solution)/shard_map/add | solution.py:38
  48.8 12.1 %gather_fusion = f32[3584,256]{1,0:T(8,128)} fusion(f32[5760,256]{1,0:T(8,128)} %bitcast.14, s32[4096]{0:T(1024)S(1)} %pad_clamp_fusion), kind=kCustom, calls=%fused_computation | custom fusion | bytes 7354368 | tf_op jit(solution)/shard_map/gather | solution.py:173
  60.9 66.9 %shard_map.37 = f32[112,256]{1,0:T(8,128)} custom-call(f32[32,112,256]{2,1,0:T(8,128)} %bitcast.15), custom_call_target="tpu_custom_call" | custom-call | tf_op jit(solution)/shard_map/pallas_call | solution.py:126
  127.8 1.6 %copy.6 = f32[112,256]{1,0:T(8,128)} copy(f32[112,256]{1,0:T(8,128)} %shard_map.37) | data formatting | bytes 229376
  (2 shorter events, 0.0 us)
Async XLA Ops:
  0.0 11.8 %copy-start = (bf16[384,256]{1,0:T(8,128)(2,1)S(1)}, bf16[384,256]{1,0:T(8,128)(2,1)}, u32[]{:S(2)}) copy-start(bf16[384,256]{1,0:T(8,128)(2,1)} %param.4) | copy-start | bytes 589828
  0.0 11.9 %copy-start.1 = (bf16[6,24,40,384]{3,2,1,0:T(8,128)(2,1)S(1)}, bf16[6,24,40,384]{3,2,1,0:T(8,128)(2,1)}, u32[]{:S(2)}) copy-start(bf16[6,24,40,384]{3,2,1,0:T(8,128)(2,1)} %param.3) | copy-start | bytes 13271044
  3.9 34.5 %collective-permute-start = (bf16[2,24,40,384]{3,2,1,0:T(8,128)(2,1)}, bf16[2,24,40,384]{3,2,1,0:T(8,128)(2,1)S(1)}, u32[]{:S(2)}, u32[]{:S(2)}) collective-permute-start(bf16[2,24,40,384]{3,2,1,0:T(8,128)(2,1)} %get-tuple-element.5), channel_id=1, source_target_pairs={{0,32},{32,64},{64,96},{96,128},{128,160},{160,192},{192,224},{224... | collective-permute-start | bytes 4423688 | tf_op jit(solution)/shard_map/ppermute | solution.py:149
  5.8 7.8 %copy-start.2 = (s32[3584]{0:T(1024)S(1)}, s32[3584]{0:T(1024)}, u32[]{:S(2)}) copy-start(s32[3584]{0:T(1024)} %param.5) | copy-start | bytes 43012
  5.8 35.4 %collective-permute-start.1 = (bf16[2,24,40,384]{3,2,1,0:T(8,128)(2,1)}, bf16[2,24,40,384]{3,2,1,0:T(8,128)(2,1)S(1)}, u32[]{:S(2)}, u32[]{:S(2)}) collective-permute-start(bf16[2,24,40,384]{3,2,1,0:T(8,128)(2,1)} %get-tuple-element.6), channel_id=1, source_target_pairs={{32,0},{64,32},{96,64},{128,96},{160,128},{192,160},{224,192},{256... | collective-permute-start | bytes 4423688 | tf_op jit(solution)/shard_map/ppermute | solution.py:150

commit v14 on v13

--- a/solution.py
+++ b/solution.py
@@ -168,8 +168,9 @@
     local = project_smooth_xy(volume, sketch_matrix, kernel)
     lower = project_smooth_xy(below, sketch_matrix, kernel)
     upper = project_smooth_xy(above, sketch_matrix, kernel)
-    padded = jnp.concatenate([lower, local, upper])
-    signal = smooth_planes(padded, planes, kernel)
+    early = smooth_planes(jnp.concatenate([lower, local]), planes - 2, kernel)
+    late = smooth_planes(jnp.concatenate([local[2:], upper]), 2, kernel)
+    signal = jnp.concatenate([early, late])
     partial = signal.reshape(slab_cells, rank)[brain_voxels]
     return reduce_scatter_ta(partial, lax.axis_size("ta"))
 

time: 130 us -> 131 us (level)
    concatenate x0 -> x1, other arithmetic: none -> 2.95 us  [shards(): signal = jnp.concatenate([early, late])]
    add x1 -> x2, other arithmetic: 4.12 us -> 2.21 us  [smooth_planes(): summed + kernel[shift_k] * padded[shift_k:shift_k + planes].astype(jnp.fl...]
    add x5 -> x6, other arithmetic: 9.62 us -> 9.39 us  [smooth_along(): summed + kernel[shift_k] * lax.slice_in_dim(padded, shift_k, shift_k + ex...]
  transfers between devices with their start and end apart: 2 -> 2, of which waited for: 2 -> 2; matrix products, arithmetic and copies ran while one was open for 7% -> 8% of each run, Pallas kernels for 0% -> 0%
where the time goes in v14:
time: 131 us; the launch traced here: 130 us
  Pallas kernels  67.7 us (52%)
  waiting for transfers between devices  19 us (15%)
  local copies, waits for them, and re-layouts  17.5 us (13%)
  other arithmetic  14.6 us (11%)
  starting transfers between devices  7.95 us (6%)
  matrix products  3.06 us (2%)
    pallas_call x1, Pallas kernels, reduce_scatter_ta(): pl.pallas_call(functools.partial(rs_kernel, nz, parts), out_shape=jax.Sha...  67.7 us
    ppermute x1, waiting for transfers between devices, exchange_halo(): below = lax.ppermute(shard[length - width:], axis, up)  18.4 us
    gather x1, local copies, waits for them, and re-layouts, shards(): partial = signal.reshape(slab_cells, rank)[brain_voxels]  12.1 us
    add x6, other arithmetic, smooth_along(): summed + kernel[shift_k] * lax.slice_in_dim(padded, shift_k, shift_k + ex...  9.39 us
    ppermute x1, starting transfers between devices, exchange_halo(): above = lax.ppermute(shard[:width], axis, down)  6.04 us
    slice x1, local copies, waits for them, and re-layouts, exchange_halo(): below = lax.ppermute(shard[length - width:], axis, up)  3.86 us
    dot_general x3, matrix products, project_smooth_xy(): jnp.dot(planes_bf16.reshape(-1, time_local), sketch_matrix, preferred_ele...  3.06 us
    concatenate x1, other arithmetic, shards(): signal = jnp.concatenate([early, late])  2.95 us
  transfers between devices with their start and end apart: 2, of which 2 were waited for; matrix products, arithmetic and copies ran while one was open for 8% of the time, Pallas kernels for 0%

profile of v14, /device:TPU:24, one launch (start us, length us, event | category | flops | bytes accessed | tf_op | source)
XLA Modules:
  0.0 129.9 jit_solution(3705761938785734951)
XLA Ops:
  0.0 0.0 copy-start
  0.0 0.0 copy-start.1
  0.0 3.9 %fusion.66 = (bf16[2,24,40,384]{3,2,1,0:T(8,128)(2,1)}, bf16[2,24,40,384]{3,2,1,0:T(8,128)(2,1)}) fusion(bf16[6,24,40,384]{3,2,1,0:T(8,128)(2,1)} %param.3), kind=kLoop, calls=%fused_computation.103 | loop fusion | bytes 5898240 | tf_op jit(solution)/shard_map/slice | solution.py:149
  3.9 1.9 %collective-permute-start = (bf16[2,24,40,384]{3,2,1,0:T(8,128)(2,1)}, bf16[2,24,40,384]{3,2,1,0:T(8,128)(2,1)S(1)}, u32[]{:S(2)}, u32[]{:S(2)}) collective-permute-start(bf16[2,24,40,384]{3,2,1,0:T(8,128)(2,1)} %get-tuple-element.7), channel_id=1, source_target_pairs={{0,32},{32,64},{64,96},{96,128},{128,160},{160,192},{192,224},{224... | collective-permute-start | bytes 4423688 | tf_op jit(solution)/shard_map/ppermute | solution.py:149
  5.8 0.0 copy-start.2
  5.8 6.0 %collective-permute-start.1 = (bf16[2,24,40,384]{3,2,1,0:T(8,128)(2,1)}, bf16[2,24,40,384]{3,2,1,0:T(8,128)(2,1)S(1)}, u32[]{:S(2)}, u32[]{:S(2)}) collective-permute-start(bf16[2,24,40,384]{3,2,1,0:T(8,128)(2,1)} %get-tuple-element.8), channel_id=1, source_target_pairs={{32,0},{64,32},{96,64},{128,96},{160,128},{192,160},{224,192},{256... | collective-permute-start | bytes 4423688 | tf_op jit(solution)/shard_map/ppermute | solution.py:150
  11.8 0.0 copy-done
  11.9 0.0 copy-done.1
  11.9 1.7 %fusion.62 = f32[6,24,40,256]{3,2,1,0:T(8,128)S(1)} fusion(bf16[6,24,40,384]{3,2,1,0:T(8,128)(2,1)S(1)} %copy-done.1, bf16[384,256]{1,0:T(8,128)(2,1)S(1)} %copy-done), kind=kOutput, calls=%fused_computation.97 | convolution fusion | flops 1132462080 | bytes 10518528 | tf_op jit(solution)/shard_map/dot_general | solution.py:156
  13.6 0.0 copy-done.2
  13.6 2.8 %fusion.4 = f32[6,24,40,256]{3,2,1,0:T(8,128)S(1)} fusion(f32[6,24,40,256]{3,2,1,0:T(8,128)S(1)} %fusion.62), kind=kLoop, calls=%fused_computation.15 | loop fusion | flops 13271040 | bytes 11796480 | tf_op jit(solution)/shard_map/add | solution.py:29
  16.4 3.6 %fusion.12 = f32[6,24,40,256]{3,2,1,0:T(8,128)S(1)} fusion(f32[6,24,40,256]{3,2,1,0:T(8,128)S(1)} %fusion.4), kind=kLoop, calls=%fused_computation.23 | loop fusion | flops 13271040 | bytes 11796480 | tf_op jit(solution)/shard_map/add | solution.py:29
  20.0 18.4 %collective-permute-done = bf16[2,24,40,384]{3,2,1,0:T(8,128)(2,1)S(1)} collective-permute-done((bf16[2,24,40,384]{3,2,1,0:T(8,128)(2,1)}, bf16[2,24,40,384]{3,2,1,0:T(8,128)(2,1)S(1)}, u32[]{:S(2)}, u32[]{:S(2)}) %collective-permute-start) | collective-permute-done | bytes 1474592 | tf_op jit(solution)/shard_map/ppermute | solution.py:149
  38.3 0.7 fusion.64
  39.0 0.4 fusion.27
  39.5 1.1 fusion.43
  40.6 0.6 collective-permute-done.1
  41.2 0.7 fusion.60
  41.9 0.4 fusion.35
  42.3 1.1 fusion.51
  43.4 1.6 %fusion.21 = (f32[4,24,40,256]{3,2,1,0:T(8,128)S(1)}, f32[4,24,40,256]{3,2,1,0:T(8,128)S(1)}) fusion(f32[2,24,40,256]{3,2,1,0:T(8,128)S(1)} %fusion.43, f32[6,24,40,256]{3,2,1,0:T(8,128)S(1)} %fusion.12), kind=kLoop, calls=%fused_computation.33 | loop fusion | flops 10813440 | bytes 27525120 | tf_op jit(solution)/shard_map/add | solution.py:38
  45.0 0.6 fusion.57
  45.6 2.9 %pad_maximum_fusion = f32[6,24,40,256]{3,2,1,0:T(8,128)} fusion(f32[2,24,40,256]{3,2,1,0:T(8,128)S(1)} %fusion.57, f32[4,24,40,256]{3,2,1,0:T(8,128)S(1)} %get-tuple-element.5), kind=kLoop, calls=%fused_computation.27 | loop fusion | flops 1474560 | bytes 11796480 | tf_op jit(solution)/shard_map/concatenate | solution.py:173
  48.6 12.1 %gather_fusion = f32[3584,256]{1,0:T(8,128)} fusion(f32[5760,256]{1,0:T(8,128)} %bitcast.14, s32[4096]{0:T(1024)S(1)} %pad_clamp_fusion), kind=kCustom, calls=%fused_computation | custom fusion | bytes 7354368 | tf_op jit(solution)/shard_map/gather | solution.py:174
  60.7 67.7 %shard_map.37 = f32[112,256]{1,0:T(8,128)} custom-call(f32[32,112,256]{2,1,0:T(8,128)} %bitcast.15), custom_call_target="tpu_custom_call" | custom-call | tf_op jit(solution)/shard_map/pallas_call | solution.py:126
  128.4 1.6 %copy.6 = f32[112,256]{1,0:T(8,128)} copy(f32[112,256]{1,0:T(8,128)} %shard_map.37) | data formatting | bytes 229376
  (2 shorter events, 0.0 us)
Async XLA Ops:
  0.0 11.8 %copy-start = (bf16[384,256]{1,0:T(8,128)(2,1)S(1)}, bf16[384,256]{1,0:T(8,128)(2,1)}, u32[]{:S(2)}) copy-start(bf16[384,256]{1,0:T(8,128)(2,1)} %param.4) | copy-start | bytes 589828
  0.0 11.9 %copy-start.1 = (bf16[6,24,40,384]{3,2,1,0:T(8,128)(2,1)S(1)}, bf16[6,24,40,384]{3,2,1,0:T(8,128)(2,1)}, u32[]{:S(2)}) copy-start(bf16[6,24,40,384]{3,2,1,0:T(8,128)(2,1)} %param.3) | copy-start | bytes 13271044
  3.9 34.5 %collective-permute-start = (bf16[2,24,40,384]{3,2,1,0:T(8,128)(2,1)}, bf16[2,24,40,384]{3,2,1,0:T(8,128)(2,1)S(1)}, u32[]{:S(2)}, u32[]{:S(2)}) collective-permute-start(bf16[2,24,40,384]{3,2,1,0:T(8,128)(2,1)} %get-tuple-element.7), channel_id=1, source_target_pairs={{0,32},{32,64},{64,96},{96,128},{128,160},{160,192},{192,224},{224... | collective-permute-start | bytes 4423688 | tf_op jit(solution)/shard_map/ppermute | solution.py:149
  5.8 7.8 %copy-start.2 = (s32[3584]{0:T(1024)S(1)}, s32[3584]{0:T(1024)}, u32[]{:S(2)}) copy-start(s32[3584]{0:T(1024)} %param.5) | copy-start | bytes 43012
  5.8 35.4 %collective-permute-start.1 = (bf16[2,24,40,384]{3,2,1,0:T(8,128)(2,1)}, bf16[2,24,40,384]{3,2,1,0:T(8,128)(2,1)S(1)}, u32[]{:S(2)}, u32[]{:S(2)}) collective-permute-start(bf16[2,24,40,384]{3,2,1,0:T(8,128)(2,1)} %get-tuple-element.8), channel_id=1, source_target_pairs={{32,0},{64,32},{96,64},{128,96},{160,128},{192,160},{224,192},{256... | collective-permute-start | bytes 4423688 | tf_op jit(solution)/shard_map/ppermute | solution.py:150
